TPU v7x, 128 devices: a whole 4x4x4 slice. The times are simulated.
128 devices in a mesh: rcv: 8 (over x_hi, z), src: 16 (over y, x_lo, core).
Axes of the slice: x: 4 (x_hi: 2, x_lo: 2; x = x_hi * 2 + x_lo), y: 4, z: 4, core: 2. Of those that a mesh axis runs over, the one named last changes fastest.
Arguments:
- reflection: bfloat16 [2, 16384, 16384], P(None, 'rcv', 'src'), may hold values from -6 to 6
- green: bfloat16 [2, 16384, 512], P(None, 'rcv', 'src'), may hold values from -0.046875 to 0.046875
- tile_mask: int32 [64, 64], replicated, may hold values from 0 to 1, as said below
- reference_index: int32 [512], P(('rcv', 'src')), may hold values from 0 to 511
Outputs:
- aligned: float32 [512, 2, 512], P(('rcv', 'src'))
Inputs may be any that keep to these rules, and one draw needn't show every extreme that they name: `tile_mask`: entries below the diagonal are 0.
All inputs are finite; a program needn't handle non-finite values.
Results may differ from a plain program's by a relative error of at most 0.02.
Values may be sent and summed in bfloat16 or wider, within the bound.
No kernel may reach another device: no remote copies, remote signals or barrier semaphores. Data moves between devices by JAX's collectives and lax.ppermute only.
A program may use at most 128 MiB of HBM per device.

v0:
```python
import jax
import jax.numpy as jnp
from jax import lax
from jax.sharding import PartitionSpec as P

P_SIZE = 512
TILE = 256


def filled_up(lines, devices):
    spare = -lines.shape[0] % devices
    if not spare:
        return lines
    return jnp.concatenate([lines, jnp.zeros((spare, *lines.shape[1:]), lines.dtype)])


def spread(value, axis, root):
    lines = jnp.where(lax.axis_index(axis) == root, value, jnp.zeros_like(value)).reshape(
        -1, *value.shape[1:][-1:]
    )
    padded = filled_up(lines, lax.axis_size(axis))
    own = lax.psum_scatter(padded, axis, scatter_dimension=0, tiled=True)
    return lax.all_gather(own, axis, axis=0, tiled=True)[: len(lines)].reshape(value.shape)


def across(first, second, precision=None):
    return lax.dot_general(
        first,
        second,
        (((0,), (0,)), ((), ())),
        precision=precision,
        preferred_element_type=jnp.float32,
    )


def body(reflection, green, tile_mask, reference_index):
    rows_blk = reflection.shape[1]
    col_count = reflection.shape[2]
    rcv_index = lax.axis_index("rcv")
    src_index = lax.axis_index("src")
    green_block = lax.all_gather(green, "src", axis=2, tiled=True)
    src_per_rcv = lax.axis_size("src") // lax.axis_size("rcv")
    green_piece = lax.dynamic_slice_in_dim(
        green_block, src_index % src_per_rcv * col_count, col_count, 1
    )
    green_src = spread(green_piece, "rcv", src_index // src_per_rcv)
    row_tiles_count = rows_blk // TILE
    col_tiles_count = col_count // TILE
    tile_block = lax.dynamic_slice(
        tile_mask,
        (rcv_index * row_tiles_count, src_index * col_tiles_count),
        (row_tiles_count, col_tiles_count),
    )
    row_ids = rcv_index * row_tiles_count + jnp.arange(row_tiles_count)
    col_ids = src_index * col_tiles_count + jnp.arange(col_tiles_count)
    kept_tiles = tile_block == 1
    off_diag = kept_tiles & (row_ids[:, None] != col_ids[None, :])
    shaped = reflection.reshape(2, row_tiles_count, TILE, col_tiles_count, TILE)
    zero_value = jnp.zeros((), jnp.bfloat16)
    acquired = jnp.where(kept_tiles[None, :, None, :, None], shaped, zero_value).reshape(
        2, rows_blk, col_count
    )
    mirror_part = jnp.where(off_diag[None, :, None, :, None], shaped, zero_value).reshape(
        2, rows_blk, col_count
    )
    data_wide = jnp.concatenate([acquired[0], acquired[1], mirror_part[0], mirror_part[1]], axis=1)
    green_wide = jnp.concatenate([green_block[0], green_block[1]], axis=1)
    products = across(data_wide, green_wide)

    def quarter(row_slot, col_slot):
        return products[
            row_slot * col_count : (row_slot + 1) * col_count,
            col_slot * P_SIZE : (col_slot + 1) * P_SIZE,
        ]

    front_real = (quarter(0, 0) + quarter(1, 1)).astype(jnp.bfloat16)
    front_imag = (quarter(1, 0) - quarter(0, 1)).astype(jnp.bfloat16)
    back_real = (quarter(2, 0) - quarter(3, 1)).astype(jnp.bfloat16)
    back_imag = (quarter(3, 0) + quarter(2, 1)).astype(jnp.bfloat16)
    src_real = green_src[0]
    src_imag = green_src[1]
    green_stack = jnp.concatenate([src_real, src_imag], axis=0)
    mirror_left = jnp.concatenate(
        [
            jnp.concatenate([back_real, back_imag], axis=1),
            jnp.concatenate([back_imag, -back_real], axis=1),
        ],
        axis=0,
    )
    mirrored = across(green_stack, mirror_left)
    weights = jnp.concatenate(
        [
            jnp.concatenate([src_real, src_imag], axis=1),
            jnp.concatenate([-src_imag, src_real], axis=1),
        ],
        axis=0,
    )
    left_rows = jnp.concatenate([front_real, front_imag], axis=0)
    combined = across(left_rows, weights) + mirrored
    focal = lax.psum_scatter(combined, ("rcv", "src"), scatter_dimension=0, tiled=True)
    focal_real = focal[:, :P_SIZE]
    focal_imag = focal[:, P_SIZE:]
    chosen = jnp.arange(P_SIZE)[None, :] == reference_index[:, None]
    anchor_real = jnp.sum(jnp.where(chosen, focal_real, 0.0), axis=1)[:, None]
    anchor_imag = jnp.sum(jnp.where(chosen, focal_imag, 0.0), axis=1)[:, None]
    out_real = focal_real * anchor_real + focal_imag * anchor_imag
    out_imag = focal_imag * anchor_real - focal_real * anchor_imag
    return jnp.stack([out_real, out_imag], axis=1)


def solution(mesh):
    return jax.shard_map(
        body,
        mesh=mesh,
        in_specs=(P(None, "rcv", "src"), P(None, "rcv", "src"), P(), P(("rcv", "src"))),
        out_specs=P(("rcv", "src"), None, None),
        check_vma=False,
    )
```

profile of v0, /device:TPU:0, one launch (start us, length us, event | category | flops | bytes accessed | tf_op | source)
XLA Modules:
  0.0 370.4 jit_solution(2756795983004442803)
XLA Ops:
  6.5 1.9 copy.12
  8.6 14.5 %reshape.34 = bf16[2,8,256,4,256]{4,3,2,1,0:T(4,128)(2,1)} reshape(bf16[2,2048,1024]{2,1,0:T(8,128)(2,1)} %param.4) | data formatting | bytes 16777216 | tf_op jit(solution)/shard_map/reshape | solution.py:58
  23.9 25.1 %all-gather.3.cloned.1.call-done = bf16[2,2048,512]{1,0,2:T(2,128)(2,1)} async-done(((bf16[2,2048,32]{1,0,2:T(2,128)(2,1)}), bf16[2,2048,512]{1,0,2:T(2,128)(2,1)}) %all-gather.3.cloned.1.call-update) | async-done | bytes 4194320 | tf_op jit(solution)/shard_map/all_gather | solution.py:41
  49.0 4.4 %constant_dynamic-slice_fusion = bf16[2,1024,512]{1,0,2:T(2,128)(2,1)} fusion(bf16[2,2048,512]{1,0,2:T(2,128)(2,1)} %all-gather.3.cloned.1.call-done, s32[]{:T(128)S(6)} %select_n.49), kind=kLoop, calls=%fused_computation.52 | loop fusion | bytes 4194308 | tf_op jit(solution)/shard_map/dynamic_slice | solution.py:43
  53.3 4.7 %copy.19 = bf16[2,1024,512]{2,1,0:T(8,128)(2,1)S(1)} copy(bf16[2,1024,512]{1,0,2:T(2,128)(2,1)} %constant_dynamic-slice_fusion) | data formatting | bytes 4194304
  58.1 1.5 broadcast_select_fusion.2
  59.6 8.2 %broadcast_select_fusion.1 = (bf16[2,8,256,4,256]{4,3,2,1,0:T(4,128)(2,1)S(1)}, bf16[2,8,256,4,256]{4,3,2,1,0:T(4,128)(2,1)S(1)}) fusion(bf16[2,8,256,4,256]{4,3,2,1,0:T(4,128)(2,1)} %reshape.34, pred[8,4]{1,0:T(8,128)(4,1)S(1)} %get-tuple-element.10, pred[8,4]{1,0:T(8,128)(4,1)S(1)} %get-tuple-element.9), kind=kLoop, calls=%fused_computation.9 | loop fusion | flops 8388608 | bytes 25165888 | tf_op jit(solution)/shard_map/jit(_where)/select_n | solution.py:60
  67.8 6.2 %fusion.42 = (bf16[1,8,256,4,256]{4,3,2,1,0:T(4,128)(2,1)S(1)}, bf16[1,8,256,4,256]{4,3,2,1,0:T(4,128)(2,1)S(1)}, bf16[1,8,256,4,256]{4,3,2,1,0:T(4,128)(2,1)S(1)}, bf16[1,8,256,4,256]{4,3,2,1,0:T(4,128)(2,1)S(1)}) fusion(bf16[2,8,256,4,256]{4,3,2,1,0:T(4,128)(2,1)S(1)} %get-tuple-element.16, bf16[2,8,256,4,256]{4,3,2,1,0:T(4,128)(2,1)S(1)} %get-tuple-element.17), kind=kLoop, calls=%fused_computation.58 | loop fusion | bytes 33554432 | tf_op jit(solution)/shard_map/slice | solution.py:66
  74.0 3.0 copy.21
  77.0 3.0 copy.22
  80.0 3.0 copy.23
  83.0 3.0 copy.20
  86.0 6.9 %fusion.44 = (bf16[1,2048,512]{1,0,2:T(2,128)(2,1)}, bf16[1,2048,512]{1,0,2:T(2,128)(2,1)}) fusion(bf16[2,2048,512]{1,0,2:T(2,128)(2,1)S(1)} %copy-done), kind=kLoop, calls=%fused_computation.60 | loop fusion | bytes 8388608 | tf_op jit(solution)/shard_map/slice | solution.py:67
  92.9 9.0 %copy.17 = bf16[1,2048,512]{2,1,0:T(8,128)(2,1)S(1)} copy(bf16[1,2048,512]{1,0,2:T(2,128)(2,1)} %get-tuple-element.20) | data formatting | bytes 4194304
  101.9 10.5 %copy.18 = bf16[1,2048,512]{2,1,0:T(8,128)(2,1)} copy(bf16[1,2048,512]{1,0,2:T(2,128)(2,1)} %get-tuple-element.21) | data formatting | bytes 4194304
  112.4 22.6 %reduce-scatter.2.cloned.1.call-done = bf16[256,512]{1,0:T(8,128)(2,1)} async-done(((bf16[2048,512]{1,0:T(8,128)(2,1)}), bf16[256,512]{1,0:T(8,128)(2,1)}) %reduce-scatter.2.cloned.1.call-update) | async-done | bytes 262160 | tf_op jit(solution)/shard_map/reduce_scatter | solution.py:22
  135.3 27.2 %fusion = f32[4096,1024]{0,1:T(8,128)} fusion(bf16[2048,1024]{1,0:T(8,128)(2,1)} %bitcast.27, bf16[2048,1024]{1,0:T(8,128)(2,1)} %bitcast.26, bf16[2048,1024]{1,0:T(8,128)(2,1)} %bitcast.25, bf16[2048,1024]{1,0:T(8,128)(2,1)} %bitcast.28, bf16[2048,512]{1,0:T(8,128)(2,1)} %bitcast.30, bf16[2048,512]{1,0:T(8,128)(2,1)S(1)} %bitcast.29), kind=kOutput, calls=%fused_computation | convolution fusion | flops 17255366656 | bytes 37748736 | tf_op jit(solution)/shard_map/dot_general | solution.py:27
  162.4 2.8 fusion.40
  165.2 7.4 %fusion.27 = (bf16[1024,512]{0,1:T(8,128)(2,1)S(1)}, bf16[1024,512]{0,1:T(8,128)(2,1)}, bf16[1024,512]{0,1:T(8,128)(2,1)}) fusion(f32[4096,1024]{0,1:T(8,128)} %fusion), kind=kLoop, calls=%fused_computation.30 | loop fusion | flops 3145728 | bytes 15728640 | tf_op jit(solution)/shard_map/convert_element_type | solution.py:79
  172.7 17.7 %all-gather.5.cloned.1.call-done = bf16[2048,512]{1,0:T(8,128)(2,1)} async-done(((bf16[256,512]{1,0:T(8,128)(2,1)}), bf16[2048,512]{1,0:T(8,128)(2,1)}) %all-gather.5.cloned.1.call-update) | async-done | bytes 2097168 | tf_op jit(solution)/shard_map/all_gather | solution.py:23
  190.3 1.9 fusion.45
  192.5 2.4 fusion.11
  194.9 18.3 %fusion.34 = f32[512,1024]{1,0:T(8,128)} fusion(f32[512,1024]{1,0:T(8,128)S(1)} %fusion.11, bf16[2048,512]{1,0:T(8,128)(2,1)S(1)} %copy-done.1, bf16[1024,512]{0,1:T(8,128)(2,1)S(1)} %get-tuple-element.7, bf16[1024,512]{0,1:T(8,128)(2,1)S(1)} %get-tuple-element.11, bf16[1024,512]{0,1:T(8,128)(2,1)S(1)} %get-tuple-element.8), kind=kOutput, calls=%fused_computation.41 | convolution fusion | flops 2164785152 | bytes 9437184 | tf_op jit(solution)/shard_map/dot_general | solution.py:27
  213.2 148.3 %all-reduce.3.cloned.1.call-done = f32[512,1024]{1,0:T(8,128)} async-done(((f32[512,1024]{1,0:T(8,128)}), f32[512,1024]{1,0:T(8,128)}) %all-reduce.3.cloned.1.call-update) | async-done | bytes 2097168
  (25 shorter events, 3.8 us)
Async XLA Ops:
  6.5 42.5 %all-gather.3.cloned.1.call-start = ((), (), s32[]{:S(2)}) async-start(), calls=%async_computation.1 | async-start | bytes 4456448 | tf_op jit(solution)/shard_map/all_gather | solution.py:41
  8.5 126.5 %reduce-scatter.2.cloned.1.call-start = ((), (), s32[]{:S(2)}) async-start(), calls=%async_computation.2 | async-start | bytes 2359296 | tf_op jit(solution)/shard_map/reduce_scatter | solution.py:22
  59.6 130.8 %all-gather.5.cloned.1.call-start = ((), (), s32[]{:S(2)}) async-start(), calls=%async_computation.3 | async-start | bytes 2359296 | tf_op jit(solution)/shard_map/all_gather | solution.py:23
  83.0 3.0 copy-start
  135.0 226.5 %all-reduce.3.cloned.1.call-start = ((), (), s32[]{:S(2)}) async-start(), calls=%async_computation.4 | async-start | bytes 4194304
  190.3 1.9 copy-start.2
  190.3 2.2 copy-start.3
  192.5 2.4 copy-start.1
  194.9 166.6 %copy-start.4 = (s32[4]{0:T(128)S(1)}, s32[4]{0:T(128)}, u32[]{:S(2)}) copy-start(s32[4]{0:T(128)} %param.7) | copy-start | bytes 52
Sparse Core Ops, SparseCore 0:
  9.1 39.8 all-gather.2
  59.7 75.2 reduce-scatter.1
  137.4 52.9 all-gather.4
  213.3 148.1 all-reduce.2
where the time goes:
time: 372 us; the launch traced here: 370 us
  waiting for transfers between devices  214 us (58%)
  local copies, waits for them, and re-layouts  71.1 us (19%)
  matrix products  47.8 us (13%)
  other arithmetic  24.3 us (7%)
  between operations  13.2 us (4%)
    unnamed x5, waiting for transfers between devices  148 us
    dot_general x3, matrix products, across(): lax.dot_general(first, second, (((0,), (0,)), ((), ())), precision=precis...  47.8 us
    unnamed x18, local copies, waits for them, and re-layouts  38.4 us
    all_gather x1, waiting for transfers between devices, body(): green_block = lax.all_gather(green, 'src', axis=2, tiled=True)  25.1 us
    reduce_scatter x1, waiting for transfers between devices, spread(): own = lax.psum_scatter(padded, axis, scatter_dimension=0, tiled=True)  22.6 us
    all_gather x1, waiting for transfers between devices, spread(): lax.all_gather(own, axis, axis=0, tiled=True)[:len(lines)]  17.7 us
    reshape x1, local copies, waits for them, and re-layouts, body(): shaped = reflection.reshape(2, row_tiles_count, TILE, col_tiles_count, TILE)  14.5 us
    select_n x1, other arithmetic, body(): jnp.where(kept_tiles[None, :, None, :, None], shaped, zero_value)  8.16 us
  transfers between devices with their start and end apart: 4, of which 4 were waited for; matrix products, arithmetic and copies ran while one was open for 28% of the time, Pallas kernels for 0%

commit v1 on v0

v1 whole, which is shorter than its diff:
```python
import jax
import jax.numpy as jnp
from jax import lax
from jax.experimental import pallas as pl
from jax.experimental.pallas import tpu as pltpu
from jax.sharding import Mesh, PartitionSpec as P

P_SIZE = 512
TILE = 256
PARTS = (("xh", 2), ("z", 4), ("y", 4), ("xl", 2), ("core", 2))
RCV = ("xh", "z")
SRC = ("y", "xl", "core")
ALL = RCV + SRC
CHIPS = RCV + SRC[:2]
ROWS = 2048
COLS = 1024
ROW_TILES = ROWS // TILE
COL_TILES = COLS // TILE
SHARD = 32
N_CHIPS = 64
SWAP = [(0, 1), (1, 0)]


def place(xh, z, y, xl, core):
    return (((xh * 4 + z) * 4 + y) * 2 + xl) * 2 + core


def crossing(cross):
    return [
        (place(xh, z, y, xl, core), place(xl, y, 2 * xh + z // 2, z % 2, core ^ cross))
        for xh in range(2)
        for z in range(4)
        for y in range(4)
        for xl in range(2)
        for core in range(2)
    ]


def ring(step):
    return [(i, (i + step) % 4) for i in range(4)]


def dot(a, b):
    return lax.dot_general(a, b, (((1,), (0,)), ((), ())), preferred_element_type=jnp.float32)


def dot_nt(a, b):
    return lax.dot_general(a, b, (((1,), (1,)), ((), ())), preferred_element_type=jnp.float32)


def project_kernel(st, gk, a, out, gbuf, abuf, obuf, real_acc, imag_acc, gsem, asem, osem):
    half = P_SIZE

    def g_copy(r):
        return pltpu.make_async_copy(
            gk.at[:, pl.ds(r * TILE, TILE)], gbuf.at[:, pl.ds(r * TILE, TILE)], gsem.at[r]
        )

    def a_copy(c):
        return pltpu.make_async_copy(a.at[:, :, pl.ds(c * TILE, TILE)], abuf.at[c], asem.at[c])

    def o_copy(c):
        return pltpu.make_async_copy(
            obuf.at[:, :, pl.ds(c * TILE, TILE)], out.at[:, :, pl.ds(c * TILE, TILE)], osem.at[c]
        )

    @pl.when(st[32] != 0)
    def _():
        a_copy(0).start()
        for r in range(ROW_TILES):
            g_copy(r).start()
        for c in range(1, COL_TILES):
            a_copy(c).start()
        for r in range(ROW_TILES):
            g_copy(r).wait()

        def column(c, carry):
            a_copy(c).wait()
            real_acc[...] = jnp.zeros_like(real_acc)
            imag_acc[...] = jnp.zeros_like(imag_acc)
            lanes = pl.ds(pl.multiple_of(c * TILE, TILE), TILE)
            for r in range(ROW_TILES):

                @pl.when(st[r * COL_TILES + c] == 1)
                def _():
                    g = gbuf[:, r * TILE : (r + 1) * TILE]
                    real_acc[...] += dot(g, abuf[c, 0, r * TILE : (r + 1) * TILE, :])
                    imag_acc[...] += dot(g, abuf[c, 1, r * TILE : (r + 1) * TILE, :])

            obuf[2, :, lanes] = (real_acc[:half] - imag_acc[half:]).astype(jnp.bfloat16)
            obuf[3, :, lanes] = (imag_acc[:half] + real_acc[half:]).astype(jnp.bfloat16)

            @pl.when(st[36 + c] == 1)
            def _():
                rows = pl.ds(pl.multiple_of(st[40 + c] * TILE, TILE), TILE)
                g = gbuf[:, rows]
                real_acc[...] += dot(g, abuf[c, 0, rows, :])
                imag_acc[...] += dot(g, abuf[c, 1, rows, :])

            obuf[0, :, lanes] = (real_acc[:half] + imag_acc[half:]).astype(jnp.bfloat16)
            obuf[1, :, lanes] = (imag_acc[:half] - real_acc[half:]).astype(jnp.bfloat16)
            return carry

        lax.fori_loop(0, COL_TILES, column, 0)
        for c in range(COL_TILES):
            o_copy(c).start()
        for c in range(COL_TILES):
            o_copy(c).wait()


def focus_kernel(st, fb, own, near, after, before, far_a, far_b, keep, send, fbuf, gbuf, acc_r, acc_i, fsem, gsem):
    core = st[33]
    xh = st[34]
    z = st[35]

    def f_copy(c):
        return pltpu.make_async_copy(
            fb.at[:, :, pl.ds(c * TILE, TILE)], fbuf.at[:, :, pl.ds(c * TILE, TILE)], fsem.at[c]
        )

    def g_copies():
        copies = []

        def add(ref, x_other, z_step, part):
            block = 2 * ((z + z_step + 4) % 4) + (1 - xh if x_other else xh)
            slot = core if part == 0 else 1 - core
            row = pl.multiple_of(block * 64 + slot * SHARD, SHARD)
            copies.append(
                pltpu.make_async_copy(ref, gbuf.at[:, pl.ds(row, SHARD), :], gsem.at[len(copies)])
            )

        for part in range(2):
            add(own.at[part], False, 0, part)
            add(near.at[part], True, 0, part)
        for x_other in range(2):
            for part in range(2):
                add(after.at[x_other, part], x_other, -1, part)
                add(before.at[x_other, part], x_other, 1, part)
        for x_other in range(2):
            add(far_a.at[x_other], x_other, 2, 0)
            add(far_b.at[x_other], x_other, 2, 1)
        return copies

    sub = lax.broadcasted_iota(jnp.int32, (N_CHIPS, 8, P_SIZE), 1)
    low = sub < 4

    @pl.when(st[32] != 0)
    def _():
        copies = g_copies()
        for copy in copies:
            copy.start()
        for c in range(COL_TILES):
            f_copy(c).start()
        for copy in copies:
            copy.wait()
        for c in range(COL_TILES):
            f_copy(c).wait()
            cols = slice(c * TILE, (c + 1) * TILE)
            gr = gbuf[0, :, cols]
            gi = gbuf[1, :, cols]
            br = fbuf[2, :, cols]
            bi = fbuf[3, :, cols]
            left = jnp.concatenate([fbuf[0, :, cols], fbuf[1, :, cols], gr, gi], axis=1)
            right_r = jnp.concatenate([gr, -gi, br, bi], axis=1)
            right_i = jnp.concatenate([gi, gr, bi, -br], axis=1)
            if c == 0:
                acc_r[...] = dot_nt(left, right_r)
                acc_i[...] = dot_nt(left, right_i)
            else:
                acc_r[...] += dot_nt(left, right_r)
                acc_i[...] += dot_nt(left, right_i)
        re = acc_r[...].reshape(N_CHIPS, 8, P_SIZE)
        im = acc_i[...].reshape(N_CHIPS, 8, P_SIZE)
        first = jnp.where(low, re, pltpu.roll(im, 4, 1)).astype(jnp.bfloat16)
        second = jnp.where(low, pltpu.roll(re, 4, 1), im).astype(jnp.bfloat16)

        @pl.when(core == 0)
        def _():
            keep[...] = first
            send[...] = second

        @pl.when(core != 0)
        def _():
            keep[...] = second
            send[...] = first

    @pl.when(st[32] == 0)
    def _():
        keep[...] = jnp.zeros_like(keep)
        send[...] = jnp.zeros_like(send)


def align_kernel(index, parts, out):
    total = jnp.sum(parts[...].astype(jnp.float32), axis=0)
    lane = lax.broadcasted_iota(jnp.int32, (1, P_SIZE), 1)
    for i in range(4):
        re = total[i : i + 1]
        im = total[4 + i : 5 + i]
        chosen = lane == index[i]
        anchor_re = jnp.sum(jnp.where(chosen, re, 0.0), axis=1, keepdims=True)
        anchor_im = jnp.sum(jnp.where(chosen, im, 0.0), axis=1, keepdims=True)
        out[i, 0:1, :] = re * anchor_re + im * anchor_im
        out[i, 1:2, :] = im * anchor_re - re * anchor_im


def any_spec():
    return pl.BlockSpec(memory_space=pl.ANY)


def smem_spec():
    return pl.BlockSpec(memory_space=pltpu.SMEM)


def vmem_spec():
    return pl.BlockSpec(memory_space=pltpu.VMEM)


def tile_states(tile_mask):
    rcv = lax.axis_index(RCV)
    src = lax.axis_index(SRC)
    tiles = lax.dynamic_slice(tile_mask, (rcv * ROW_TILES, src * COL_TILES), (ROW_TILES, COL_TILES))
    kept = (tiles == 1).astype(jnp.int32)
    rows = jnp.arange(ROW_TILES)[:, None] + rcv * ROW_TILES
    cols = jnp.arange(COL_TILES)[None, :] + src * COL_TILES
    diag = (rows == cols).astype(jnp.int32)
    state = kept * (1 + diag)
    diag_row = jnp.clip(cols[0] - rcv * ROW_TILES, 0, ROW_TILES - 1)
    diag_on = jnp.max(kept * diag, axis=0)
    scalars = jnp.stack(
        [jnp.max(kept), lax.axis_index("core"), lax.axis_index("xh"), lax.axis_index("z")]
    )
    return jnp.concatenate([state.reshape(-1), scalars, diag_on, diag_row]).astype(jnp.int32)


def body(reflection, green, tile_mask, reference_index):
    lines = jnp.transpose(green, (0, 2, 1))
    gathered = lax.all_gather(lines, SRC, axis=1, tiled=True)
    state = tile_states(tile_mask)
    core = lax.axis_index("core")
    mid = ROWS // 2
    same = lax.dynamic_slice_in_dim(lines, core * mid, mid, 2)
    other = lax.dynamic_slice_in_dim(lines, (1 - core) * mid, mid, 2)
    own = jnp.stack([lax.ppermute(same, ALL, crossing(0)), lax.ppermute(other, ALL, crossing(1))])
    near = lax.ppermute(own, "xh", SWAP)
    pair = jnp.stack([own, near])
    after = lax.ppermute(pair, "z", ring(1))
    before = lax.ppermute(pair, "z", ring(-1))
    far_a = lax.ppermute(after[:, 0], "z", ring(1))
    far_b = lax.ppermute(before[:, 1], "z", ring(-1))

    fb = pl.pallas_call(
        project_kernel,
        out_shape=jax.ShapeDtypeStruct((4, P_SIZE, COLS), jnp.bfloat16),
        in_specs=[smem_spec(), any_spec(), any_spec()],
        out_specs=any_spec(),
        scratch_shapes=[
            pltpu.VMEM((2 * P_SIZE, ROWS), jnp.bfloat16),
            pltpu.VMEM((COL_TILES, 2, ROWS, TILE), jnp.bfloat16),
            pltpu.VMEM((4, P_SIZE, COLS), jnp.bfloat16),
            pltpu.VMEM((2 * P_SIZE, TILE), jnp.float32),
            pltpu.VMEM((2 * P_SIZE, TILE), jnp.float32),
            pltpu.SemaphoreType.DMA((ROW_TILES,)),
            pltpu.SemaphoreType.DMA((COL_TILES,)),
            pltpu.SemaphoreType.DMA((COL_TILES,)),
        ],
        compiler_params=pltpu.CompilerParams(vmem_limit_bytes=40 << 20),
        cost_estimate=pl.CostEstimate(flops=8 << 30, transcendentals=0, bytes_accessed=16 << 20),
        name="project",
    )(state, gathered.reshape(2 * P_SIZE, ROWS), reflection)

    block = jax.ShapeDtypeStruct((N_CHIPS, 8, P_SIZE), jnp.bfloat16)
    keep, send = pl.pallas_call(
        focus_kernel,
        out_shape=(block, block),
        in_specs=[smem_spec()] + [any_spec()] * 7,
        out_specs=(vmem_spec(), vmem_spec()),
        scratch_shapes=[
            pltpu.VMEM((4, P_SIZE, COLS), jnp.bfloat16),
            pltpu.VMEM((2, P_SIZE, COLS), jnp.bfloat16),
            pltpu.VMEM((P_SIZE, P_SIZE), jnp.float32),
            pltpu.VMEM((P_SIZE, P_SIZE), jnp.float32),
            pltpu.SemaphoreType.DMA((COL_TILES,)),
            pltpu.SemaphoreType.DMA((16,)),
        ],
        compiler_params=pltpu.CompilerParams(vmem_limit_bytes=40 << 20),
        cost_estimate=pl.CostEstimate(flops=4 << 30, transcendentals=0, bytes_accessed=8 << 20),
        name="focus",
    )(state, fb, own, near, after, before, far_a, far_b)
    taken = lax.ppermute(send, "core", SWAP)
    summed = (keep.astype(jnp.float32) + taken.astype(jnp.float32)).astype(jnp.bfloat16)
    parts = lax.all_to_all(summed, CHIPS, 0, 0)
    return pl.pallas_call(
        align_kernel,
        out_shape=jax.ShapeDtypeStruct((4, 2, P_SIZE), jnp.float32),
        in_specs=[smem_spec(), vmem_spec()],
        out_specs=vmem_spec(),
        name="align",
    )(reference_index, parts)


def solution(mesh):
    fine = Mesh(mesh.devices.reshape([size for _, size in PARTS]), [name for name, _ in PARTS])
    return jax.shard_map(
        body,
        mesh=fine,
        in_specs=(P(None, RCV, SRC), P(None, RCV, SRC), P(), P(ALL)),
        out_specs=P(ALL, None, None),
        check_vma=False,
    )
```

time: 372 us -> 117 us (0.31)
  waiting for transfers between devices: 214 us -> 24.5 us
  local copies, waits for them, and re-layouts: 71.1 us -> 4.13 us
  matrix products: 47.8 us -> 0 us
  starting transfers between devices: 0.3 us -> 29.8 us
  blocking collectives: 0 us -> 23.6 us
  other arithmetic: 24.3 us -> 1.79 us
  Pallas kernels: 0 us -> 19 us
    unnamed x5 -> x1, waiting for transfers between devices: 148 us -> 0.71 us
    dot_general x3 -> x0, matrix products: 47.8 us -> none  [across(): lax.dot_general(first, second, (((0,), (0,)), ((), ())), precision=precis...]
    all_gather x2 -> x1, waiting for transfers between devices: 42.8 us -> 0.02 us  [body(): gathered = lax.all_gather(lines, SRC, axis=1, tiled=True)]
    unnamed x18 -> x2, local copies, waits for them, and re-layouts: 38.4 us -> 2.18 us
    ppermute x0 -> x8, starting transfers between devices: none -> 29.8 us  [the longest x1 13.5 us: body(): near = lax.ppermute(own, 'xh', SWAP)]
    ppermute x0 -> x8, waiting for transfers between devices: none -> 23.8 us  [the longest x1 12 us: body(): near = lax.ppermute(own, 'xh', SWAP)]
    all_to_all x0 -> x1, blocking collectives: none -> 23.6 us  [body(): parts = lax.all_to_all(summed, CHIPS, 0, 0)]
    reduce_scatter x1 -> x0, waiting for transfers between devices: 22.6 us -> none  [spread(): own = lax.psum_scatter(padded, axis, scatter_dimension=0, tiled=True)]
  transfers between devices with their start and end apart: 4 -> 9, of which waited for: 4 -> 5; matrix products, arithmetic and copies ran while one was open for 28% -> 3% of each run, Pallas kernels for 0% -> 8%
where the time goes in v1:
time: 117 us; the launch traced here: 116 us
  starting transfers between devices  29.8 us (25%)
  waiting for transfers between devices  24.5 us (21%)
  blocking collectives  23.6 us (20%)
  Pallas kernels  19 us (16%)
  between operations  13.5 us (12%)
  local copies, waits for them, and re-layouts  4.13 us (4%)
  other arithmetic  1.79 us (2%)
    all_to_all x1, blocking collectives, body(): parts = lax.all_to_all(summed, CHIPS, 0, 0)  23.6 us
    ppermute x1, starting transfers between devices, body(): near = lax.ppermute(own, 'xh', SWAP)  13.5 us
    ppermute x1, waiting for transfers between devices, body(): near = lax.ppermute(own, 'xh', SWAP)  12 us
    pallas_call x1, Pallas kernels, body(): pl.pallas_call(project_kernel, out_shape=jax.ShapeDtypeStruct((4, P_SIZE,...  9.08 us
    ppermute x1, waiting for transfers between devices, body(): after = lax.ppermute(pair, 'z', ring(1))  8.94 us
    pallas_call x1, Pallas kernels, body(): pl.pallas_call(focus_kernel, out_shape=(block, block), in_specs=[smem_spe...  8.11 us
    ppermute x1, starting transfers between devices, body(): before = lax.ppermute(pair, 'z', ring(-1))  5.65 us
    ppermute x1, starting transfers between devices, body(): after = lax.ppermute(pair, 'z', ring(1))  4.75 us
  transfers between devices with their start and end apart: 9, of which 5 were waited for; matrix products, arithmetic and copies ran while one was open for 3% of the time, Pallas kernels for 8%

profile of v1, /device:TPU:0, one launch (start us, length us, event | category | flops | bytes accessed | tf_op | source)
XLA Modules:
  0.0 116.3 jit_solution(3144345573609203788)
XLA Ops:
  6.5 0.7 all-gather.2.cloned.1.call-update
  7.3 1.0 dynamic-slice_bitcast_fusion.1
  8.3 0.1 collective-permute-start.1
  8.3 0.7 collective-permute-start
  9.0 0.7 collective-permute-done.1
  9.7 13.5 %collective-permute-start.2 = (bf16[2,2,32,1024]{3,2,1,0:T(8,128)(2,1)S(1)}, bf16[2,2,32,1024]{3,2,1,0:T(8,128)(2,1)S(1)}, u32[]{:S(2)}, u32[]{:S(2)}) collective-permute-start(bf16[2,2,32,1024]{3,2,1,0:T(8,128)(2,1)S(1)} %get-tuple-element.13.own), channel_id=1, source_target_pairs={{0,64},{64,0},{1,65},{65,1},{2,66},{66,2},{3,67},{67,3},{4,68},{68... | collective-permute-start | bytes 786440 | tf_op jit(solution)/shard_map/ppermute | solution.py:244
  23.3 12.0 %collective-permute-done.2.near = bf16[2,2,32,1024]{3,2,1,0:T(8,128)(2,1)S(1)} collective-permute-done((bf16[2,2,32,1024]{3,2,1,0:T(8,128)(2,1)S(1)}, bf16[2,2,32,1024]{3,2,1,0:T(8,128)(2,1)S(1)}, u32[]{:S(2)}, u32[]{:S(2)}) %collective-permute-start.2) | collective-permute-done | bytes 262176 | tf_op jit(solution)/shard_map/ppermute | solution.py:244
  35.3 4.7 %collective-permute-start.3 = (bf16[2,2,2,32,1024]{4,3,2,0,1:T(8,128)(2,1)S(1)}, bf16[2,2,2,32,1024]{4,3,2,0,1:T(8,128)(2,1)S(1)}, u32[]{:S(2)}, u32[]{:S(2)}) collective-permute-start(bf16[2,2,2,32,1024]{4,3,2,0,1:T(8,128)(2,1)S(1)} %pad_maximum_fusion), channel_id=1, source_target_pairs={{0,16},{16,32},{32,48},{48,0},{1,17},{17,33},{33,49},{49,1},{2,18}... | collective-permute-start | bytes 1572872 | tf_op jit(solution)/shard_map/ppermute | solution.py:246
  40.1 1.5 %fusion.2 = (s32[4]{0:T(128)S(1)}, s32[]{:T(128)}, pred[8,4]{1,0:T(8,128)(4,1)S(1)}) fusion(s32[4]{0:T(128)S(1)} %iota_add_fusion, s32[8]{0:T(128)S(1)} %iota_add_fusion.1, s32[64,64]{1,0:T(8,128)} %param.6, s32[]{:T(128)S(6)} %select_n.12, s32[]{:T(128)S(6)} %select_n.13), kind=kLoop, calls=%fused_computation.12 | loop fusion | flops 187 | bytes 236 | tf_op jit(solution)/shard_map/reduce_max | solution.py:228
  41.5 5.6 %collective-permute-start.4 = (bf16[2,2,2,32,1024]{4,3,2,0,1:T(8,128)(2,1)S(1)}, bf16[2,2,2,32,1024]{4,3,2,0,1:T(8,128)(2,1)S(1)}, u32[]{:S(2)}, u32[]{:S(2)}) collective-permute-start(bf16[2,2,2,32,1024]{4,3,2,0,1:T(8,128)(2,1)S(1)} %pad_maximum_fusion), channel_id=1, source_target_pairs={{0,48},{16,0},{32,16},{48,32},{1,49},{17,1},{33,17},{49,33},{2,50}... | collective-permute-start | bytes 1572872 | tf_op jit(solution)/shard_map/ppermute | solution.py:247
  47.3 0.1 reshape.17
  47.4 0.8 concatenate.3.st
  48.1 8.9 %collective-permute-done.3 = bf16[2,2,2,32,1024]{4,3,2,0,1:T(8,128)(2,1)S(1)} collective-permute-done((bf16[2,2,2,32,1024]{4,3,2,0,1:T(8,128)(2,1)S(1)}, bf16[2,2,2,32,1024]{4,3,2,0,1:T(8,128)(2,1)S(1)}, u32[]{:S(2)}, u32[]{:S(2)}) %collective-permute-start.3) | collective-permute-done | bytes 524320 | tf_op jit(solution)/shard_map/ppermute | solution.py:246
  57.1 0.1 collective-permute-start.5
  57.2 0.7 collective-permute-done.4
  57.9 3.8 %collective-permute-start.6 = (bf16[2,2,32,1024]{3,2,1,0:T(8,128)(2,1)S(1)}, bf16[2,2,32,1024]{3,2,1,0:T(8,128)(2,1)S(1)}, u32[]{:S(2)}, u32[]{:S(2)}) collective-permute-start(bf16[2,2,32,1024]{3,2,1,0:T(8,128)(2,1)S(1)} %slice_bitcast_fusion), channel_id=1, source_target_pairs={{0,48},{16,0},{32,16},{48,32},{1,49},{17,1},{33,17},{49,33},{2,50}... | collective-permute-start | bytes 786440 | tf_op jit(solution)/shard_map/ppermute | solution.py:249
  61.7 2.2 %copy-done = bf16[2,512,2048]{2,1,0:T(8,128)(2,1)S(1)} copy-done((bf16[2,512,2048]{2,1,0:T(8,128)(2,1)S(1)}, bf16[2,512,2048]{2,1,0:T(8,128)(2,1)}, u32[]{:S(2)}) %copy-start) | copy-done | bytes 4194328
  63.9 9.1 %project.1.fb = bf16[4,512,1024]{2,1,0:T(8,128)(2,1)S(1)} custom-call(s32[44]{0:T(128)S(1)} %concatenate.3.st, bf16[1024,2048]{1,0:T(8,128)(2,1)S(1)} %bitcast.22, bf16[2,2048,1024]{2,1,0:T(8,128)(2,1)} %a.1), custom_call_target="tpu_custom_call" | custom-call | flops 8589934592 | bytes 16777216 | tf_op jit(solution)/shard_map/project/pallas_call | solution.py:251
  73.0 8.1 %focus.1 = (bf16[64,8,512]{2,1,0:T(8,128)(2,1)S(1)}, bf16[64,8,512]{2,1,0:T(8,128)(2,1)S(1)}) custom-call(s32[44]{0:T(128)S(1)} %concatenate.3.st, bf16[4,512,1024]{2,1,0:T(8,128)(2,1)S(1)} %project.1.fb, bf16[2,2,32,1024]{3,2,1,0:T(8,128)(2,1)S(1)} %get-tuple-element.13.own, bf16[2,2,32,1024]{3,2,1,0:T(8,128)(2,1)S(1)} %collective-permute-done.2.near, ...), custom_call_target="tpu_custom_call" | custom-call | flops 4294967296 | bytes 8388608 | tf_op jit(solution)/shard_map/focus/pallas_call | solution.py:272
  81.1 1.3 %collective-permute-start.7 = (bf16[64,8,512]{2,1,0:T(8,128)(2,1)S(1)}, bf16[64,8,512]{2,1,0:T(8,128)(2,1)S(1)}, u32[]{:S(2)}, u32[]{:S(2)}) collective-permute-start(bf16[64,8,512]{2,1,0:T(8,128)(2,1)S(1)} %get-tuple-element.8), channel_id=1, source_target_pairs={{0,1},{1,0},{2,3},{3,2},{4,5},{5,4},{6,7},{7,6},{8,9},{9,8},{10,11... | collective-permute-start | bytes 1572872 | tf_op jit(solution)/shard_map/ppermute | solution.py:289
  82.4 1.5 %collective-permute-done.7 = bf16[64,8,512]{2,1,0:T(8,128)(2,1)S(1)} collective-permute-done((bf16[64,8,512]{2,1,0:T(8,128)(2,1)S(1)}, bf16[64,8,512]{2,1,0:T(8,128)(2,1)S(1)}, u32[]{:S(2)}, u32[]{:S(2)}) %collective-permute-start.7) | collective-permute-done | bytes 524320 | tf_op jit(solution)/shard_map/ppermute | solution.py:289
  84.0 0.1 add_convert_fusion
  84.1 23.6 %all_to_all.5.parts = bf16[64,8,512]{2,1,0:T(8,128)(2,1)} all-to-all(bf16[64,8,512]{2,1,0:T(8,128)(2,1)S(1)} %add_convert_fusion), channel_id=1, replica_groups=mesh['xh'=2,'z'=4,'y'=4,'xl'=2,'core'=2] {'xh','z','y','xl'}, dimensions={0} | all-to-all | bytes 1048576 | tf_op jit(solution)/shard_map/all_to_all | solution.py:291
  107.7 1.8 %align.1 = f32[4,2,512]{2,1,0:T(2,128)} custom-call(s32[4]{0:T(128)} %index.1, bf16[64,8,512]{2,1,0:T(8,128)(2,1)} %all_to_all.5.parts), custom_call_target="tpu_custom_call" | custom-call | tf_op jit(solution)/shard_map/align/pallas_call | solution.py:292
  (16 shorter events, 0.3 us)
Async XLA Ops:
  6.5 55.2 %all-gather.2.cloned.1.call-start = ((), (), s32[]{:S(2)}) async-start(), calls=%async_computation.1 | async-start | bytes 4456448 | tf_op jit(solution)/shard_map/all_gather | solution.py:237
  8.3 1.4 %collective-permute-start.1 = (bf16[2,32,1024]{2,1,0:T(8,128)(2,1)S(1)}, bf16[2,32,1024]{2,1,0:T(8,128)(2,1)S(1)}, u32[]{:S(2)}, u32[]{:S(2)}) collective-permute-start(bf16[2,32,1024]{2,1,0:T(8,128)(2,1)S(1)} %get-tuple-element.15), channel_id=1, source_target_pairs={{0,1},{1,0},{2,65},{3,64},{4,17},{5,16},{6,81},{7,80},{8,33},{9,32... | collective-permute-start | bytes 393224 | tf_op jit(solution)/shard_map/ppermute | solution.py:243
  8.3 1.3 %collective-permute-start = (bf16[2,32,1024]{2,1,0:T(8,128)(2,1)S(1)}, bf16[2,32,1024]{2,1,0:T(8,128)(2,1)S(1)}, u32[]{:S(2)}, u32[]{:S(2)}) collective-permute-start(bf16[2,32,1024]{2,1,0:T(8,128)(2,1)S(1)} %get-tuple-element.14), channel_id=1, source_target_pairs={{0,0},{1,1},{2,64},{3,65},{4,16},{5,17},{6,80},{7,81},{8,32},{9,33... | collective-permute-start | bytes 393224 | tf_op jit(solution)/shard_map/ppermute | solution.py:243
  9.7 25.5 %collective-permute-start.2 = (bf16[2,2,32,1024]{3,2,1,0:T(8,128)(2,1)S(1)}, bf16[2,2,32,1024]{3,2,1,0:T(8,128)(2,1)S(1)}, u32[]{:S(2)}, u32[]{:S(2)}) collective-permute-start(bf16[2,2,32,1024]{3,2,1,0:T(8,128)(2,1)S(1)} %get-tuple-element.13.own), channel_id=1, source_target_pairs={{0,64},{64,0},{1,65},{65,1},{2,66},{66,2},{3,67},{67,3},{4,68},{68... | collective-permute-start | bytes 786440 | tf_op jit(solution)/shard_map/ppermute | solution.py:244
  35.3 21.8 %collective-permute-start.3 = (bf16[2,2,2,32,1024]{4,3,2,0,1:T(8,128)(2,1)S(1)}, bf16[2,2,2,32,1024]{4,3,2,0,1:T(8,128)(2,1)S(1)}, u32[]{:S(2)}, u32[]{:S(2)}) collective-permute-start(bf16[2,2,2,32,1024]{4,3,2,0,1:T(8,128)(2,1)S(1)} %pad_maximum_fusion), channel_id=1, source_target_pairs={{0,16},{16,32},{32,48},{48,0},{1,17},{17,33},{33,49},{49,1},{2,18}... | collective-permute-start | bytes 1572872 | tf_op jit(solution)/shard_map/ppermute | solution.py:246
  41.5 16.3 %collective-permute-start.4 = (bf16[2,2,2,32,1024]{4,3,2,0,1:T(8,128)(2,1)S(1)}, bf16[2,2,2,32,1024]{4,3,2,0,1:T(8,128)(2,1)S(1)}, u32[]{:S(2)}, u32[]{:S(2)}) collective-permute-start(bf16[2,2,2,32,1024]{4,3,2,0,1:T(8,128)(2,1)S(1)} %pad_maximum_fusion), channel_id=1, source_target_pairs={{0,48},{16,0},{32,16},{48,32},{1,49},{17,1},{33,17},{49,33},{2,50}... | collective-permute-start | bytes 1572872 | tf_op jit(solution)/shard_map/ppermute | solution.py:247
  57.1 15.9 %collective-permute-start.5 = (bf16[2,2,32,1024]{3,2,1,0:T(8,128)(2,1)S(1)}, bf16[2,2,32,1024]{3,2,1,0:T(8,128)(2,1)S(1)}, u32[]{:S(2)}, u32[]{:S(2)}) collective-permute-start(bf16[2,2,32,1024]{3,2,1,0:T(8,128)(2,1)S(1)} %slice_bitcast_fusion.1), channel_id=1, source_target_pairs={{0,16},{16,32},{32,48},{48,0},{1,17},{17,33},{33,49},{49,1},{2,18}... | collective-permute-start | bytes 786440 | tf_op jit(solution)/shard_map/ppermute | solution.py:248
  57.9 15.2 %collective-permute-start.6 = (bf16[2,2,32,1024]{3,2,1,0:T(8,128)(2,1)S(1)}, bf16[2,2,32,1024]{3,2,1,0:T(8,128)(2,1)S(1)}, u32[]{:S(2)}, u32[]{:S(2)}) collective-permute-start(bf16[2,2,32,1024]{3,2,1,0:T(8,128)(2,1)S(1)} %slice_bitcast_fusion), channel_id=1, source_target_pairs={{0,48},{16,0},{32,16},{48,32},{1,49},{17,1},{33,17},{49,33},{2,50}... | collective-permute-start | bytes 786440 | tf_op jit(solution)/shard_map/ppermute | solution.py:249
  61.7 2.2 %copy-start = (bf16[2,512,2048]{2,1,0:T(8,128)(2,1)S(1)}, bf16[2,512,2048]{2,1,0:T(8,128)(2,1)}, u32[]{:S(2)}) copy-start(bf16[2,512,2048]{2,1,0:T(8,128)(2,1)} %all-gather.2.cloned.1.call-done) | copy-start | bytes 12582916
  81.1 2.8 %collective-permute-start.7 = (bf16[64,8,512]{2,1,0:T(8,128)(2,1)S(1)}, bf16[64,8,512]{2,1,0:T(8,128)(2,1)S(1)}, u32[]{:S(2)}, u32[]{:S(2)}) collective-permute-start(bf16[64,8,512]{2,1,0:T(8,128)(2,1)S(1)} %get-tuple-element.8), channel_id=1, source_target_pairs={{0,1},{1,0},{2,3},{3,2},{4,5},{5,4},{6,7},{7,6},{8,9},{9,8},{10,11... | collective-permute-start | bytes 1572872 | tf_op jit(solution)/shard_map/ppermute | solution.py:289
Sparse Core Ops, SparseCore 0:
  9.0 45.5 all-gather.1

commit v2 on v1

v2 whole, which is shorter than its diff:
```python
import jax
import jax.numpy as jnp
from jax import lax
from jax.experimental import pallas as pl
from jax.experimental.pallas import tpu as pltpu
from jax.sharding import Mesh, PartitionSpec as P

P_SIZE = 512
TILE = 256
PARTS = (("xh", 2), ("z", 4), ("y", 4), ("xl", 2), ("core", 2))
RCV = ("xh", "z")
SRC = ("y", "xl", "core")
ALL = RCV + SRC
CHIPS = RCV + SRC[:2]
ROWS = 2048
COLS = 1024
ROW_TILES = ROWS // TILE
COL_TILES = COLS // TILE
SHARD = 32
N_CHIPS = 64
SWAP = [(0, 1), (1, 0)]


def place(xh, z, y, xl, core):
    return (((xh * 4 + z) * 4 + y) * 2 + xl) * 2 + core


def crossing(cross):
    return [
        (place(xh, z, y, xl, core), place(xl, y, 2 * xh + z // 2, z % 2, core ^ cross))
        for xh in range(2)
        for z in range(4)
        for y in range(4)
        for xl in range(2)
        for core in range(2)
    ]


def ring(step):
    return [(i, (i + step) % 4) for i in range(4)]


def dot(a, b):
    return lax.dot_general(a, b, (((1,), (0,)), ((), ())), preferred_element_type=jnp.float32)


def dot_nt(a, b):
    return lax.dot_general(a, b, (((1,), (1,)), ((), ())), preferred_element_type=jnp.float32)


def project_kernel(st, own, after, before, far_a, far_b, swap, swap_far, a, out, gbuf, abuf, acc, gsem, asem):
    half = P_SIZE
    core = st[49]
    xl = st[52]
    y = st[53]
    mid = ROWS // 2

    def g_copies():
        copies = []

        def add(ref, x_other, y_step, other, lanes):
            line = 4 * ((y + y_step + 4) % 4) + 2 * (1 - xl if x_other else xl)
            row = pl.multiple_of((line + (1 - core if other else core)) * SHARD, SHARD)
            target = gbuf.at[:, pl.ds(row, SHARD), lanes]
            copies.append(pltpu.make_async_copy(ref, target, gsem.at[len(copies)]))

        whole = pl.ds(0, ROWS)
        low = pl.ds(0, mid)
        high = pl.ds(mid, mid)
        for x in range(2):
            add(own.at[x], x, 0, False, whole)
            add(after.at[x], x, -1, False, whole)
            add(before.at[x], x, 1, False, whole)
            add(far_a.at[x], x, 2, False, low)
            add(far_b.at[x], x, 2, False, high)
        for x in range(2):
            add(swap.at[0, x], x, 0, True, whole)
            add(swap.at[1, x], x, -1, True, whole)
            add(swap.at[2, x], x, 1, True, whole)
            add(swap_far.at[0, x], x, 2, True, low)
            add(swap_far.at[1, x], x, 2, True, high)
        return copies

    def a_copy(c, i):
        row = pl.multiple_of(st[8 + c * ROW_TILES + i] * TILE, TILE)
        return pltpu.make_async_copy(
            a.at[:, pl.ds(row, TILE), pl.ds(c * TILE, TILE)],
            abuf.at[c, :, pl.ds(i * TILE, TILE), :],
            asem.at[c, i],
        )

    def d_copy(c):
        row = pl.multiple_of(st[44 + c] * TILE, TILE)
        return pltpu.make_async_copy(
            a.at[:, pl.ds(row, TILE), pl.ds(c * TILE, TILE)],
            abuf.at[c, :, pl.ds(ROWS, TILE), :],
            asem.at[c, ROW_TILES],
        )

    @pl.when(st[48] != 0)
    def _():
        copies = g_copies()
        for copy in copies:
            copy.start()
        for c in range(COL_TILES):
            for i in range(ROW_TILES):

                @pl.when(i < st[c])
                def _():
                    a_copy(c, i).start()

            @pl.when(st[40 + c] != 0)
            def _():
                d_copy(c).start()

        for copy in copies:
            copy.wait()

        def column(c, carry):
            n = st[c]
            lanes = pl.ds(pl.multiple_of(c * TILE, TILE), TILE)

            def product(tiles, start):
                left = jnp.concatenate(
                    [
                        gbuf[:, :, pl.ds(pl.multiple_of(t * TILE, TILE), TILE)].reshape(2 * half, TILE)
                        for t in tiles
                    ],
                    axis=1,
                )
                rows = pl.ds(pl.multiple_of(start * TILE, TILE), len(tiles) * TILE)
                right = jnp.concatenate([abuf[c, 0, rows, :], abuf[c, 1, rows, :]], axis=1)
                return dot(left, right)

            def listed(first, count):
                return [st[8 + c * ROW_TILES + first + i] for i in range(count)]

            for i in range(ROW_TILES):

                @pl.when(i < n)
                def _():
                    a_copy(c, i).wait()

            @pl.when(n < 4)
            def _():
                acc[...] = jnp.zeros_like(acc)

            @pl.when(n >= 4)
            def _():
                acc[...] = product(listed(0, 4), 0)

            @pl.when(n == 8)
            def _():
                acc[...] += product(listed(4, 4), 4)

            @pl.when((n & 2) != 0)
            def _():
                first = n & 4
                acc[...] += product(listed(first, 2), first)

            @pl.when((n & 1) != 0)
            def _():
                acc[...] += product(listed(n - 1, 1), n - 1)

            out[2, :, lanes] = (acc[:half, :TILE] - acc[half:, TILE:]).astype(jnp.bfloat16)
            out[3, :, lanes] = (acc[:half, TILE:] + acc[half:, :TILE]).astype(jnp.bfloat16)

            @pl.when(st[40 + c] != 0)
            def _():
                d_copy(c).wait()
                acc[...] += product([st[44 + c]], ROW_TILES)

            out[0, :, lanes] = (acc[:half, :TILE] + acc[half:, TILE:]).astype(jnp.bfloat16)
            out[1, :, lanes] = (acc[:half, TILE:] - acc[half:, :TILE]).astype(jnp.bfloat16)
            return carry

        lax.fori_loop(0, COL_TILES, column, 0)


def focus_kernel(st, fb, own, near, after, before, near_after, near_before, far_a, far_b, keep, send, gbuf, acc, gsem):
    core = st[49]
    xh = st[50]
    z = st[51]

    def g_copies():
        copies = []

        def add(ref, x_other, z_step, part):
            block = 2 * ((z + z_step + 4) % 4) + (1 - xh if x_other else xh)
            slot = core if part == 0 else 1 - core
            row = pl.multiple_of(block * 64 + slot * SHARD, SHARD)
            copies.append(
                pltpu.make_async_copy(ref, gbuf.at[:, pl.ds(row, SHARD), :], gsem.at[len(copies)])
            )

        for part in range(2):
            add(own.at[part], False, 0, part)
            add(near.at[part], True, 0, part)
            add(after.at[part], False, -1, part)
            add(before.at[part], False, 1, part)
            add(near_after.at[part], True, -1, part)
            add(near_before.at[part], True, 1, part)
        for x_other in range(2):
            add(far_a.at[x_other], x_other, 2, 0)
            add(far_b.at[x_other], x_other, 2, 1)
        return copies

    sub = lax.broadcasted_iota(jnp.int32, (N_CHIPS, 8, P_SIZE), 1)
    low = sub < 4

    @pl.when(st[48] != 0)
    def _():
        copies = g_copies()
        for copy in copies:
            copy.start()
        for copy in copies:
            copy.wait()
        for c in range(COL_TILES):
            cols = slice(c * TILE, (c + 1) * TILE)
            gr = gbuf[0, :, cols]
            gi = gbuf[1, :, cols]
            fr = fb[0, :, cols]
            fi = fb[1, :, cols]
            left = jnp.concatenate(
                [
                    jnp.concatenate([fr, -fi, gr, gi], axis=1),
                    jnp.concatenate([fi, fr, -gi, gr], axis=1),
                ],
                axis=0,
            )
            right = jnp.concatenate([gr, gi, fb[2, :, cols], fb[3, :, cols]], axis=1)
            if c == 0:
                acc[...] = dot_nt(left, right)
            else:
                acc[...] += dot_nt(left, right)
        re = acc[:P_SIZE].reshape(N_CHIPS, 8, P_SIZE)
        im = acc[P_SIZE:].reshape(N_CHIPS, 8, P_SIZE)
        first = jnp.where(low, re, pltpu.roll(im, 4, 1)).astype(jnp.bfloat16)
        second = jnp.where(low, pltpu.roll(re, 4, 1), im).astype(jnp.bfloat16)

        @pl.when(core == 0)
        def _():
            keep[...] = first
            send[...] = second

        @pl.when(core != 0)
        def _():
            keep[...] = second
            send[...] = first

    @pl.when(st[48] == 0)
    def _():
        keep[...] = jnp.zeros_like(keep)
        send[...] = jnp.zeros_like(send)


def align_kernel(index, parts, out):
    total = jnp.sum(parts[...].astype(jnp.float32), axis=0)
    lane = lax.broadcasted_iota(jnp.int32, (1, P_SIZE), 1)
    for i in range(4):
        re = total[i : i + 1]
        im = total[4 + i : 5 + i]
        chosen = lane == index[i]
        anchor_re = jnp.sum(jnp.where(chosen, re, 0.0), axis=1, keepdims=True)
        anchor_im = jnp.sum(jnp.where(chosen, im, 0.0), axis=1, keepdims=True)
        out[i, 0:1, :] = re * anchor_re + im * anchor_im
        out[i, 1:2, :] = im * anchor_re - re * anchor_im


def any_spec():
    return pl.BlockSpec(memory_space=pl.ANY)


def hbm_spec():
    return pl.BlockSpec(memory_space=pltpu.HBM)


def smem_spec():
    return pl.BlockSpec(memory_space=pltpu.SMEM)


def vmem_spec():
    return pl.BlockSpec(memory_space=pltpu.VMEM)


def tile_states(tile_mask):
    rcv = lax.axis_index(RCV)
    src = lax.axis_index(SRC)
    tiles = lax.dynamic_slice(tile_mask, (rcv * ROW_TILES, src * COL_TILES), (ROW_TILES, COL_TILES))
    kept = (tiles == 1).T
    rows = jnp.arange(ROW_TILES)[None, :]
    diag_row = jnp.arange(COL_TILES)[:, None] + src * COL_TILES - rcv * ROW_TILES
    diag = rows == diag_row
    plain = (kept & ~diag).astype(jnp.int32)
    count = jnp.sum(plain, axis=1)
    before = jnp.sum(plain[:, None, :] * (rows[0][None, :] < rows[0][:, None]), axis=2)
    hit = (before[:, None, :] == rows[0][None, :, None]) & (plain[:, None, :] == 1)
    order = jnp.sum(jnp.where(hit, rows[0][None, None, :], 0), axis=2)
    diag_on = jnp.sum((kept & diag).astype(jnp.int32), axis=1)
    diag_at = jnp.clip(diag_row[:, 0], 0, ROW_TILES - 1)
    scalars = jnp.stack(
        [jnp.max(kept.astype(jnp.int32))] + [lax.axis_index(name) for name in ("core", "xh", "z", "xl", "y")]
    )
    return jnp.concatenate(
        [count, jnp.zeros((4,), jnp.int32), order.reshape(-1), diag_on, diag_at, scalars]
    ).astype(jnp.int32)


def body(reflection, green, tile_mask, reference_index):
    lines = jnp.transpose(green, (0, 2, 1))
    state = tile_states(tile_mask)
    core = lax.axis_index("core")
    mid = ROWS // 2

    beside = lax.ppermute(lines, "xl", SWAP)
    same = lax.dynamic_slice_in_dim(lines, core * mid, mid, 2)
    other = lax.dynamic_slice_in_dim(lines, (1 - core) * mid, mid, 2)
    part_a = lax.ppermute(same, ALL, crossing(0))
    part_b = lax.ppermute(other, ALL, crossing(1))

    g_own = jnp.stack([lines, beside])
    g_after = lax.ppermute(g_own, "y", ring(1))
    g_before = lax.ppermute(g_own, "y", ring(-1))
    own = jnp.stack([part_a, part_b])
    after = lax.ppermute(own, "z", ring(1))
    before = lax.ppermute(own, "z", ring(-1))
    near = lax.ppermute(own, "xh", SWAP)
    g_far_a = lax.ppermute(g_after[..., :mid], "y", ring(1))
    g_far_b = lax.ppermute(g_before[..., mid:], "y", ring(-1))
    swap = lax.ppermute(jnp.stack([g_own, g_after, g_before]), "core", SWAP)
    near_after = lax.ppermute(near, "z", ring(1))
    near_before = lax.ppermute(near, "z", ring(-1))
    swap_far = lax.ppermute(jnp.stack([g_far_a, g_far_b]), "core", SWAP)
    far_a = lax.ppermute(jnp.stack([after[0], near_after[0]]), "z", ring(1))
    far_b = lax.ppermute(jnp.stack([before[1], near_before[1]]), "z", ring(-1))

    fb = pl.pallas_call(
        project_kernel,
        out_shape=jax.ShapeDtypeStruct((4, P_SIZE, COLS), jnp.bfloat16),
        in_specs=[smem_spec()] + [any_spec()] * 7 + [hbm_spec()],
        out_specs=vmem_spec(),
        scratch_shapes=[
            pltpu.VMEM((2, P_SIZE, ROWS), jnp.bfloat16),
            pltpu.VMEM((COL_TILES, 2, ROWS + TILE, TILE), jnp.bfloat16),
            pltpu.VMEM((2 * P_SIZE, 2 * TILE), jnp.float32),
            pltpu.SemaphoreType.DMA((20,)),
            pltpu.SemaphoreType.DMA((COL_TILES, ROW_TILES + 1)),
        ],
        compiler_params=pltpu.CompilerParams(vmem_limit_bytes=44 << 20),
        cost_estimate=pl.CostEstimate(flops=8 << 30, transcendentals=0, bytes_accessed=16 << 20),
        name="project",
    )(state, g_own, g_after, g_before, g_far_a, g_far_b, swap, swap_far, reflection)

    block = jax.ShapeDtypeStruct((N_CHIPS, 8, P_SIZE), jnp.bfloat16)
    keep, send = pl.pallas_call(
        focus_kernel,
        out_shape=(block, block),
        in_specs=[smem_spec(), vmem_spec()] + [any_spec()] * 8,
        out_specs=(vmem_spec(), vmem_spec()),
        scratch_shapes=[
            pltpu.VMEM((2, P_SIZE, COLS), jnp.bfloat16),
            pltpu.VMEM((2 * P_SIZE, P_SIZE), jnp.float32),
            pltpu.SemaphoreType.DMA((16,)),
        ],
        compiler_params=pltpu.CompilerParams(vmem_limit_bytes=44 << 20),
        cost_estimate=pl.CostEstimate(flops=4 << 30, transcendentals=0, bytes_accessed=8 << 20),
        name="focus",
    )(state, fb, own, near, after, before, near_after, near_before, far_a, far_b)
    taken = lax.ppermute(send, "core", SWAP)
    summed = (keep.astype(jnp.float32) + taken.astype(jnp.float32)).astype(jnp.bfloat16)
    parts = lax.all_to_all(summed, CHIPS, 0, 0)
    return pl.pallas_call(
        align_kernel,
        out_shape=jax.ShapeDtypeStruct((4, 2, P_SIZE), jnp.float32),
        in_specs=[smem_spec(), vmem_spec()],
        out_specs=vmem_spec(),
        name="align",
    )(reference_index, parts)


def solution(mesh):
    fine = Mesh(mesh.devices.reshape([size for _, size in PARTS]), [name for name, _ in PARTS])
    return jax.shard_map(
        body,
        mesh=fine,
        in_specs=(P(None, RCV, SRC), P(None, RCV, SRC), P(), P(ALL)),
        out_specs=P(ALL, None, None),
        check_vma=False,
    )
```

time: 117 us -> 116 us (level)
  starting transfers between devices: 29.8 us -> 45.5 us
  between operations: 13.5 us -> 0.15 us
  other arithmetic: 1.79 us -> 5.17 us
  local copies, waits for them, and re-layouts: 4.13 us -> 1.12 us
  Pallas kernels: 19 us -> 16.2 us
  waiting for transfers between devices: 24.5 us -> 26.9 us
  blocking collectives: 23.6 us -> 21.5 us
    ppermute x6 -> x15, waiting for transfers between devices: 10.3 us -> 25.4 us  [the longest x1 11 us: body(): g_after = lax.ppermute(g_own, 'y', ring(1))]
    ppermute x6 -> x15, starting transfers between devices: 15 us -> 30 us  [the longest x1 6.98 us: body(): before = lax.ppermute(own, 'z', ring(-1))]
    ppermute x1, waiting for transfers between devices: 12 us -> 0.01 us  [body(): near = lax.ppermute(own, 'xh', SWAP)]
    another operation x2 -> x6, other arithmetic: 0.09 us -> 3.25 us  [the longest x2 2.34 us: body(): swap = lax.ppermute(jnp.stack([g_own, g_after, g_before]), 'core', SWAP)]
    unnamed x2, local copies, waits for them, and re-layouts: 2.18 us -> 0.01 us
    all_to_all x1, blocking collectives: 23.6 us -> 21.5 us  [body(): parts = lax.all_to_all(summed, CHIPS, 0, 0)]
    ppermute x1, starting transfers between devices: 1.28 us -> 3.35 us  [body(): taken = lax.ppermute(send, 'core', SWAP)]
    pallas_call x1, Pallas kernels: 9.08 us -> 7.11 us  [body(): pl.pallas_call(project_kernel, out_shape=jax.ShapeDtypeStruct((4, P_SIZE,...]
  transfers between devices with their start and end apart: 9 -> 17, of which waited for: 5 -> 7; matrix products, arithmetic and copies ran while one was open for 3% -> 3% of each run, Pallas kernels for 8% -> 6%
where the time goes in v2:
time: 116 us
  starting transfers between devices  45.5 us (39%)
  waiting for transfers between devices  26.9 us (23%)
  blocking collectives  21.5 us (19%)
  Pallas kernels  16.2 us (14%)
  other arithmetic  5.17 us (4%)
    all_to_all x1, blocking collectives, body(): parts = lax.all_to_all(summed, CHIPS, 0, 0)  21.5 us
    ppermute x1, starting transfers between devices, body(): near = lax.ppermute(own, 'xh', SWAP)  12.1 us
    ppermute x1, waiting for transfers between devices, body(): g_after = lax.ppermute(g_own, 'y', ring(1))  11 us
    pallas_call x1, Pallas kernels, body(): pl.pallas_call(focus_kernel, out_shape=(block, block), in_specs=[smem_spe...  7.22 us
    pallas_call x1, Pallas kernels, body(): pl.pallas_call(project_kernel, out_shape=jax.ShapeDtypeStruct((4, P_SIZE,...  7.11 us
    ppermute x1, starting transfers between devices, body(): before = lax.ppermute(own, 'z', ring(-1))  6.98 us
    ppermute x1, starting transfers between devices, body(): g_far_b = lax.ppermute(g_before[..., mid:], 'y', ring(-1))  6.82 us
    ppermute x1, waiting for transfers between devices, body(): beside = lax.ppermute(lines, 'xl', SWAP)  6.51 us
  transfers between devices with their start and end apart: 17, of which 7 were waited for; matrix products, arithmetic and copies ran while one was open for 3% of the time, Pallas kernels for 6%

profile of v2, /device:TPU:0, one launch (start us, length us, event | category | flops | bytes accessed | tf_op | source)
XLA Modules:
  0.0 116.5 jit_solution(8482642500169697750)
XLA Ops:
  0.0 1.6 %collective-permute-start = (bf16[2,32,2048]{2,1,0:T(8,128)(2,1)}, bf16[2,32,2048]{2,1,0:T(8,128)(2,1)S(1)}, u32[]{:S(2)}, u32[]{:S(2)}) collective-permute-start(bf16[2,32,2048]{2,1,0:T(8,128)(2,1)} %bitcast.29), channel_id=1, source_target_pairs={{0,2},{2,0},{1,3},{3,1},{4,6},{6,4},{5,7},{7,5},{8,10},{10,8},{9,1... | collective-permute-start | bytes 786440 | tf_op jit(solution)/shard_map/ppermute | solution.py:315
  1.6 6.5 %collective-permute-done = bf16[2,32,2048]{2,1,0:T(8,128)(2,1)S(1)} collective-permute-done((bf16[2,32,2048]{2,1,0:T(8,128)(2,1)}, bf16[2,32,2048]{2,1,0:T(8,128)(2,1)S(1)}, u32[]{:S(2)}, u32[]{:S(2)}) %collective-permute-start) | collective-permute-done | bytes 262176 | tf_op jit(solution)/shard_map/ppermute | solution.py:315
  8.1 1.0 fusion.8
  9.1 1.9 %collective-permute-start.1 = (bf16[2,2,32,2048]{3,2,1,0:T(8,128)(2,1)S(1)}, bf16[2,2,32,2048]{3,2,1,0:T(8,128)(2,1)S(1)}, u32[]{:S(2)}, u32[]{:S(2)}) collective-permute-start(bf16[2,2,32,2048]{3,2,1,0:T(8,128)(2,1)S(1)} %get-tuple-element.17.own), channel_id=1, source_target_pairs={{0,4},{4,8},{8,12},{12,0},{1,5},{5,9},{9,13},{13,1},{2,6},{6,10},{... | collective-permute-start | bytes 1572872 | tf_op jit(solution)/shard_map/ppermute | solution.py:322
  11.0 1.5 %collective-permute-start.2 = (bf16[2,2,32,2048]{3,2,1,0:T(8,128)(2,1)S(1)}, bf16[2,2,32,2048]{3,2,1,0:T(8,128)(2,1)S(1)}, u32[]{:S(2)}, u32[]{:S(2)}) collective-permute-start(bf16[2,2,32,2048]{3,2,1,0:T(8,128)(2,1)S(1)} %get-tuple-element.17.own), channel_id=1, source_target_pairs={{0,12},{4,0},{8,4},{12,8},{1,13},{5,1},{9,5},{13,9},{2,14},{6,2},{... | collective-permute-start | bytes 1572872 | tf_op jit(solution)/shard_map/ppermute | solution.py:323
  12.5 11.0 %collective-permute-done.1.after = bf16[2,2,32,2048]{3,2,1,0:T(8,128)(2,1)S(1)} collective-permute-done((bf16[2,2,32,2048]{3,2,1,0:T(8,128)(2,1)S(1)}, bf16[2,2,32,2048]{3,2,1,0:T(8,128)(2,1)S(1)}, u32[]{:S(2)}, u32[]{:S(2)}) %collective-permute-start.1) | collective-permute-done | bytes 524320 | tf_op jit(solution)/shard_map/ppermute | solution.py:322
  23.5 1.3 %pad_maximum_fusion = bf16[3,2,2,32,2048]{4,3,2,1,0:T(8,128)(2,1)} fusion(bf16[1,2,2,32,2048]{4,3,2,1,0:T(8,128)(2,1)S(1)} %bitcast.26, bf16[1,2,2,32,2048]{4,3,2,1,0:T(8,128)(2,1)S(1)} %bitcast.25, bf16[1,2,2,32,2048]{4,3,2,1,0:T(8,128)(2,1)S(1)} %get-tuple-element.16), kind=kLoop, calls=%fused_computation | loop fusion | flops 1572864 | bytes 3145728 | tf_op jit(solution)/shard_map/stack | solution.py:330
  26.9 1.5 %collective-permute-done.8 = bf16[2,32,1024]{2,1,0:T(8,128)(2,1)S(1)} collective-permute-done((bf16[2,32,1024]{2,1,0:T(8,128)(2,1)S(1)}, bf16[2,32,1024]{2,1,0:T(8,128)(2,1)S(1)}, u32[]{:S(2)}, u32[]{:S(2)}) %collective-permute-start.8) | collective-permute-done | bytes 131104 | tf_op jit(solution)/shard_map/ppermute | solution.py:319
  28.5 12.1 %collective-permute-start.9 = (bf16[2,2,32,1024]{3,2,1,0:T(8,128)(2,1)S(1)}, bf16[2,2,32,1024]{3,2,1,0:T(8,128)(2,1)}, u32[]{:S(2)}, u32[]{:S(2)}) collective-permute-start(bf16[2,2,32,1024]{3,2,1,0:T(8,128)(2,1)S(1)} %pad_maximum_fusion.3.own), channel_id=1, source_target_pairs={{0,64},{64,0},{1,65},{65,1},{2,66},{66,2},{3,67},{67,3},{4,68},{68... | collective-permute-start | bytes 786440 | tf_op jit(solution)/shard_map/ppermute | solution.py:327
  40.6 4.3 %collective-permute-start.3 = (bf16[2,2,32,1024]{3,2,1,0:T(8,128)(2,1)S(1)}, bf16[2,2,32,1024]{3,2,1,0:T(8,128)(2,1)S(1)}, u32[]{:S(2)}, u32[]{:S(2)}) collective-permute-start(bf16[2,2,32,1024]{3,2,1,0:T(8,128)(2,1)S(1)} %slice.24), channel_id=1, source_target_pairs={{0,4},{4,8},{8,12},{12,0},{1,5},{5,9},{9,13},{13,1},{2,6},{6,10},{... | collective-permute-start | bytes 786440 | tf_op jit(solution)/shard_map/ppermute | solution.py:328
  45.0 6.8 %collective-permute-start.4 = (bf16[2,2,32,1024]{3,2,1,0:T(8,128)(2,1)S(1)}, bf16[2,2,32,1024]{3,2,1,0:T(8,128)(2,1)S(1)}, u32[]{:S(2)}, u32[]{:S(2)}) collective-permute-start(bf16[2,2,32,1024]{3,2,1,0:T(8,128)(2,1)S(1)} %slice.25), channel_id=1, source_target_pairs={{0,12},{4,0},{8,4},{12,8},{1,13},{5,1},{9,5},{13,9},{2,14},{6,2},{... | collective-permute-start | bytes 786440 | tf_op jit(solution)/shard_map/ppermute | solution.py:329
  51.9 7.0 %collective-permute-start.11 = (bf16[2,2,32,1024]{3,2,1,0:T(8,128)(2,1)S(1)}, bf16[2,2,32,1024]{3,2,1,0:T(8,128)(2,1)S(1)}, u32[]{:S(2)}, u32[]{:S(2)}) collective-permute-start(bf16[2,2,32,1024]{3,2,1,0:T(8,128)(2,1)S(1)} %pad_maximum_fusion.3.own), channel_id=1, source_target_pairs={{0,48},{16,0},{32,16},{48,32},{1,49},{17,1},{33,17},{49,33},{2,50}... | collective-permute-start | bytes 786440 | tf_op jit(solution)/shard_map/ppermute | solution.py:326
  58.9 0.8 pad_maximum_fusion.2
  60.0 1.4 %collective-permute-done.10.after = bf16[2,2,32,1024]{3,2,1,0:T(8,128)(2,1)S(1)} collective-permute-done((bf16[2,2,32,1024]{3,2,1,0:T(8,128)(2,1)S(1)}, bf16[2,2,32,1024]{3,2,1,0:T(8,128)(2,1)S(1)}, u32[]{:S(2)}, u32[]{:S(2)}) %collective-permute-start.10) | collective-permute-done | bytes 262176 | tf_op jit(solution)/shard_map/ppermute | solution.py:325
  61.4 1.9 %collective-permute-start.13 = (bf16[2,2,32,1024]{3,2,1,0:T(8,128)(2,1)}, bf16[2,2,32,1024]{3,2,1,0:T(8,128)(2,1)S(1)}, u32[]{:S(2)}, u32[]{:S(2)}) collective-permute-start(bf16[2,2,32,1024]{3,2,1,0:T(8,128)(2,1)} %collective-permute-done.9.near), channel_id=1, source_target_pairs={{0,48},{16,0},{32,16},{48,32},{1,49},{17,1},{33,17},{49,33},{2,50}... | collective-permute-start | bytes 786440 | tf_op jit(solution)/shard_map/ppermute | solution.py:332
  65.0 3.0 %collective-permute-done.12.near_after = bf16[2,2,32,1024]{3,2,1,0:T(8,128)(2,1)S(1)} collective-permute-done((bf16[2,2,32,1024]{3,2,1,0:T(8,128)(2,1)}, bf16[2,2,32,1024]{3,2,1,0:T(8,128)(2,1)S(1)}, u32[]{:S(2)}, u32[]{:S(2)}) %collective-permute-start.12) | collective-permute-done | bytes 262176 | tf_op jit(solution)/shard_map/ppermute | solution.py:331
  68.1 2.0 %collective-permute-done.13.near_before = bf16[2,2,32,1024]{3,2,1,0:T(8,128)(2,1)S(1)} collective-permute-done((bf16[2,2,32,1024]{3,2,1,0:T(8,128)(2,1)}, bf16[2,2,32,1024]{3,2,1,0:T(8,128)(2,1)S(1)}, u32[]{:S(2)}, u32[]{:S(2)}) %collective-permute-start.13) | collective-permute-done | bytes 262176 | tf_op jit(solution)/shard_map/ppermute | solution.py:332
  70.1 3.7 %collective-permute-start.15 = (bf16[2,2,32,1024]{3,2,1,0:T(8,128)(2,1)S(1)}, bf16[2,2,32,1024]{3,2,1,0:T(8,128)(2,1)S(1)}, u32[]{:S(2)}, u32[]{:S(2)}) collective-permute-start(bf16[2,2,32,1024]{3,2,1,0:T(8,128)(2,1)S(1)} %pad_maximum_fusion.5), channel_id=1, source_target_pairs={{0,48},{16,0},{32,16},{48,32},{1,49},{17,1},{33,17},{49,33},{2,50}... | collective-permute-start | bytes 786440 | tf_op jit(solution)/shard_map/ppermute | solution.py:335
  73.8 7.1 %project.1.fb = bf16[4,512,1024]{2,1,0:T(8,128)(2,1)S(1)} custom-call(s32[54]{0:T(128)S(1)} %concatenate.3.st, bf16[2,2,32,2048]{3,2,1,0:T(8,128)(2,1)S(1)} %get-tuple-element.17.own, bf16[2,2,32,2048]{3,2,1,0:T(8,128)(2,1)S(1)} %collective-permute-done.1.after, bf16[2,2,32,2048]{3,2,1,0:T(8,128)(2,1)S(1)} %collective-permute-done.2.before, ...), custom_call_target="tpu_custom_call" | custom-call | flops 8589934592 | bytes 16777216 | tf_op jit(solution)/shard_map/project/pallas_call | solution.py:337
  80.9 7.2 %focus.1 = (bf16[64,8,512]{2,1,0:T(8,128)(2,1)S(1)}, bf16[64,8,512]{2,1,0:T(8,128)(2,1)S(1)}) custom-call(s32[54]{0:T(128)S(1)} %concatenate.3.st, bf16[4,512,1024]{2,1,0:T(8,128)(2,1)S(1)} %project.1.fb, bf16[2,2,32,1024]{3,2,1,0:T(8,128)(2,1)S(1)} %pad_maximum_fusion.3.own, bf16[2,2,32,1024]{3,2,1,0:T(8,128)(2,1)} %collective-permute-done.9.near, ...), custom_call_target="tpu_custom_call" | custom-call | flops 4294967296 | bytes 8388608 | tf_op jit(solution)/shard_map/focus/pallas_call | solution.py:355
  88.1 3.4 %collective-permute-start.16 = (bf16[64,8,512]{2,1,0:T(8,128)(2,1)S(1)}, bf16[64,8,512]{2,1,0:T(8,128)(2,1)S(1)}, u32[]{:S(2)}, u32[]{:S(2)}) collective-permute-start(bf16[64,8,512]{2,1,0:T(8,128)(2,1)S(1)} %get-tuple-element.8), channel_id=1, source_target_pairs={{0,1},{1,0},{2,3},{3,2},{4,5},{5,4},{6,7},{7,6},{8,9},{9,8},{10,11... | collective-permute-start | bytes 1572872 | tf_op jit(solution)/shard_map/ppermute | solution.py:369
  91.5 1.5 %collective-permute-done.16 = bf16[64,8,512]{2,1,0:T(8,128)(2,1)S(1)} collective-permute-done((bf16[64,8,512]{2,1,0:T(8,128)(2,1)S(1)}, bf16[64,8,512]{2,1,0:T(8,128)(2,1)S(1)}, u32[]{:S(2)}, u32[]{:S(2)}) %collective-permute-start.16) | collective-permute-done | bytes 524320 | tf_op jit(solution)/shard_map/ppermute | solution.py:369
  93.2 21.5 %all_to_all.5.parts = bf16[64,8,512]{2,1,0:T(8,128)(2,1)} all-to-all(bf16[64,8,512]{2,1,0:T(8,128)(2,1)S(1)} %add_convert_fusion), channel_id=1, replica_groups=mesh['xh'=2,'z'=4,'y'=4,'xl'=2,'core'=2] {'xh','z','y','xl'}, dimensions={0} | all-to-all | bytes 1048576 | tf_op jit(solution)/shard_map/all_to_all | solution.py:371
  114.6 1.8 %align.1 = f32[4,2,512]{2,1,0:T(2,128)} custom-call(s32[4]{0:T(128)} %index.1, bf16[64,8,512]{2,1,0:T(8,128)(2,1)} %all_to_all.5.parts), custom_call_target="tpu_custom_call" | custom-call | tf_op jit(solution)/shard_map/align/pallas_call | solution.py:372
  (42 shorter events, 4.5 us)
Async XLA Ops:
  0.0 8.1 %collective-permute-start = (bf16[2,32,2048]{2,1,0:T(8,128)(2,1)}, bf16[2,32,2048]{2,1,0:T(8,128)(2,1)S(1)}, u32[]{:S(2)}, u32[]{:S(2)}) collective-permute-start(bf16[2,32,2048]{2,1,0:T(8,128)(2,1)} %bitcast.29), channel_id=1, source_target_pairs={{0,2},{2,0},{1,3},{3,1},{4,6},{6,4},{5,7},{7,5},{8,10},{10,8},{9,1... | collective-permute-start | bytes 786440 | tf_op jit(solution)/shard_map/ppermute | solution.py:315
  9.1 14.4 %collective-permute-start.1 = (bf16[2,2,32,2048]{3,2,1,0:T(8,128)(2,1)S(1)}, bf16[2,2,32,2048]{3,2,1,0:T(8,128)(2,1)S(1)}, u32[]{:S(2)}, u32[]{:S(2)}) collective-permute-start(bf16[2,2,32,2048]{3,2,1,0:T(8,128)(2,1)S(1)} %get-tuple-element.17.own), channel_id=1, source_target_pairs={{0,4},{4,8},{8,12},{12,0},{1,5},{5,9},{9,13},{13,1},{2,6},{6,10},{... | collective-permute-start | bytes 1572872 | tf_op jit(solution)/shard_map/ppermute | solution.py:322
  11.0 12.5 %collective-permute-start.2 = (bf16[2,2,32,2048]{3,2,1,0:T(8,128)(2,1)S(1)}, bf16[2,2,32,2048]{3,2,1,0:T(8,128)(2,1)S(1)}, u32[]{:S(2)}, u32[]{:S(2)}) collective-permute-start(bf16[2,2,32,2048]{3,2,1,0:T(8,128)(2,1)S(1)} %get-tuple-element.17.own), channel_id=1, source_target_pairs={{0,12},{4,0},{8,4},{12,8},{1,13},{5,1},{9,5},{13,9},{2,14},{6,2},{... | collective-permute-start | bytes 1572872 | tf_op jit(solution)/shard_map/ppermute | solution.py:323
  23.5 1.3 %copy-start = (bf16[2,2048,32]{1,2,0:T(8,128)(2,1)S(1)}, bf16[2,2048,32]{1,2,0:T(8,128)(2,1)}, u32[]{:S(2)}) copy-start(bf16[2,2048,32]{1,2,0:T(8,128)(2,1)} %param.5) | copy-start | bytes 786436
  24.8 48.9 %collective-permute-start.5 = (bf16[3,2,2,32,2048]{4,3,2,1,0:T(8,128)(2,1)}, bf16[3,2,2,32,2048]{4,3,2,1,0:T(8,128)(2,1)}, u32[]{:S(2)}, u32[]{:S(2)}) collective-permute-start(bf16[3,2,2,32,2048]{4,3,2,1,0:T(8,128)(2,1)} %pad_maximum_fusion), channel_id=1, source_target_pairs={{0,1},{1,0},{2,3},{3,2},{4,5},{5,4},{6,7},{7,6},{8,9},{9,8},{10,11... | collective-permute-start | bytes 4718600 | tf_op jit(solution)/shard_map/ppermute | solution.py:330
  24.9 2.0 %collective-permute-start.7 = (bf16[2,32,1024]{2,1,0:T(8,128)(2,1)S(1)}, bf16[2,32,1024]{2,1,0:T(8,128)(2,1)S(1)}, u32[]{:S(2)}, u32[]{:S(2)}) collective-permute-start(bf16[2,32,1024]{2,1,0:T(8,128)(2,1)S(1)} %get-tuple-element.18), channel_id=1, source_target_pairs={{0,0},{1,1},{2,64},{3,65},{4,16},{5,17},{6,80},{7,81},{8,32},{9,33... | collective-permute-start | bytes 393224 | tf_op jit(solution)/shard_map/ppermute | solution.py:318
  25.5 2.9 %collective-permute-start.8 = (bf16[2,32,1024]{2,1,0:T(8,128)(2,1)S(1)}, bf16[2,32,1024]{2,1,0:T(8,128)(2,1)S(1)}, u32[]{:S(2)}, u32[]{:S(2)}) collective-permute-start(bf16[2,32,1024]{2,1,0:T(8,128)(2,1)S(1)} %get-tuple-element.19), channel_id=1, source_target_pairs={{0,1},{1,0},{2,65},{3,64},{4,17},{5,16},{6,81},{7,80},{8,33},{9,32... | collective-permute-start | bytes 393224 | tf_op jit(solution)/shard_map/ppermute | solution.py:319
  28.5 23.4 %collective-permute-start.9 = (bf16[2,2,32,1024]{3,2,1,0:T(8,128)(2,1)S(1)}, bf16[2,2,32,1024]{3,2,1,0:T(8,128)(2,1)}, u32[]{:S(2)}, u32[]{:S(2)}) collective-permute-start(bf16[2,2,32,1024]{3,2,1,0:T(8,128)(2,1)S(1)} %pad_maximum_fusion.3.own), channel_id=1, source_target_pairs={{0,64},{64,0},{1,65},{65,1},{2,66},{66,2},{3,67},{67,3},{4,68},{68... | collective-permute-start | bytes 786440 | tf_op jit(solution)/shard_map/ppermute | solution.py:327
  40.6 18.3 %collective-permute-start.3 = (bf16[2,2,32,1024]{3,2,1,0:T(8,128)(2,1)S(1)}, bf16[2,2,32,1024]{3,2,1,0:T(8,128)(2,1)S(1)}, u32[]{:S(2)}, u32[]{:S(2)}) collective-permute-start(bf16[2,2,32,1024]{3,2,1,0:T(8,128)(2,1)S(1)} %slice.24), channel_id=1, source_target_pairs={{0,4},{4,8},{8,12},{12,0},{1,5},{5,9},{9,13},{13,1},{2,6},{6,10},{... | collective-permute-start | bytes 786440 | tf_op jit(solution)/shard_map/ppermute | solution.py:328
  45.0 13.9 %collective-permute-start.4 = (bf16[2,2,32,1024]{3,2,1,0:T(8,128)(2,1)S(1)}, bf16[2,2,32,1024]{3,2,1,0:T(8,128)(2,1)S(1)}, u32[]{:S(2)}, u32[]{:S(2)}) collective-permute-start(bf16[2,2,32,1024]{3,2,1,0:T(8,128)(2,1)S(1)} %slice.25), channel_id=1, source_target_pairs={{0,12},{4,0},{8,4},{12,8},{1,13},{5,1},{9,5},{13,9},{2,14},{6,2},{... | collective-permute-start | bytes 786440 | tf_op jit(solution)/shard_map/ppermute | solution.py:329
  51.8 9.6 %collective-permute-start.10 = (bf16[2,2,32,1024]{3,2,1,0:T(8,128)(2,1)S(1)}, bf16[2,2,32,1024]{3,2,1,0:T(8,128)(2,1)S(1)}, u32[]{:S(2)}, u32[]{:S(2)}) collective-permute-start(bf16[2,2,32,1024]{3,2,1,0:T(8,128)(2,1)S(1)} %pad_maximum_fusion.3.own), channel_id=1, source_target_pairs={{0,16},{16,32},{32,48},{48,0},{1,17},{17,33},{33,49},{49,1},{2,18}... | collective-permute-start | bytes 786440 | tf_op jit(solution)/shard_map/ppermute | solution.py:325
  51.9 13.1 %collective-permute-start.11 = (bf16[2,2,32,1024]{3,2,1,0:T(8,128)(2,1)S(1)}, bf16[2,2,32,1024]{3,2,1,0:T(8,128)(2,1)S(1)}, u32[]{:S(2)}, u32[]{:S(2)}) collective-permute-start(bf16[2,2,32,1024]{3,2,1,0:T(8,128)(2,1)S(1)} %pad_maximum_fusion.3.own), channel_id=1, source_target_pairs={{0,48},{16,0},{32,16},{48,32},{1,49},{17,1},{33,17},{49,33},{2,50}... | collective-permute-start | bytes 786440 | tf_op jit(solution)/shard_map/ppermute | solution.py:326
  58.9 9.1 %collective-permute-start.12 = (bf16[2,2,32,1024]{3,2,1,0:T(8,128)(2,1)}, bf16[2,2,32,1024]{3,2,1,0:T(8,128)(2,1)S(1)}, u32[]{:S(2)}, u32[]{:S(2)}) collective-permute-start(bf16[2,2,32,1024]{3,2,1,0:T(8,128)(2,1)} %collective-permute-done.9.near), channel_id=1, source_target_pairs={{0,16},{16,32},{32,48},{48,0},{1,17},{17,33},{33,49},{49,1},{2,18}... | collective-permute-start | bytes 786440 | tf_op jit(solution)/shard_map/ppermute | solution.py:331
  59.7 14.0 %collective-permute-start.6 = (bf16[2,2,2,32,1024]{4,3,2,1,0:T(8,128)(2,1)}, bf16[2,2,2,32,1024]{4,3,2,1,0:T(8,128)(2,1)}, u32[]{:S(2)}, u32[]{:S(2)}) collective-permute-start(bf16[2,2,2,32,1024]{4,3,2,1,0:T(8,128)(2,1)} %pad_maximum_fusion.2), channel_id=1, source_target_pairs={{0,1},{1,0},{2,3},{3,2},{4,5},{5,4},{6,7},{7,6},{8,9},{9,8},{10,11... | collective-permute-start | bytes 1572872 | tf_op jit(solution)/shard_map/ppermute | solution.py:333
  61.4 8.7 %collective-permute-start.13 = (bf16[2,2,32,1024]{3,2,1,0:T(8,128)(2,1)}, bf16[2,2,32,1024]{3,2,1,0:T(8,128)(2,1)S(1)}, u32[]{:S(2)}, u32[]{:S(2)}) collective-permute-start(bf16[2,2,32,1024]{3,2,1,0:T(8,128)(2,1)} %collective-permute-done.9.near), channel_id=1, source_target_pairs={{0,48},{16,0},{32,16},{48,32},{1,49},{17,1},{33,17},{49,33},{2,50}... | collective-permute-start | bytes 786440 | tf_op jit(solution)/shard_map/ppermute | solution.py:332
  68.0 12.9 %collective-permute-start.14 = (bf16[2,2,32,1024]{3,2,1,0:T(8,128)(2,1)S(1)}, bf16[2,2,32,1024]{3,2,1,0:T(8,128)(2,1)S(1)}, u32[]{:S(2)}, u32[]{:S(2)}) collective-permute-start(bf16[2,2,32,1024]{3,2,1,0:T(8,128)(2,1)S(1)} %pad_maximum_fusion.4), channel_id=1, source_target_pairs={{0,16},{16,32},{32,48},{48,0},{1,17},{17,33},{33,49},{49,1},{2,18}... | collective-permute-start | bytes 786440 | tf_op jit(solution)/shard_map/ppermute | solution.py:334
  70.1 10.8 %collective-permute-start.15 = (bf16[2,2,32,1024]{3,2,1,0:T(8,128)(2,1)S(1)}, bf16[2,2,32,1024]{3,2,1,0:T(8,128)(2,1)S(1)}, u32[]{:S(2)}, u32[]{:S(2)}) collective-permute-start(bf16[2,2,32,1024]{3,2,1,0:T(8,128)(2,1)S(1)} %pad_maximum_fusion.5), channel_id=1, source_target_pairs={{0,48},{16,0},{32,16},{48,32},{1,49},{17,1},{33,17},{49,33},{2,50}... | collective-permute-start | bytes 786440 | tf_op jit(solution)/shard_map/ppermute | solution.py:335
  88.1 4.9 %collective-permute-start.16 = (bf16[64,8,512]{2,1,0:T(8,128)(2,1)S(1)}, bf16[64,8,512]{2,1,0:T(8,128)(2,1)S(1)}, u32[]{:S(2)}, u32[]{:S(2)}) collective-permute-start(bf16[64,8,512]{2,1,0:T(8,128)(2,1)S(1)} %get-tuple-element.8), channel_id=1, source_target_pairs={{0,1},{1,0},{2,3},{3,2},{4,5},{5,4},{6,7},{7,6},{8,9},{9,8},{10,11... | collective-permute-start | bytes 1572872 | tf_op jit(solution)/shard_map/ppermute | solution.py:369

commit v3 on v2

v3 whole, which is shorter than its diff:
```python
import jax
import jax.numpy as jnp
from jax import lax
from jax.experimental import pallas as pl
from jax.experimental.pallas import tpu as pltpu
from jax.sharding import Mesh, PartitionSpec as P

P_SIZE = 512
TILE = 256
PARTS = (("xh", 2), ("z", 4), ("y", 4), ("xl", 2), ("core", 2))
RCV = ("xh", "z")
SRC = ("y", "xl", "core")
ALL = RCV + SRC
CHIPS = RCV + SRC[:2]
ROWS = 2048
COLS = 1024
ROW_TILES = ROWS // TILE
COL_TILES = COLS // TILE
SHARD = 32
N_CHIPS = 64
SWAP = [(0, 1), (1, 0)]


def place(xh, z, y, xl, core):
    return (((xh * 4 + z) * 4 + y) * 2 + xl) * 2 + core


def crossing(cross):
    return [
        (place(xh, z, y, xl, core), place(xl, y, 2 * xh + z // 2, z % 2, core ^ cross))
        for xh in range(2)
        for z in range(4)
        for y in range(4)
        for xl in range(2)
        for core in range(2)
    ]


def ring(step):
    return [(i, (i + step) % 4) for i in range(4)]


def dot(a, b):
    return lax.dot_general(a, b, (((1,), (0,)), ((), ())), preferred_element_type=jnp.float32)


def dot_nt(a, b):
    return lax.dot_general(a, b, (((1,), (1,)), ((), ())), preferred_element_type=jnp.float32)


def load_kernel(st, a, abuf, asem):
    def tile_copy(c, source, i):
        row = pl.multiple_of(source * TILE, TILE)
        return pltpu.make_async_copy(
            a.at[:, pl.ds(row, TILE), pl.ds(c * TILE, TILE)],
            abuf.at[c, :, pl.ds(i * TILE, TILE), :],
            asem.at[c, i],
        )

    def visit(act):
        for c in range(COL_TILES):
            for i in range(ROW_TILES):

                @pl.when(i < st[c])
                def _():
                    act(tile_copy(c, st[8 + c * ROW_TILES + i], i))

            @pl.when(st[40 + c] != 0)
            def _():
                act(tile_copy(c, st[44 + c], ROW_TILES))

    visit(lambda copy: copy.start())
    visit(lambda copy: copy.wait())


def project(st, abuf, acc, fb, left_of, targets):
    def column(c, carry):
        n = st[c]
        lanes = pl.ds(pl.multiple_of(c * TILE, TILE), TILE)

        def product(tiles, start):
            left = jnp.concatenate([left_of(t) for t in tiles], axis=1)
            rows = pl.ds(pl.multiple_of(start * TILE, TILE), len(tiles) * TILE)
            right = jnp.concatenate([abuf[c, 0, rows, :], abuf[c, 1, rows, :]], axis=1)
            return dot(left, right)

        def listed(first, count):
            return [st[8 + c * ROW_TILES + first + i] for i in range(count)]

        @pl.when(n < 4)
        def _():
            acc[...] = jnp.zeros_like(acc)

        @pl.when(n >= 4)
        def _():
            acc[...] = product(listed(0, 4), 0)

        @pl.when(n == 8)
        def _():
            acc[...] += product(listed(4, 4), 4)

        @pl.when((n & 2) != 0)
        def _():
            first = n & 4
            acc[...] += product(listed(first, 2), first)

        @pl.when((n & 1) != 0)
        def _():
            acc[...] += product(listed(n - 1, 1), n - 1)

        def store(front, back):
            for b, row in enumerate(targets):
                rows = pl.ds(pl.multiple_of(row, SHARD), SHARD)
                at = 2 * SHARD * b
                rr = acc[at : at + SHARD, :TILE]
                ri = acc[at : at + SHARD, TILE:]
                ir = acc[at + SHARD : at + 2 * SHARD, :TILE]
                ii = acc[at + SHARD : at + 2 * SHARD, TILE:]
                if front:
                    fb[0, rows, lanes] = (rr + ii).astype(jnp.bfloat16)
                    fb[1, rows, lanes] = (ri - ir).astype(jnp.bfloat16)
                if back:
                    fb[2, rows, lanes] = (rr - ii).astype(jnp.bfloat16)
                    fb[3, rows, lanes] = (ri + ir).astype(jnp.bfloat16)

        @pl.when(st[40 + c] == 0)
        def _():
            store(True, True)

        @pl.when(st[40 + c] != 0)
        def _():
            store(False, True)
            acc[...] += product([st[44 + c]], ROW_TILES)
            store(True, False)

        return carry

    lax.fori_loop(0, COL_TILES, column, 0)


def line_row(st, x_other, y_step, other):
    core, xl, y = st[49], st[52], st[53]
    line = 4 * ((y + y_step + 4) % 4) + 2 * (1 - xl if x_other else xl)
    return (line + (1 - core if other else core)) * SHARD


def tile_lanes(t):
    return pl.ds(pl.multiple_of(t * TILE, TILE), TILE)


def near_kernel(st, abuf, own, after, before, fb, acc):
    @pl.when(st[48] != 0)
    def _():
        def left_of(t):
            return jnp.concatenate(
                [ref[:, :, :, tile_lanes(t)].reshape(4 * SHARD, TILE) for ref in (own, after, before)], axis=0
            )

        targets = [line_row(st, x, step, False) for step in (0, -1, 1) for x in range(2)]
        project(st, abuf, acc, fb, left_of, targets)


def swap_kernel(st, abuf, fb_in, swap, fb, acc):
    @pl.when(st[48] != 0)
    def _():
        def left_of(t):
            return swap[:, :, :, :, tile_lanes(t)].reshape(12 * SHARD, TILE)

        targets = [line_row(st, x, step, True) for step in (0, -1, 1) for x in range(2)]
        project(st, abuf, acc, fb, left_of, targets)


def finish_kernel(
    st, abuf, fb_in, g_far_a, g_far_b, swap_far,
    own, near, after, before, near_after, near_before, far_a, far_b,
    fb, keep, send, gbuf, acc, wide, gsem,
):
    core = st[49]
    xh = st[50]
    z = st[51]

    def g_copies():
        copies = []

        def add(ref, x_other, z_step, part):
            block = 2 * ((z + z_step + 4) % 4) + (1 - xh if x_other else xh)
            slot = core if part == 0 else 1 - core
            row = pl.multiple_of(block * 64 + slot * SHARD, SHARD)
            copies.append(
                pltpu.make_async_copy(ref, gbuf.at[:, pl.ds(row, SHARD), :], gsem.at[len(copies)])
            )

        for part in range(2):
            add(own.at[part], False, 0, part)
            add(near.at[part], True, 0, part)
            add(after.at[part], False, -1, part)
            add(before.at[part], False, 1, part)
            add(near_after.at[part], True, -1, part)
            add(near_before.at[part], True, 1, part)
            add(far_a.at[part], False, 2, part)
            add(far_b.at[part], True, 2, part)
        return copies

    sub = lax.broadcasted_iota(jnp.int32, (N_CHIPS, 8, P_SIZE), 1)
    low = sub < 4

    @pl.when(st[48] != 0)
    def _():
        copies = g_copies()
        for copy in copies:
            copy.start()

        def left_of(t):
            lanes = tile_lanes(t)
            return jnp.concatenate(
                [
                    g_far_a[:, :, lanes].reshape(2 * SHARD, TILE),
                    g_far_b[:, :, lanes].reshape(2 * SHARD, TILE),
                    swap_far[:, :, :, lanes].reshape(4 * SHARD, TILE),
                ],
                axis=0,
            )

        targets = [line_row(st, x, 2, other) for other in (False, True) for x in range(2)]
        project(st, abuf, acc, fb, left_of, targets)
        for copy in copies:
            copy.wait()
        for c in range(COL_TILES):
            cols = slice(c * TILE, (c + 1) * TILE)
            gr = gbuf[0, :, cols]
            gi = gbuf[1, :, cols]
            fr = fb[0, :, cols]
            fi = fb[1, :, cols]
            left = jnp.concatenate(
                [
                    jnp.concatenate([fr, -fi, gr, gi], axis=1),
                    jnp.concatenate([fi, fr, -gi, gr], axis=1),
                ],
                axis=0,
            )
            right = jnp.concatenate([gr, gi, fb[2, :, cols], fb[3, :, cols]], axis=1)
            if c == 0:
                wide[...] = dot_nt(left, right)
            else:
                wide[...] += dot_nt(left, right)
        re = wide[:P_SIZE].reshape(N_CHIPS, 8, P_SIZE)
        im = wide[P_SIZE:].reshape(N_CHIPS, 8, P_SIZE)
        first = jnp.where(low, re, pltpu.roll(im, 4, 1)).astype(jnp.bfloat16)
        second = jnp.where(low, pltpu.roll(re, 4, 1), im).astype(jnp.bfloat16)

        @pl.when(core == 0)
        def _():
            keep[...] = first
            send[...] = second

        @pl.when(core != 0)
        def _():
            keep[...] = second
            send[...] = first

    @pl.when(st[48] == 0)
    def _():
        keep[...] = jnp.zeros_like(keep)
        send[...] = jnp.zeros_like(send)


def align_kernel(index, parts, out):
    total = jnp.sum(parts[...].astype(jnp.float32), axis=0)
    lane = lax.broadcasted_iota(jnp.int32, (1, P_SIZE), 1)
    for i in range(4):
        re = total[i : i + 1]
        im = total[4 + i : 5 + i]
        chosen = lane == index[i]
        anchor_re = jnp.sum(jnp.where(chosen, re, 0.0), axis=1, keepdims=True)
        anchor_im = jnp.sum(jnp.where(chosen, im, 0.0), axis=1, keepdims=True)
        out[i, 0:1, :] = re * anchor_re + im * anchor_im
        out[i, 1:2, :] = im * anchor_re - re * anchor_im


def any_spec():
    return pl.BlockSpec(memory_space=pl.ANY)


def hbm_spec():
    return pl.BlockSpec(memory_space=pltpu.HBM)


def smem_spec():
    return pl.BlockSpec(memory_space=pltpu.SMEM)


def vmem_spec():
    return pl.BlockSpec(memory_space=pltpu.VMEM)


def tile_states(tile_mask):
    rcv = lax.axis_index(RCV)
    src = lax.axis_index(SRC)
    tiles = lax.dynamic_slice(tile_mask, (rcv * ROW_TILES, src * COL_TILES), (ROW_TILES, COL_TILES))
    kept = (tiles == 1).T
    rows = jnp.arange(ROW_TILES)[None, :]
    diag_row = jnp.arange(COL_TILES)[:, None] + src * COL_TILES - rcv * ROW_TILES
    diag = rows == diag_row
    plain = (kept & ~diag).astype(jnp.int32)
    count = jnp.sum(plain, axis=1)
    before = jnp.sum(plain[:, None, :] * (rows[0][None, :] < rows[0][:, None]), axis=2)
    hit = (before[:, None, :] == rows[0][None, :, None]) & (plain[:, None, :] == 1)
    order = jnp.sum(jnp.where(hit, rows[0][None, None, :], 0), axis=2)
    diag_on = jnp.sum((kept & diag).astype(jnp.int32), axis=1)
    diag_at = jnp.clip(diag_row[:, 0], 0, ROW_TILES - 1)
    scalars = jnp.stack(
        [jnp.max(kept.astype(jnp.int32))] + [lax.axis_index(name) for name in ("core", "xh", "z", "xl", "y")]
    )
    return jnp.concatenate(
        [count, jnp.zeros((4,), jnp.int32), order.reshape(-1), diag_on, diag_at, scalars]
    ).astype(jnp.int32)


def body(reflection, green, tile_mask, reference_index):
    lines = jnp.transpose(green, (0, 2, 1))
    state = tile_states(tile_mask)
    core = lax.axis_index("core")
    mid = ROWS // 2

    abuf_shape = jax.ShapeDtypeStruct((COL_TILES, 2, ROWS + TILE, TILE), jnp.bfloat16)
    fb_shape = jax.ShapeDtypeStruct((4, P_SIZE, COLS), jnp.bfloat16)
    abuf = pl.pallas_call(
        load_kernel,
        out_shape=abuf_shape,
        in_specs=[smem_spec(), hbm_spec()],
        out_specs=vmem_spec(),
        scratch_shapes=[pltpu.SemaphoreType.DMA((COL_TILES, ROW_TILES + 1))],
        compiler_params=pltpu.CompilerParams(vmem_limit_bytes=12 << 20),
        cost_estimate=pl.CostEstimate(flops=0, transcendentals=0, bytes_accessed=8 << 20),
        name="load",
    )(state, reflection)

    same = lax.dynamic_slice_in_dim(lines, core * mid, mid, 2)
    other = lax.dynamic_slice_in_dim(lines, (1 - core) * mid, mid, 2)
    part_a = lax.ppermute(same, ALL, crossing(0))
    part_b = lax.ppermute(other, ALL, crossing(1))
    beside = lax.ppermute(lines, "xl", SWAP)
    part_a, part_b, beside, abuf = lax.optimization_barrier((part_a, part_b, beside, abuf))

    g_own = jnp.stack([lines, beside])
    own = jnp.stack([part_a, part_b])
    g_after = lax.ppermute(g_own, "y", ring(1))
    g_before = lax.ppermute(g_own, "y", ring(-1))
    after = lax.ppermute(own, "z", ring(1))
    before = lax.ppermute(own, "z", ring(-1))
    near = lax.ppermute(own, "xh", SWAP)
    g_after, g_before, after, before, near = lax.optimization_barrier(
        (g_after, g_before, after, before, near)
    )

    swap = lax.ppermute(jnp.stack([g_own, g_after, g_before]), "core", SWAP)
    g_far_a = lax.ppermute(g_after[0], "y", ring(1))
    g_far_b = lax.ppermute(g_before[1], "y", ring(-1))
    near_after = lax.ppermute(near, "z", ring(1))
    near_before = lax.ppermute(near, "z", ring(-1))
    far_a = lax.ppermute(after, "z", ring(1))
    fb = pl.pallas_call(
        near_kernel,
        out_shape=fb_shape,
        in_specs=[smem_spec()] + [vmem_spec()] * 4,
        out_specs=vmem_spec(),
        scratch_shapes=[pltpu.VMEM((12 * SHARD, 2 * TILE), jnp.float32)],
        compiler_params=pltpu.CompilerParams(vmem_limit_bytes=24 << 20),
        cost_estimate=pl.CostEstimate(flops=3 << 30, transcendentals=0, bytes_accessed=8 << 20),
        name="near",
    )(state, abuf, g_own, g_after, g_before)
    g_far_a, g_far_b, near_after, near_before, fb = lax.optimization_barrier(
        (g_far_a, g_far_b, near_after, near_before, fb)
    )

    swap_far = lax.ppermute(jnp.stack([g_far_a, g_far_b]), "core", SWAP)
    far_b = lax.ppermute(near_before, "z", ring(-1))
    fb = pl.pallas_call(
        swap_kernel,
        out_shape=fb_shape,
        in_specs=[smem_spec()] + [vmem_spec()] * 3,
        out_specs=vmem_spec(),
        scratch_shapes=[pltpu.VMEM((12 * SHARD, 2 * TILE), jnp.float32)],
        input_output_aliases={2: 0},
        compiler_params=pltpu.CompilerParams(vmem_limit_bytes=24 << 20),
        cost_estimate=pl.CostEstimate(flops=3 << 30, transcendentals=0, bytes_accessed=8 << 20),
        name="swap",
    )(state, abuf, fb, swap)

    block = jax.ShapeDtypeStruct((N_CHIPS, 8, P_SIZE), jnp.bfloat16)
    _, keep, send = pl.pallas_call(
        finish_kernel,
        out_shape=(fb_shape, block, block),
        in_specs=[smem_spec()] + [vmem_spec()] * 5 + [any_spec()] * 8,
        out_specs=(vmem_spec(),) * 3,
        scratch_shapes=[
            pltpu.VMEM((2, P_SIZE, COLS), jnp.bfloat16),
            pltpu.VMEM((8 * SHARD, 2 * TILE), jnp.float32),
            pltpu.VMEM((2 * P_SIZE, P_SIZE), jnp.float32),
            pltpu.SemaphoreType.DMA((16,)),
        ],
        input_output_aliases={2: 0},
        compiler_params=pltpu.CompilerParams(vmem_limit_bytes=32 << 20),
        cost_estimate=pl.CostEstimate(flops=6 << 30, transcendentals=0, bytes_accessed=8 << 20),
        name="finish",
    )(
        state, abuf, fb, g_far_a, g_far_b, swap_far,
        own, near, after, before, near_after, near_before, far_a, far_b,
    )
    taken = lax.ppermute(send, "core", SWAP)
    summed = (keep.astype(jnp.float32) + taken.astype(jnp.float32)).astype(jnp.bfloat16)
    parts = lax.all_to_all(summed, CHIPS, 0, 0)
    return pl.pallas_call(
        align_kernel,
        out_shape=jax.ShapeDtypeStruct((4, 2, P_SIZE), jnp.float32),
        in_specs=[smem_spec(), vmem_spec()],
        out_specs=vmem_spec(),
        name="align",
    )(reference_index, parts)


def solution(mesh):
    fine = Mesh(mesh.devices.reshape([size for _, size in PARTS]), [name for name, _ in PARTS])
    return jax.shard_map(
        body,
        mesh=fine,
        in_specs=(P(None, RCV, SRC), P(None, RCV, SRC), P(), P(ALL)),
        out_specs=P(ALL, None, None),
        check_vma=False,
    )
```

time: 116 us -> 97.2 us (0.84)
  starting transfers between devices: 45.5 us -> 29.1 us
  waiting for transfers between devices: 26.9 us -> 20.4 us
  local copies, waits for them, and re-layouts: 1.12 us -> 5.39 us
  other arithmetic: 5.17 us -> 2.23 us
  Pallas kernels: 16.2 us -> 18.3 us
    ppermute x4, starting transfers between devices: 14.9 us -> 5.47 us  [the longest x1 1.99 us: body(): far_a = lax.ppermute(after, 'z', ring(1))]
    ppermute x4, waiting for transfers between devices: 0.01 us -> 9.41 us  [the longest x1 3.8 us: body(): far_a = lax.ppermute(after, 'z', ring(1))]
    ppermute x1, waiting for transfers between devices: 11 us -> 1.64 us  [body(): g_after = lax.ppermute(g_own, 'y', ring(1))]
    ppermute x1, starting transfers between devices: 12.1 us -> 2.92 us  [body(): near = lax.ppermute(own, 'xh', SWAP)]
    ppermute x1, waiting for transfers between devices: 6.51 us -> 0.01 us  [body(): beside = lax.ppermute(lines, 'xl', SWAP)]
    ppermute x1, starting transfers between devices: 1.52 us -> 7.84 us  [body(): g_before = lax.ppermute(g_own, 'y', ring(-1))]
    ppermute x1, starting transfers between devices: 6.98 us -> 1.57 us  [body(): before = lax.ppermute(own, 'z', ring(-1))]
    ppermute x1, starting transfers between devices: 1.57 us -> 6.94 us  [body(): beside = lax.ppermute(lines, 'xl', SWAP)]
  transfers between devices with their start and end apart: 17 -> 17, of which waited for: 7 -> 9; matrix products, arithmetic and copies ran while one was open for 3% -> 3% of each run, Pallas kernels for 6% -> 7%
where the time goes in v3:
time: 97.2 us; the launch traced here: 97.1 us
  starting transfers between devices  29.1 us (30%)
  blocking collectives  21.6 us (22%)
  waiting for transfers between devices  20.4 us (21%)
  Pallas kernels  18.3 us (19%)
  local copies, waits for them, and re-layouts  5.39 us (6%)
  other arithmetic  2.23 us (2%)
    all_to_all x1, blocking collectives, body(): parts = lax.all_to_all(summed, CHIPS, 0, 0)  21.6 us
    pallas_call x1, Pallas kernels, body(): pl.pallas_call(finish_kernel, out_shape=(fb_shape, block, block), in_spec...  9.19 us
    ppermute x1, starting transfers between devices, body(): g_before = lax.ppermute(g_own, 'y', ring(-1))  7.84 us
    ppermute x1, starting transfers between devices, body(): beside = lax.ppermute(lines, 'xl', SWAP)  6.94 us
    ppermute x1, waiting for transfers between devices, body(): near = lax.ppermute(own, 'xh', SWAP)  4.26 us
    ppermute x1, waiting for transfers between devices, body(): far_a = lax.ppermute(after, 'z', ring(1))  3.8 us
    ppermute x1, waiting for transfers between devices, body(): g_far_b = lax.ppermute(g_before[1], 'y', ring(-1))  3.77 us
    unnamed x4, local copies, waits for them, and re-layouts  3.39 us
  transfers between devices with their start and end apart: 17, of which 9 were waited for; matrix products, arithmetic and copies ran while one was open for 3% of the time, Pallas kernels for 7%

profile of v3, /device:TPU:0, one launch (start us, length us, event | category | flops | bytes accessed | tf_op | source)
XLA Modules:
  0.0 97.1 jit_solution(9784353396241098246)
XLA Ops:
  0.0 1.0 %dynamic-slice_bitcast_fusion = (bf16[2,32,1024]{2,1,0:T(8,128)(2,1)S(1)}, bf16[2,32,1024]{2,1,0:T(8,128)(2,1)S(1)}) fusion(bf16[2,2048,32]{1,2,0:T(8,128)(2,1)} %param.5, s32[]{:T(128)S(6)} %select_n.20, s32[]{:T(128)S(6)} %select_n.19), kind=kLoop, calls=%fused_computation.7 | loop fusion | bytes 524296 | tf_op jit(solution)/shard_map/dynamic_slice | solution.py:339
  1.7 6.9 %collective-permute-start.2 = (bf16[2,32,2048]{2,1,0:T(8,128)(2,1)}, bf16[2,32,2048]{2,1,0:T(8,128)(2,1)S(1)}, u32[]{:S(2)}, u32[]{:S(2)}) collective-permute-start(bf16[2,32,2048]{2,1,0:T(8,128)(2,1)} %bitcast.33), channel_id=1, source_target_pairs={{0,2},{2,0},{1,3},{3,1},{4,6},{6,4},{5,7},{7,5},{8,10},{10,8},{9,1... | collective-permute-start | bytes 786440 | tf_op jit(solution)/shard_map/ppermute | solution.py:342
  11.4 3.4 %copy-done = bf16[2,2048,1024]{2,1,0:T(8,128)(2,1)S(1)} copy-done((bf16[2,2048,1024]{2,1,0:T(8,128)(2,1)S(1)}, bf16[2,2048,1024]{2,1,0:T(8,128)(2,1)}, u32[]{:S(2)}) %copy-start) | copy-done | bytes 8388632
  14.8 1.6 %load.1.abuf = bf16[4,2,2304,256]{3,2,1,0:T(8,128)(2,1)S(1)} custom-call(s32[54]{0:T(128)S(1)} %concatenate.3.st, bf16[2,2048,1024]{2,1,0:T(8,128)(2,1)S(1)} %copy-done), custom_call_target="tpu_custom_call" | custom-call | bytes 8388608 | tf_op jit(solution)/shard_map/load/pallas_call | solution.py:327
  16.6 7.8 %collective-permute-start.4 = (bf16[2,2,32,2048]{3,2,1,0:T(8,128)(2,1)S(1)}, bf16[2,2,32,2048]{3,2,1,0:T(8,128)(2,1)S(1)}, u32[]{:S(2)}, u32[]{:S(2)}) collective-permute-start(bf16[2,2,32,2048]{3,2,1,0:T(8,128)(2,1)S(1)} %get-tuple-element.45.own), channel_id=1, source_target_pairs={{0,12},{4,0},{8,4},{12,8},{1,13},{5,1},{9,5},{13,9},{2,14},{6,2},{... | collective-permute-start | bytes 1572872 | tf_op jit(solution)/shard_map/ppermute | solution.py:348
  24.4 2.9 %collective-permute-start.7 = (bf16[2,2,32,1024]{3,2,1,0:T(8,128)(2,1)S(1)}, bf16[2,2,32,1024]{3,2,1,0:T(8,128)(2,1)S(1)}, u32[]{:S(2)}, u32[]{:S(2)}) collective-permute-start(bf16[2,2,32,1024]{3,2,1,0:T(8,128)(2,1)S(1)} %pad_maximum_fusion.3.own), channel_id=1, source_target_pairs={{0,64},{64,0},{1,65},{65,1},{2,66},{66,2},{3,67},{67,3},{4,68},{68... | collective-permute-start | bytes 786440 | tf_op jit(solution)/shard_map/ppermute | solution.py:351
  27.4 1.6 %collective-permute-start.6 = (bf16[2,2,32,1024]{3,2,1,0:T(8,128)(2,1)S(1)}, bf16[2,2,32,1024]{3,2,1,0:T(8,128)(2,1)S(1)}, u32[]{:S(2)}, u32[]{:S(2)}) collective-permute-start(bf16[2,2,32,1024]{3,2,1,0:T(8,128)(2,1)S(1)} %pad_maximum_fusion.3.own), channel_id=1, source_target_pairs={{0,48},{16,0},{32,16},{48,32},{1,49},{17,1},{33,17},{49,33},{2,50}... | collective-permute-start | bytes 786440 | tf_op jit(solution)/shard_map/ppermute | solution.py:350
  29.4 4.3 %collective-permute-done.7.near = bf16[2,2,32,1024]{3,2,1,0:T(8,128)(2,1)S(1)} collective-permute-done((bf16[2,2,32,1024]{3,2,1,0:T(8,128)(2,1)S(1)}, bf16[2,2,32,1024]{3,2,1,0:T(8,128)(2,1)S(1)}, u32[]{:S(2)}, u32[]{:S(2)}) %collective-permute-start.7) | collective-permute-done | bytes 262176 | tf_op jit(solution)/shard_map/ppermute | solution.py:351
  33.7 1.5 %collective-permute-done.6.before = bf16[2,2,32,1024]{3,2,1,0:T(8,128)(2,1)S(1)} collective-permute-done((bf16[2,2,32,1024]{3,2,1,0:T(8,128)(2,1)S(1)}, bf16[2,2,32,1024]{3,2,1,0:T(8,128)(2,1)S(1)}, u32[]{:S(2)}, u32[]{:S(2)}) %collective-permute-start.6) | collective-permute-done | bytes 262176 | tf_op jit(solution)/shard_map/ppermute | solution.py:350
  35.1 1.9 %collective-permute-done.5.after = bf16[2,2,32,1024]{3,2,1,0:T(8,128)(2,1)S(1)} collective-permute-done((bf16[2,2,32,1024]{3,2,1,0:T(8,128)(2,1)S(1)}, bf16[2,2,32,1024]{3,2,1,0:T(8,128)(2,1)S(1)}, u32[]{:S(2)}, u32[]{:S(2)}) %collective-permute-start.5) | collective-permute-done | bytes 262176 | tf_op jit(solution)/shard_map/ppermute | solution.py:349
  37.1 1.6 %collective-permute-done.3.after = bf16[2,2,32,2048]{3,2,1,0:T(8,128)(2,1)S(1)} collective-permute-done((bf16[2,2,32,2048]{3,2,1,0:T(8,128)(2,1)S(1)}, bf16[2,2,32,2048]{3,2,1,0:T(8,128)(2,1)S(1)}, u32[]{:S(2)}, u32[]{:S(2)}) %collective-permute-start.3) | collective-permute-done | bytes 524320 | tf_op jit(solution)/shard_map/ppermute | solution.py:347
  38.7 1.8 %collective-permute-start.11 = (bf16[2,2,32,1024]{3,2,1,0:T(8,128)(2,1)S(1)}, bf16[2,2,32,1024]{3,2,1,0:T(8,128)(2,1)S(1)}, u32[]{:S(2)}, u32[]{:S(2)}) collective-permute-start(bf16[2,2,32,1024]{3,2,1,0:T(8,128)(2,1)S(1)} %collective-permute-done.7.near), channel_id=1, source_target_pairs={{0,48},{16,0},{32,16},{48,32},{1,49},{17,1},{33,17},{49,33},{2,50}... | collective-permute-start | bytes 786440 | tf_op jit(solution)/shard_map/ppermute | solution.py:360
  42.1 1.7 %collective-permute-start.8 = (bf16[2,32,2048]{2,1,0:T(8,128)(2,1)S(1)}, bf16[2,32,2048]{2,1,0:T(8,128)(2,1)S(1)}, u32[]{:S(2)}, u32[]{:S(2)}) collective-permute-start(bf16[2,32,2048]{2,1,0:T(8,128)(2,1)S(1)} %slice_bitcast_fusion.1), channel_id=1, source_target_pairs={{0,4},{4,8},{8,12},{12,0},{1,5},{5,9},{9,13},{13,1},{2,6},{6,10},{... | collective-permute-start | bytes 786440 | tf_op jit(solution)/shard_map/ppermute | solution.py:357
  43.8 2.8 %near.1.fb_in = bf16[4,512,1024]{2,1,0:T(8,128)(2,1)S(1)} custom-call(s32[54]{0:T(128)S(1)} %concatenate.3.st, bf16[4,2,2304,256]{3,2,1,0:T(8,128)(2,1)S(1)} %load.1.abuf, bf16[2,2,32,2048]{3,2,1,0:T(8,128)(2,1)S(1)} %get-tuple-element.45.own, bf16[2,2,32,2048]{3,2,1,0:T(8,128)(2,1)S(1)} %collective-permute-done.3.after, ...), custom_call_target="tpu_custom_call" | custom-call | flops 3221225472 | bytes 8388608 | tf_op jit(solution)/shard_map/near/pallas_call | solution.py:362
  46.6 3.8 %collective-permute-done.9.g_far_b = bf16[2,32,2048]{2,1,0:T(8,128)(2,1)S(1)} collective-permute-done((bf16[2,32,2048]{2,1,0:T(8,128)(2,1)S(1)}, bf16[2,32,2048]{2,1,0:T(8,128)(2,1)S(1)}, u32[]{:S(2)}, u32[]{:S(2)}) %collective-permute-start.9) | collective-permute-done | bytes 262176 | tf_op jit(solution)/shard_map/ppermute | solution.py:358
  50.4 1.4 %collective-permute-done.8.g_far_a = bf16[2,32,2048]{2,1,0:T(8,128)(2,1)S(1)} collective-permute-done((bf16[2,32,2048]{2,1,0:T(8,128)(2,1)S(1)}, bf16[2,32,2048]{2,1,0:T(8,128)(2,1)S(1)}, u32[]{:S(2)}, u32[]{:S(2)}) %collective-permute-start.8) | collective-permute-done | bytes 262176 | tf_op jit(solution)/shard_map/ppermute | solution.py:357
  51.9 2.0 %collective-permute-start.14 = (bf16[2,2,32,1024]{3,2,1,0:T(8,128)(2,1)S(1)}, bf16[2,2,32,1024]{3,2,1,0:T(8,128)(2,1)S(1)}, u32[]{:S(2)}, u32[]{:S(2)}) collective-permute-start(bf16[2,2,32,1024]{3,2,1,0:T(8,128)(2,1)S(1)} %collective-permute-done.5.after), channel_id=1, source_target_pairs={{0,16},{16,32},{32,48},{48,0},{1,17},{17,33},{33,49},{49,1},{2,18}... | collective-permute-start | bytes 786440 | tf_op jit(solution)/shard_map/ppermute | solution.py:361
  53.9 1.3 %collective-permute-start.15 = (bf16[2,2,32,1024]{3,2,1,0:T(8,128)(2,1)S(1)}, bf16[2,2,32,1024]{3,2,1,0:T(8,128)(2,1)S(1)}, u32[]{:S(2)}, u32[]{:S(2)}) collective-permute-start(bf16[2,2,32,1024]{3,2,1,0:T(8,128)(2,1)S(1)} %collective-permute-done.11.near_before), channel_id=1, source_target_pairs={{0,48},{16,0},{32,16},{48,32},{1,49},{17,1},{33,17},{49,33},{2,50}... | collective-permute-start | bytes 786440 | tf_op jit(solution)/shard_map/ppermute | solution.py:377
  55.2 2.8 %swap.1.fb_in = bf16[4,512,1024]{2,1,0:T(8,128)(2,1)S(1)} custom-call(s32[54]{0:T(128)S(1)} %concatenate.3.st, bf16[4,2,2304,256]{3,2,1,0:T(8,128)(2,1)S(1)} %load.1.abuf, bf16[4,512,1024]{2,1,0:T(8,128)(2,1)S(1)} %near.1.fb_in, bf16[3,2,2,32,2048]{4,3,2,1,0:T(8,128)(2,1)S(1)} %collective-permute-done.12.swap), custom_call_target="tpu_custom_call", output_to_operand_aliasing={{}: (2, {})} | custom-call | flops 3221225472 | bytes 8388608 | tf_op jit(solution)/shard_map/swap/pallas_call | solution.py:378
  58.1 3.8 %collective-permute-done.14.far_a = bf16[2,2,32,1024]{3,2,1,0:T(8,128)(2,1)S(1)} collective-permute-done((bf16[2,2,32,1024]{3,2,1,0:T(8,128)(2,1)S(1)}, bf16[2,2,32,1024]{3,2,1,0:T(8,128)(2,1)S(1)}, u32[]{:S(2)}, u32[]{:S(2)}) %collective-permute-start.14) | collective-permute-done | bytes 262176 | tf_op jit(solution)/shard_map/ppermute | solution.py:361
  62.3 9.2 %finish.1 = (bf16[4,512,1024]{2,1,0:T(8,128)(2,1)S(1)}, bf16[64,8,512]{2,1,0:T(8,128)(2,1)S(1)}, bf16[64,8,512]{2,1,0:T(8,128)(2,1)S(1)}) custom-call(s32[54]{0:T(128)S(1)} %concatenate.3.st, bf16[4,2,2304,256]{3,2,1,0:T(8,128)(2,1)S(1)} %load.1.abuf, bf16[4,512,1024]{2,1,0:T(8,128)(2,1)S(1)} %swap.1.fb_in, ...), custom_call_target="tpu_custom_call", output_to_operand_aliasing={{0}: (2, {})} | custom-call | flops 6442450944 | bytes 8388608 | tf_op jit(solution)/shard_map/finish/pallas_call | solution.py:391
  71.9 1.6 %collective-permute-done.16 = bf16[64,8,512]{2,1,0:T(8,128)(2,1)S(1)} collective-permute-done((bf16[64,8,512]{2,1,0:T(8,128)(2,1)S(1)}, bf16[64,8,512]{2,1,0:T(8,128)(2,1)S(1)}, u32[]{:S(2)}, u32[]{:S(2)}) %collective-permute-start.16) | collective-permute-done | bytes 524320 | tf_op jit(solution)/shard_map/ppermute | solution.py:410
  73.6 21.6 %all_to_all.5.parts = bf16[64,8,512]{2,1,0:T(8,128)(2,1)} all-to-all(bf16[64,8,512]{2,1,0:T(8,128)(2,1)S(1)} %add_convert_fusion), channel_id=1, replica_groups=mesh['xh'=2,'z'=4,'y'=4,'xl'=2,'core'=2] {'xh','z','y','xl'}, dimensions={0} | all-to-all | bytes 1048576 | tf_op jit(solution)/shard_map/all_to_all | solution.py:412
  95.2 1.8 %align.1 = f32[4,2,512]{2,1,0:T(2,128)} custom-call(s32[4]{0:T(128)} %index.1, bf16[64,8,512]{2,1,0:T(8,128)(2,1)} %all_to_all.5.parts), custom_call_target="tpu_custom_call" | custom-call | tf_op jit(solution)/shard_map/align/pallas_call | solution.py:413
  (40 shorter events, 6.7 us)
Async XLA Ops:
  1.0 15.5 %collective-permute-start.1 = (bf16[2,32,1024]{2,1,0:T(8,128)(2,1)S(1)}, bf16[2,32,1024]{2,1,0:T(8,128)(2,1)S(1)}, u32[]{:S(2)}, u32[]{:S(2)}) collective-permute-start(bf16[2,32,1024]{2,1,0:T(8,128)(2,1)S(1)} %get-tuple-element.46), channel_id=1, source_target_pairs={{0,1},{1,0},{2,65},{3,64},{4,17},{5,16},{6,81},{7,80},{8,33},{9,32... | collective-permute-start | bytes 393224 | tf_op jit(solution)/shard_map/ppermute | solution.py:341
  1.1 15.4 %collective-permute-start = (bf16[2,32,1024]{2,1,0:T(8,128)(2,1)S(1)}, bf16[2,32,1024]{2,1,0:T(8,128)(2,1)S(1)}, u32[]{:S(2)}, u32[]{:S(2)}) collective-permute-start(bf16[2,32,1024]{2,1,0:T(8,128)(2,1)S(1)} %get-tuple-element.47), channel_id=1, source_target_pairs={{0,0},{1,1},{2,64},{3,65},{4,16},{5,17},{6,80},{7,81},{8,32},{9,33... | collective-permute-start | bytes 393224 | tf_op jit(solution)/shard_map/ppermute | solution.py:340
  1.7 14.7 %collective-permute-start.2 = (bf16[2,32,2048]{2,1,0:T(8,128)(2,1)}, bf16[2,32,2048]{2,1,0:T(8,128)(2,1)S(1)}, u32[]{:S(2)}, u32[]{:S(2)}) collective-permute-start(bf16[2,32,2048]{2,1,0:T(8,128)(2,1)} %bitcast.33), channel_id=1, source_target_pairs={{0,2},{2,0},{1,3},{3,1},{4,6},{6,4},{5,7},{7,5},{8,10},{10,8},{9,1... | collective-permute-start | bytes 786440 | tf_op jit(solution)/shard_map/ppermute | solution.py:342
  11.4 3.4 %copy-start = (bf16[2,2048,1024]{2,1,0:T(8,128)(2,1)S(1)}, bf16[2,2048,1024]{2,1,0:T(8,128)(2,1)}, u32[]{:S(2)}) copy-start(bf16[2,2048,1024]{2,1,0:T(8,128)(2,1)} %a.1) | copy-start | bytes 25165828
  14.8 1.7 %copy-start.1 = (bf16[2,2048,32]{1,2,0:T(8,128)(2,1)S(1)}, bf16[2,2048,32]{1,2,0:T(8,128)(2,1)}, u32[]{:S(2)}) copy-start(bf16[2,2048,32]{1,2,0:T(8,128)(2,1)} %param.5) | copy-start | bytes 786436
  16.6 20.5 %collective-permute-start.4 = (bf16[2,2,32,2048]{3,2,1,0:T(8,128)(2,1)S(1)}, bf16[2,2,32,2048]{3,2,1,0:T(8,128)(2,1)S(1)}, u32[]{:S(2)}, u32[]{:S(2)}) collective-permute-start(bf16[2,2,32,2048]{3,2,1,0:T(8,128)(2,1)S(1)} %get-tuple-element.45.own), channel_id=1, source_target_pairs={{0,12},{4,0},{8,4},{12,8},{1,13},{5,1},{9,5},{13,9},{2,14},{6,2},{... | collective-permute-start | bytes 1572872 | tf_op jit(solution)/shard_map/ppermute | solution.py:348
  24.4 14.3 %collective-permute-start.3 = (bf16[2,2,32,2048]{3,2,1,0:T(8,128)(2,1)S(1)}, bf16[2,2,32,2048]{3,2,1,0:T(8,128)(2,1)S(1)}, u32[]{:S(2)}, u32[]{:S(2)}) collective-permute-start(bf16[2,2,32,2048]{3,2,1,0:T(8,128)(2,1)S(1)} %get-tuple-element.45.own), channel_id=1, source_target_pairs={{0,4},{4,8},{8,12},{12,0},{1,5},{5,9},{9,13},{13,1},{2,6},{6,10},{... | collective-permute-start | bytes 1572872 | tf_op jit(solution)/shard_map/ppermute | solution.py:347
  24.4 9.2 %collective-permute-start.7 = (bf16[2,2,32,1024]{3,2,1,0:T(8,128)(2,1)S(1)}, bf16[2,2,32,1024]{3,2,1,0:T(8,128)(2,1)S(1)}, u32[]{:S(2)}, u32[]{:S(2)}) collective-permute-start(bf16[2,2,32,1024]{3,2,1,0:T(8,128)(2,1)S(1)} %pad_maximum_fusion.3.own), channel_id=1, source_target_pairs={{0,64},{64,0},{1,65},{65,1},{2,66},{66,2},{3,67},{67,3},{4,68},{68... | collective-permute-start | bytes 786440 | tf_op jit(solution)/shard_map/ppermute | solution.py:351
  27.4 7.7 %collective-permute-start.6 = (bf16[2,2,32,1024]{3,2,1,0:T(8,128)(2,1)S(1)}, bf16[2,2,32,1024]{3,2,1,0:T(8,128)(2,1)S(1)}, u32[]{:S(2)}, u32[]{:S(2)}) collective-permute-start(bf16[2,2,32,1024]{3,2,1,0:T(8,128)(2,1)S(1)} %pad_maximum_fusion.3.own), channel_id=1, source_target_pairs={{0,48},{16,0},{32,16},{48,32},{1,49},{17,1},{33,17},{49,33},{2,50}... | collective-permute-start | bytes 786440 | tf_op jit(solution)/shard_map/ppermute | solution.py:350
  28.9 8.1 %collective-permute-start.5 = (bf16[2,2,32,1024]{3,2,1,0:T(8,128)(2,1)S(1)}, bf16[2,2,32,1024]{3,2,1,0:T(8,128)(2,1)S(1)}, u32[]{:S(2)}, u32[]{:S(2)}) collective-permute-start(bf16[2,2,32,1024]{3,2,1,0:T(8,128)(2,1)S(1)} %pad_maximum_fusion.3.own), channel_id=1, source_target_pairs={{0,16},{16,32},{32,48},{48,0},{1,17},{17,33},{33,49},{49,1},{2,18}... | collective-permute-start | bytes 786440 | tf_op jit(solution)/shard_map/ppermute | solution.py:349
  38.7 13.1 %collective-permute-start.11 = (bf16[2,2,32,1024]{3,2,1,0:T(8,128)(2,1)S(1)}, bf16[2,2,32,1024]{3,2,1,0:T(8,128)(2,1)S(1)}, u32[]{:S(2)}, u32[]{:S(2)}) collective-permute-start(bf16[2,2,32,1024]{3,2,1,0:T(8,128)(2,1)S(1)} %collective-permute-done.7.near), channel_id=1, source_target_pairs={{0,48},{16,0},{32,16},{48,32},{1,49},{17,1},{33,17},{49,33},{2,50}... | collective-permute-start | bytes 786440 | tf_op jit(solution)/shard_map/ppermute | solution.py:360
  40.5 11.3 %collective-permute-start.10 = (bf16[2,2,32,1024]{3,2,1,0:T(8,128)(2,1)S(1)}, bf16[2,2,32,1024]{3,2,1,0:T(8,128)(2,1)S(1)}, u32[]{:S(2)}, u32[]{:S(2)}) collective-permute-start(bf16[2,2,32,1024]{3,2,1,0:T(8,128)(2,1)S(1)} %collective-permute-done.7.near), channel_id=1, source_target_pairs={{0,16},{16,32},{32,48},{48,0},{1,17},{17,33},{33,49},{49,1},{2,18}... | collective-permute-start | bytes 786440 | tf_op jit(solution)/shard_map/ppermute | solution.py:359
  41.5 13.8 %collective-permute-start.12 = (bf16[3,2,2,32,2048]{4,3,2,1,0:T(8,128)(2,1)S(1)}, bf16[3,2,2,32,2048]{4,3,2,1,0:T(8,128)(2,1)S(1)}, u32[]{:S(2)}, u32[]{:S(2)}) collective-permute-start(bf16[3,2,2,32,2048]{4,3,2,1,0:T(8,128)(2,1)S(1)} %pad_maximum_fusion), channel_id=1, source_target_pairs={{0,1},{1,0},{2,3},{3,2},{4,5},{5,4},{6,7},{7,6},{8,9},{9,8},{10,11... | collective-permute-start | bytes 4718600 | tf_op jit(solution)/shard_map/ppermute | solution.py:356
  41.6 8.8 %collective-permute-start.9 = (bf16[2,32,2048]{2,1,0:T(8,128)(2,1)S(1)}, bf16[2,32,2048]{2,1,0:T(8,128)(2,1)S(1)}, u32[]{:S(2)}, u32[]{:S(2)}) collective-permute-start(bf16[2,32,2048]{2,1,0:T(8,128)(2,1)S(1)} %slice_bitcast_fusion), channel_id=1, source_target_pairs={{0,12},{4,0},{8,4},{12,8},{1,13},{5,1},{9,5},{13,9},{2,14},{6,2},{... | collective-permute-start | bytes 786440 | tf_op jit(solution)/shard_map/ppermute | solution.py:358
  42.1 9.7 %collective-permute-start.8 = (bf16[2,32,2048]{2,1,0:T(8,128)(2,1)S(1)}, bf16[2,32,2048]{2,1,0:T(8,128)(2,1)S(1)}, u32[]{:S(2)}, u32[]{:S(2)}) collective-permute-start(bf16[2,32,2048]{2,1,0:T(8,128)(2,1)S(1)} %slice_bitcast_fusion.1), channel_id=1, source_target_pairs={{0,4},{4,8},{8,12},{12,0},{1,5},{5,9},{9,13},{13,1},{2,6},{6,10},{... | collective-permute-start | bytes 786440 | tf_op jit(solution)/shard_map/ppermute | solution.py:357
  51.8 10.5 %collective-permute-start.13 = (bf16[2,2,32,2048]{3,2,1,0:T(8,128)(2,1)S(1)}, bf16[2,2,32,2048]{3,2,1,0:T(8,128)(2,1)S(1)}, u32[]{:S(2)}, u32[]{:S(2)}) collective-permute-start(bf16[2,2,32,2048]{3,2,1,0:T(8,128)(2,1)S(1)} %pad_maximum_fusion.2), channel_id=1, source_target_pairs={{0,1},{1,0},{2,3},{3,2},{4,5},{5,4},{6,7},{7,6},{8,9},{9,8},{10,11... | collective-permute-start | bytes 1572872 | tf_op jit(solution)/shard_map/ppermute | solution.py:376
  51.9 9.9 %collective-permute-start.14 = (bf16[2,2,32,1024]{3,2,1,0:T(8,128)(2,1)S(1)}, bf16[2,2,32,1024]{3,2,1,0:T(8,128)(2,1)S(1)}, u32[]{:S(2)}, u32[]{:S(2)}) collective-permute-start(bf16[2,2,32,1024]{3,2,1,0:T(8,128)(2,1)S(1)} %collective-permute-done.5.after), channel_id=1, source_target_pairs={{0,16},{16,32},{32,48},{48,0},{1,17},{17,33},{33,49},{49,1},{2,18}... | collective-permute-start | bytes 786440 | tf_op jit(solution)/shard_map/ppermute | solution.py:361
  53.9 8.4 %collective-permute-start.15 = (bf16[2,2,32,1024]{3,2,1,0:T(8,128)(2,1)S(1)}, bf16[2,2,32,1024]{3,2,1,0:T(8,128)(2,1)S(1)}, u32[]{:S(2)}, u32[]{:S(2)}) collective-permute-start(bf16[2,2,32,1024]{3,2,1,0:T(8,128)(2,1)S(1)} %collective-permute-done.11.near_before), channel_id=1, source_target_pairs={{0,48},{16,0},{32,16},{48,32},{1,49},{17,1},{33,17},{49,33},{2,50}... | collective-permute-start | bytes 786440 | tf_op jit(solution)/shard_map/ppermute | solution.py:377
  71.5 2.0 %collective-permute-start.16 = (bf16[64,8,512]{2,1,0:T(8,128)(2,1)S(1)}, bf16[64,8,512]{2,1,0:T(8,128)(2,1)S(1)}, u32[]{:S(2)}, u32[]{:S(2)}) collective-permute-start(bf16[64,8,512]{2,1,0:T(8,128)(2,1)S(1)} %get-tuple-element.36), channel_id=1, source_target_pairs={{0,1},{1,0},{2,3},{3,2},{4,5},{5,4},{6,7},{7,6},{8,9},{9,8},{10,11... | collective-permute-start | bytes 1572872 | tf_op jit(solution)/shard_map/ppermute | solution.py:410

commit v4 on v3

--- a/solution.py
+++ b/solution.py
@@ -160,53 +160,39 @@
         project(st, abuf, acc, fb, left_of, targets)
 
 
-def swap_kernel(st, abuf, fb_in, swap, fb, acc):
-    @pl.when(st[48] != 0)
-    def _():
-        def left_of(t):
-            return swap[:, :, :, :, tile_lanes(t)].reshape(12 * SHARD, TILE)
-
-        targets = [line_row(st, x, step, True) for step in (0, -1, 1) for x in range(2)]
-        project(st, abuf, acc, fb, left_of, targets)
-
-
-def finish_kernel(
-    st, abuf, fb_in, g_far_a, g_far_b, swap_far,
-    own, near, after, before, near_after, near_before, far_a, far_b,
-    fb, keep, send, gbuf, acc, wide, gsem,
-):
-    core = st[49]
-    xh = st[50]
-    z = st[51]
-
-    def g_copies():
-        copies = []
-
-        def add(ref, x_other, z_step, part):
+def row_copies(st, gbuf, sem, pieces):
+    core, xh, z = st[49], st[50], st[51]
+    copies = []
+    for ref, x_other, z_step in pieces:
+        for part in range(2):
             block = 2 * ((z + z_step + 4) % 4) + (1 - xh if x_other else xh)
             slot = core if part == 0 else 1 - core
             row = pl.multiple_of(block * 64 + slot * SHARD, SHARD)
-            copies.append(
-                pltpu.make_async_copy(ref, gbuf.at[:, pl.ds(row, SHARD), :], gsem.at[len(copies)])
-            )
-
-        for part in range(2):
-            add(own.at[part], False, 0, part)
-            add(near.at[part], True, 0, part)
-            add(after.at[part], False, -1, part)
-            add(before.at[part], False, 1, part)
-            add(near_after.at[part], True, -1, part)
-            add(near_before.at[part], True, 1, part)
-            add(far_a.at[part], False, 2, part)
-            add(far_b.at[part], True, 2, part)
-        return copies
-
-    sub = lax.broadcasted_iota(jnp.int32, (N_CHIPS, 8, P_SIZE), 1)
-    low = sub < 4
-
+            target = gbuf.at[:, pl.ds(row, SHARD), :]
+            copies.append(pltpu.make_async_copy(ref.at[part], target, sem.at[len(copies)]))
+    return copies
+
+
+def rest_kernel(
+    st, abuf, fb_in, swap, g_far_a, g_far_b, swap_far,
+    own, near, after, before, near_after, near_before,
+    fb, gbuf, acc, gsem,
+):
     @pl.when(st[48] != 0)
     def _():
-        copies = g_copies()
+        copies = row_copies(
+            st,
+            gbuf,
+            gsem,
+            (
+                (own, False, 0),
+                (near, True, 0),
+                (after, False, -1),
+                (before, False, 1),
+                (near_after, True, -1),
+                (near_before, True, 1),
+            ),
+        )
         for copy in copies:
             copy.start()
 
@@ -214,6 +200,7 @@
             lanes = tile_lanes(t)
             return jnp.concatenate(
                 [
+                    swap[:, :, :, :, lanes].reshape(12 * SHARD, TILE),
                     g_far_a[:, :, lanes].reshape(2 * SHARD, TILE),
                     g_far_b[:, :, lanes].reshape(2 * SHARD, TILE),
                     swap_far[:, :, :, lanes].reshape(4 * SHARD, TILE),
@@ -221,8 +208,23 @@
                 axis=0,
             )
 
-        targets = [line_row(st, x, 2, other) for other in (False, True) for x in range(2)]
+        targets = [line_row(st, x, step, True) for step in (0, -1, 1) for x in range(2)]
+        targets += [line_row(st, x, 2, other) for other in (False, True) for x in range(2)]
         project(st, abuf, acc, fb, left_of, targets)
+        for copy in copies:
+            copy.wait()
+
+
+def finish_kernel(st, fb, gbuf_in, far_a, far_b, gbuf, keep, send, wide, gsem):
+    core = st[49]
+    sub = lax.broadcasted_iota(jnp.int32, (N_CHIPS, 8, P_SIZE), 1)
+    low = sub < 4
+
+    @pl.when(st[48] != 0)
+    def _():
+        copies = row_copies(st, gbuf, gsem, ((far_a, False, 2), (far_b, True, 2)))
+        for copy in copies:
+            copy.start()
         for copy in copies:
             copy.wait()
         for c in range(COL_TILES):
@@ -322,6 +324,20 @@
     core = lax.axis_index("core")
     mid = ROWS // 2
 
+    first = lax.optimization_barrier((core, state[48]))[0]
+    same = lax.dynamic_slice_in_dim(lines, first * mid, mid, 2)
+    other = lax.dynamic_slice_in_dim(lines, (1 - first) * mid, mid, 2)
+    part_a = lax.ppermute(same, ALL, crossing(0))
+    part_b = lax.ppermute(other, ALL, crossing(1))
+    beside = lax.ppermute(lines, "xl", SWAP)
+
+    g_own = jnp.stack([lines, beside])
+    own = jnp.stack([part_a, part_b])
+    g_after = lax.ppermute(g_own, "y", ring(1))
+    g_before = lax.ppermute(g_own, "y", ring(-1))
+    after = lax.ppermute(own, "z", ring(1))
+    before = lax.ppermute(own, "z", ring(-1))
+    near = lax.ppermute(own, "xh", SWAP)
     abuf_shape = jax.ShapeDtypeStruct((COL_TILES, 2, ROWS + TILE, TILE), jnp.bfloat16)
     fb_shape = jax.ShapeDtypeStruct((4, P_SIZE, COLS), jnp.bfloat16)
     abuf = pl.pallas_call(
@@ -333,25 +349,9 @@
         compiler_params=pltpu.CompilerParams(vmem_limit_bytes=12 << 20),
         cost_estimate=pl.CostEstimate(flops=0, transcendentals=0, bytes_accessed=8 << 20),
         name="load",
-    )(state, reflection)
-
-    same = lax.dynamic_slice_in_dim(lines, core * mid, mid, 2)
-    other = lax.dynamic_slice_in_dim(lines, (1 - core) * mid, mid, 2)
-    part_a = lax.ppermute(same, ALL, crossing(0))
-    part_b = lax.ppermute(other, ALL, crossing(1))
-    beside = lax.ppermute(lines, "xl", SWAP)
-    part_a, part_b, beside, abuf = lax.optimization_barrier((part_a, part_b, beside, abuf))
-
-    g_own = jnp.stack([lines, beside])
-    own = jnp.stack([part_a, part_b])
-    g_after = lax.ppermute(g_own, "y", ring(1))
-    g_before = lax.ppermute(g_own, "y", ring(-1))
-    after = lax.ppermute(own, "z", ring(1))
-    before = lax.ppermute(own, "z", ring(-1))
-    near = lax.ppermute(own, "xh", SWAP)
-    g_after, g_before, after, before, near = lax.optimization_barrier(
-        (g_after, g_before, after, before, near)
-    )
+    )(state, pltpu.with_memory_space_constraint(reflection, pltpu.HBM))
+    g_after, g_before, _ = lax.optimization_barrier((g_after, g_before, own))
+    abuf, near, after, before = lax.optimization_barrier((abuf, near, after, before))
 
     swap = lax.ppermute(jnp.stack([g_own, g_after, g_before]), "core", SWAP)
     g_far_a = lax.ppermute(g_after[0], "y", ring(1))
@@ -375,38 +375,40 @@
 
     swap_far = lax.ppermute(jnp.stack([g_far_a, g_far_b]), "core", SWAP)
     far_b = lax.ppermute(near_before, "z", ring(-1))
-    fb = pl.pallas_call(
-        swap_kernel,
-        out_shape=fb_shape,
-        in_specs=[smem_spec()] + [vmem_spec()] * 3,
-        out_specs=vmem_spec(),
-        scratch_shapes=[pltpu.VMEM((12 * SHARD, 2 * TILE), jnp.float32)],
+    gbuf_shape = jax.ShapeDtypeStruct((2, P_SIZE, COLS), jnp.bfloat16)
+    fb, gbuf = pl.pallas_call(
+        rest_kernel,
+        out_shape=(fb_shape, gbuf_shape),
+        in_specs=[smem_spec()] + [vmem_spec()] * 6 + [any_spec()] * 6,
+        out_specs=(vmem_spec(), vmem_spec()),
+        scratch_shapes=[
+            pltpu.VMEM((20 * SHARD, 2 * TILE), jnp.float32),
+            pltpu.SemaphoreType.DMA((12,)),
+        ],
         input_output_aliases={2: 0},
         compiler_params=pltpu.CompilerParams(vmem_limit_bytes=24 << 20),
-        cost_estimate=pl.CostEstimate(flops=3 << 30, transcendentals=0, bytes_accessed=8 << 20),
-        name="swap",
-    )(state, abuf, fb, swap)
+        cost_estimate=pl.CostEstimate(flops=5 << 30, transcendentals=0, bytes_accessed=8 << 20),
+        name="rest",
+    )(
+        state, abuf, fb, swap, g_far_a, g_far_b, swap_far,
+        own, near, after, before, near_after, near_before,
+    )
 
     block = jax.ShapeDtypeStruct((N_CHIPS, 8, P_SIZE), jnp.bfloat16)
     _, keep, send = pl.pallas_call(
         finish_kernel,
-        out_shape=(fb_shape, block, block),
-        in_specs=[smem_spec()] + [vmem_spec()] * 5 + [any_spec()] * 8,
+        out_shape=(gbuf_shape, block, block),
+        in_specs=[smem_spec(), vmem_spec(), vmem_spec(), any_spec(), any_spec()],
         out_specs=(vmem_spec(),) * 3,
         scratch_shapes=[
-            pltpu.VMEM((2, P_SIZE, COLS), jnp.bfloat16),
-            pltpu.VMEM((8 * SHARD, 2 * TILE), jnp.float32),
             pltpu.VMEM((2 * P_SIZE, P_SIZE), jnp.float32),
-            pltpu.SemaphoreType.DMA((16,)),
+            pltpu.SemaphoreType.DMA((4,)),
         ],
         input_output_aliases={2: 0},
         compiler_params=pltpu.CompilerParams(vmem_limit_bytes=32 << 20),
-        cost_estimate=pl.CostEstimate(flops=6 << 30, transcendentals=0, bytes_accessed=8 << 20),
+        cost_estimate=pl.CostEstimate(flops=4 << 30, transcendentals=0, bytes_accessed=8 << 20),
         name="finish",
-    )(
-        state, abuf, fb, g_far_a, g_far_b, swap_far,
-        own, near, after, before, near_after, near_before, far_a, far_b,
-    )
+    )(state, fb, gbuf, far_a, far_b)
     taken = lax.ppermute(send, "core", SWAP)
     summed = (keep.astype(jnp.float32) + taken.astype(jnp.float32)).astype(jnp.bfloat16)
     parts = lax.all_to_all(summed, CHIPS, 0, 0)

time: 97.2 us -> 90.2 us (0.928)
  waiting for transfers between devices: 20.4 us -> 11.7 us
  starting transfers between devices: 29.1 us -> 33.3 us
  local copies, waits for them, and re-layouts: 5.39 us -> 1.94 us
  blocking collectives: 21.6 us -> 20.5 us
    ppermute x1, starting transfers between devices: 6.94 us -> 1.57 us  [body(): beside = lax.ppermute(lines, 'xl', SWAP)]
    ppermute x1, starting transfers between devices: 7.84 us -> 2.86 us  [body(): g_before = lax.ppermute(g_own, 'y', ring(-1))]
    ppermute x1, starting transfers between devices: 1.57 us -> 6.37 us  [body(): before = lax.ppermute(own, 'z', ring(-1))]
    ppermute x1, waiting for transfers between devices: 4.26 us -> 0.01 us  [body(): near = lax.ppermute(own, 'xh', SWAP)]
    ppermute x1, waiting for transfers between devices: 3.77 us -> 0.01 us  [body(): g_far_b = lax.ppermute(g_before[1], 'y', ring(-1))]
    unnamed x4 -> x0, local copies, waits for them, and re-layouts: 3.39 us -> none
    ppermute x1, waiting for transfers between devices: 0.01 us -> 3.36 us  [body(): beside = lax.ppermute(lines, 'xl', SWAP)]
    ppermute x1, starting transfers between devices: 0.47 us -> 3.29 us  [body(): g_far_b = lax.ppermute(g_before[1], 'y', ring(-1))]
  transfers between devices with their start and end apart: 17 -> 17, of which waited for: 9 -> 5; matrix products, arithmetic and copies ran while one was open for 3% -> 5% of each run, Pallas kernels for 7% -> 13%
where the time goes in v4:
time: 90.2 us; the launch traced here: 89.9 us
  starting transfers between devices  33.3 us (37%)
  blocking collectives  20.5 us (23%)
  Pallas kernels  19.2 us (21%)
  waiting for transfers between devices  11.7 us (13%)
  other arithmetic  3.12 us (3%)
  local copies, waits for them, and re-layouts  1.94 us (2%)
    all_to_all x1, blocking collectives, body(): parts = lax.all_to_all(summed, CHIPS, 0, 0)  20.5 us
    ppermute x1, starting transfers between devices, body(): before = lax.ppermute(own, 'z', ring(-1))  6.37 us
    pallas_call x1, Pallas kernels, body(): pl.pallas_call(finish_kernel, out_shape=(gbuf_shape, block, block), in_sp...  5.97 us
    ppermute x1, starting transfers between devices, body(): near = lax.ppermute(own, 'xh', SWAP)  5.47 us
    pallas_call x1, Pallas kernels, body(): pl.pallas_call(rest_kernel, out_shape=(fb_shape, gbuf_shape), in_specs=[s...  5.4 us
    ppermute x1, waiting for transfers between devices, body(): beside = lax.ppermute(lines, 'xl', SWAP)  3.36 us
    pallas_call x1, Pallas kernels, body(): pl.pallas_call(near_kernel, out_shape=fb_shape, in_specs=[smem_spec()] +...  3.31 us
    ppermute x1, starting transfers between devices, body(): g_far_b = lax.ppermute(g_before[1], 'y', ring(-1))  3.29 us
  transfers between devices with their start and end apart: 17, of which 5 were waited for; matrix products, arithmetic and copies ran while one was open for 5% of the time, Pallas kernels for 13%

profile of v4, /device:TPU:0, one launch (start us, length us, event | category | flops | bytes accessed | tf_op | source)
XLA Modules:
  0.0 89.9 jit_solution(12826914287559379665)
XLA Ops:
  0.0 1.6 %collective-permute-start.5 = (bf16[2,32,2048]{2,1,0:T(8,128)(2,1)}, bf16[2,32,2048]{2,1,0:T(8,128)(2,1)S(1)}, u32[]{:S(2)}, u32[]{:S(2)}) collective-permute-start(bf16[2,32,2048]{2,1,0:T(8,128)(2,1)} %bitcast.33), channel_id=1, source_target_pairs={{0,2},{2,0},{1,3},{3,1},{4,6},{6,4},{5,7},{7,5},{8,10},{10,8},{9,1... | collective-permute-start | bytes 786440 | tf_op jit(solution)/shard_map/ppermute | solution.py:332
  3.0 1.0 %dynamic-slice_bitcast_fusion.1 = (bf16[2,32,1024]{2,1,0:T(8,128)(2,1)S(1)}, bf16[2,32,1024]{2,1,0:T(8,128)(2,1)S(1)}) fusion(bf16[2,2048,32]{1,2,0:T(8,128)(2,1)} %param.5, s32[]{:T(128)S(6)} %select_n.19, s32[]{:T(128)S(6)} %select_n.20), kind=kLoop, calls=%fused_computation.8 | loop fusion | bytes 524296 | tf_op jit(solution)/shard_map/dynamic_slice | solution.py:328
  4.7 3.4 %collective-permute-done.5 = bf16[2,32,2048]{2,1,0:T(8,128)(2,1)S(1)} collective-permute-done((bf16[2,32,2048]{2,1,0:T(8,128)(2,1)}, bf16[2,32,2048]{2,1,0:T(8,128)(2,1)S(1)}, u32[]{:S(2)}, u32[]{:S(2)}) %collective-permute-start.5) | collective-permute-done | bytes 262176 | tf_op jit(solution)/shard_map/ppermute | solution.py:332
  8.1 1.0 %fusion.8 = (bf16[1,2,2,32,2048]{4,3,2,1,0:T(8,128)(2,1)S(1)}, bf16[2,2,32,2048]{3,2,1,0:T(8,128)(2,1)S(1)}) fusion(bf16[1,2,32,2048]{3,2,1,0:T(8,128)(2,1)S(1)} %bitcast.35, bf16[1,2,32,2048]{3,2,1,0:T(8,128)(2,1)} %bitcast.34), kind=kLoop, calls=%fused_computation.28 | loop fusion | flops 262144 | bytes 1572864 | tf_op jit(solution)/shard_map/stack | solution.py:356
  9.1 1.9 %collective-permute-start.6 = (bf16[2,2,32,2048]{3,2,1,0:T(8,128)(2,1)S(1)}, bf16[2,2,32,2048]{3,2,1,0:T(8,128)(2,1)S(1)}, u32[]{:S(2)}, u32[]{:S(2)}) collective-permute-start(bf16[2,2,32,2048]{3,2,1,0:T(8,128)(2,1)S(1)} %get-tuple-element.45.own), channel_id=1, source_target_pairs={{0,4},{4,8},{8,12},{12,0},{1,5},{5,9},{9,13},{13,1},{2,6},{6,10},{... | collective-permute-start | bytes 1572872 | tf_op jit(solution)/shard_map/ppermute | solution.py:336
  11.0 2.9 %collective-permute-start.7 = (bf16[2,2,32,2048]{3,2,1,0:T(8,128)(2,1)S(1)}, bf16[2,2,32,2048]{3,2,1,0:T(8,128)(2,1)S(1)}, u32[]{:S(2)}, u32[]{:S(2)}) collective-permute-start(bf16[2,2,32,2048]{3,2,1,0:T(8,128)(2,1)S(1)} %get-tuple-element.45.own), channel_id=1, source_target_pairs={{0,12},{4,0},{8,4},{12,8},{1,13},{5,1},{9,5},{13,9},{2,14},{6,2},{... | collective-permute-start | bytes 1572872 | tf_op jit(solution)/shard_map/ppermute | solution.py:337
  13.9 5.5 %collective-permute-start.2 = (bf16[2,2,32,1024]{3,2,1,0:T(8,128)(2,1)S(1)}, bf16[2,2,32,1024]{3,2,1,0:T(8,128)(2,1)S(1)}, u32[]{:S(2)}, u32[]{:S(2)}) collective-permute-start(bf16[2,2,32,1024]{3,2,1,0:T(8,128)(2,1)S(1)} %pad_maximum_fusion.3.own), channel_id=1, source_target_pairs={{0,64},{64,0},{1,65},{65,1},{2,66},{66,2},{3,67},{67,3},{4,68},{68... | collective-permute-start | bytes 786440 | tf_op jit(solution)/shard_map/ppermute | solution.py:340
  19.4 3.2 %collective-permute-start.3 = (bf16[2,2,32,1024]{3,2,1,0:T(8,128)(2,1)S(1)}, bf16[2,2,32,1024]{3,2,1,0:T(8,128)(2,1)S(1)}, u32[]{:S(2)}, u32[]{:S(2)}) collective-permute-start(bf16[2,2,32,1024]{3,2,1,0:T(8,128)(2,1)S(1)} %pad_maximum_fusion.3.own), channel_id=1, source_target_pairs={{0,16},{16,32},{32,48},{48,0},{1,17},{17,33},{33,49},{49,1},{2,18}... | collective-permute-start | bytes 786440 | tf_op jit(solution)/shard_map/ppermute | solution.py:338
  22.6 6.4 %collective-permute-start.4 = (bf16[2,2,32,1024]{3,2,1,0:T(8,128)(2,1)S(1)}, bf16[2,2,32,1024]{3,2,1,0:T(8,128)(2,1)S(1)}, u32[]{:S(2)}, u32[]{:S(2)}) collective-permute-start(bf16[2,2,32,1024]{3,2,1,0:T(8,128)(2,1)S(1)} %pad_maximum_fusion.3.own), channel_id=1, source_target_pairs={{0,48},{16,0},{32,16},{48,32},{1,49},{17,1},{33,17},{49,33},{2,50}... | collective-permute-start | bytes 786440 | tf_op jit(solution)/shard_map/ppermute | solution.py:339
  30.2 2.7 %load.1.abuf = bf16[4,2,2304,256]{3,2,1,0:T(8,128)(2,1)S(1)} custom-call(s32[54]{0:T(128)S(1)} %concatenate.3.st, bf16[2,2048,1024]{2,1,0:T(8,128)(2,1)} %a.1), custom_call_target="tpu_custom_call" | custom-call | bytes 8388608 | tf_op jit(solution)/shard_map/load/pallas_call | solution.py:343
  32.9 2.3 %collective-permute-done.3.after = bf16[2,2,32,1024]{3,2,1,0:T(8,128)(2,1)S(1)} collective-permute-done((bf16[2,2,32,1024]{3,2,1,0:T(8,128)(2,1)S(1)}, bf16[2,2,32,1024]{3,2,1,0:T(8,128)(2,1)S(1)}, u32[]{:S(2)}, u32[]{:S(2)}) %collective-permute-start.3) | collective-permute-done | bytes 262176 | tf_op jit(solution)/shard_map/ppermute | solution.py:338
  35.2 1.1 %collective-permute-start.10 = (bf16[2,2,32,1024]{3,2,1,0:T(8,128)(2,1)S(1)}, bf16[2,2,32,1024]{3,2,1,0:T(8,128)(2,1)S(1)}, u32[]{:S(2)}, u32[]{:S(2)}) collective-permute-start(bf16[2,2,32,1024]{3,2,1,0:T(8,128)(2,1)S(1)} %collective-permute-done.2.near), channel_id=1, source_target_pairs={{0,16},{16,32},{32,48},{48,0},{1,17},{17,33},{33,49},{49,1},{2,18}... | collective-permute-start | bytes 786440 | tf_op jit(solution)/shard_map/ppermute | solution.py:359
  36.4 2.1 %collective-permute-start.11 = (bf16[2,2,32,1024]{3,2,1,0:T(8,128)(2,1)S(1)}, bf16[2,2,32,1024]{3,2,1,0:T(8,128)(2,1)S(1)}, u32[]{:S(2)}, u32[]{:S(2)}) collective-permute-start(bf16[2,2,32,1024]{3,2,1,0:T(8,128)(2,1)S(1)} %collective-permute-done.2.near), channel_id=1, source_target_pairs={{0,48},{16,0},{32,16},{48,32},{1,49},{17,1},{33,17},{49,33},{2,50}... | collective-permute-start | bytes 786440 | tf_op jit(solution)/shard_map/ppermute | solution.py:360
  38.9 3.3 %collective-permute-start.9 = (bf16[2,32,2048]{2,1,0:T(8,128)(2,1)S(1)}, bf16[2,32,2048]{2,1,0:T(8,128)(2,1)S(1)}, u32[]{:S(2)}, u32[]{:S(2)}) collective-permute-start(bf16[2,32,2048]{2,1,0:T(8,128)(2,1)S(1)} %slice_bitcast_fusion), channel_id=1, source_target_pairs={{0,12},{4,0},{8,4},{12,8},{1,13},{5,1},{9,5},{13,9},{2,14},{6,2},{... | collective-permute-start | bytes 786440 | tf_op jit(solution)/shard_map/ppermute | solution.py:358
  42.2 3.3 %near.1.fb_in = bf16[4,512,1024]{2,1,0:T(8,128)(2,1)S(1)} custom-call(s32[54]{0:T(128)S(1)} %concatenate.3.st, bf16[4,2,2304,256]{3,2,1,0:T(8,128)(2,1)S(1)} %load.1.abuf, bf16[2,2,32,2048]{3,2,1,0:T(8,128)(2,1)S(1)} %get-tuple-element.45.own, bf16[2,2,32,2048]{3,2,1,0:T(8,128)(2,1)S(1)} %collective-permute-done.6.after, ...), custom_call_target="tpu_custom_call" | custom-call | flops 3221225472 | bytes 8388608 | tf_op jit(solution)/shard_map/near/pallas_call | solution.py:362
  45.5 3.2 %collective-permute-done.8.g_far_a = bf16[2,32,2048]{2,1,0:T(8,128)(2,1)S(1)} collective-permute-done((bf16[2,32,2048]{2,1,0:T(8,128)(2,1)S(1)}, bf16[2,32,2048]{2,1,0:T(8,128)(2,1)S(1)}, u32[]{:S(2)}, u32[]{:S(2)}) %collective-permute-start.8) | collective-permute-done | bytes 262176 | tf_op jit(solution)/shard_map/ppermute | solution.py:357
  49.0 3.2 %collective-permute-start.15 = (bf16[2,2,32,1024]{3,2,1,0:T(8,128)(2,1)S(1)}, bf16[2,2,32,1024]{3,2,1,0:T(8,128)(2,1)S(1)}, u32[]{:S(2)}, u32[]{:S(2)}) collective-permute-start(bf16[2,2,32,1024]{3,2,1,0:T(8,128)(2,1)S(1)} %collective-permute-done.11.near_before), channel_id=1, source_target_pairs={{0,48},{16,0},{32,16},{48,32},{1,49},{17,1},{33,17},{49,33},{2,50}... | collective-permute-start | bytes 786440 | tf_op jit(solution)/shard_map/ppermute | solution.py:377
  52.2 5.4 %rest.1 = (bf16[4,512,1024]{2,1,0:T(8,128)(2,1)S(1)}, bf16[2,512,1024]{2,1,0:T(8,128)(2,1)S(1)}) custom-call(s32[54]{0:T(128)S(1)} %concatenate.3.st, bf16[4,2,2304,256]{3,2,1,0:T(8,128)(2,1)S(1)} %load.1.abuf, bf16[4,512,1024]{2,1,0:T(8,128)(2,1)S(1)} %near.1.fb_in, ...), custom_call_target="tpu_custom_call", output_to_operand_aliasing={{0}: (2, {})} | custom-call | flops 5368709120 | bytes 8388608 | tf_op jit(solution)/shard_map/rest/pallas_call | solution.py:379
  57.6 1.2 %collective-permute-done.14.far_a = bf16[2,2,32,1024]{3,2,1,0:T(8,128)(2,1)S(1)} collective-permute-done((bf16[2,2,32,1024]{3,2,1,0:T(8,128)(2,1)S(1)}, bf16[2,2,32,1024]{3,2,1,0:T(8,128)(2,1)S(1)}, u32[]{:S(2)}, u32[]{:S(2)}) %collective-permute-start.14) | collective-permute-done | bytes 262176 | tf_op jit(solution)/shard_map/ppermute | solution.py:361
  58.8 6.0 %finish.1 = (bf16[2,512,1024]{2,1,0:T(8,128)(2,1)S(1)}, bf16[64,8,512]{2,1,0:T(8,128)(2,1)S(1)}, bf16[64,8,512]{2,1,0:T(8,128)(2,1)S(1)}) custom-call(s32[54]{0:T(128)S(1)} %concatenate.3.st, bf16[4,512,1024]{2,1,0:T(8,128)(2,1)S(1)} %get-tuple-element.33.fb, bf16[2,512,1024]{2,1,0:T(8,128)(2,1)S(1)} %get-tuple-element.34.gbuf_in, ...), custom_call_target="tpu_custom_call", output_to_operand_aliasing={{0}: (2, {})} | custom-call | flops 4294967296 | bytes 8388608 | tf_op jit(solution)/shard_map/finish/pallas_call | solution.py:398
  64.8 1.1 %collective-permute-start.16 = (bf16[64,8,512]{2,1,0:T(8,128)(2,1)S(1)}, bf16[64,8,512]{2,1,0:T(8,128)(2,1)S(1)}, u32[]{:S(2)}, u32[]{:S(2)}) collective-permute-start(bf16[64,8,512]{2,1,0:T(8,128)(2,1)S(1)} %get-tuple-element.36), channel_id=1, source_target_pairs={{0,1},{1,0},{2,3},{3,2},{4,5},{5,4},{6,7},{7,6},{8,9},{9,8},{10,11... | collective-permute-start | bytes 1572872 | tf_op jit(solution)/shard_map/ppermute | solution.py:412
  65.9 1.5 %collective-permute-done.16 = bf16[64,8,512]{2,1,0:T(8,128)(2,1)S(1)} collective-permute-done((bf16[64,8,512]{2,1,0:T(8,128)(2,1)S(1)}, bf16[64,8,512]{2,1,0:T(8,128)(2,1)S(1)}, u32[]{:S(2)}, u32[]{:S(2)}) %collective-permute-start.16) | collective-permute-done | bytes 524320 | tf_op jit(solution)/shard_map/ppermute | solution.py:412
  67.6 20.5 %all_to_all.5.parts = bf16[64,8,512]{2,1,0:T(8,128)(2,1)} all-to-all(bf16[64,8,512]{2,1,0:T(8,128)(2,1)S(1)} %add_convert_fusion), channel_id=1, replica_groups=mesh['xh'=2,'z'=4,'y'=4,'xl'=2,'core'=2] {'xh','z','y','xl'}, dimensions={0} | all-to-all | bytes 1048576 | tf_op jit(solution)/shard_map/all_to_all | solution.py:414
  88.1 1.8 %align.1 = f32[4,2,512]{2,1,0:T(2,128)} custom-call(s32[4]{0:T(128)} %index.1, bf16[64,8,512]{2,1,0:T(8,128)(2,1)} %all_to_all.5.parts), custom_call_target="tpu_custom_call" | custom-call | tf_op jit(solution)/shard_map/align/pallas_call | solution.py:415
  (36 shorter events, 4.2 us)
Async XLA Ops:
  0.0 8.1 %collective-permute-start.5 = (bf16[2,32,2048]{2,1,0:T(8,128)(2,1)}, bf16[2,32,2048]{2,1,0:T(8,128)(2,1)S(1)}, u32[]{:S(2)}, u32[]{:S(2)}) collective-permute-start(bf16[2,32,2048]{2,1,0:T(8,128)(2,1)} %bitcast.33), channel_id=1, source_target_pairs={{0,2},{2,0},{1,3},{3,1},{4,6},{6,4},{5,7},{7,5},{8,10},{10,8},{9,1... | collective-permute-start | bytes 786440 | tf_op jit(solution)/shard_map/ppermute | solution.py:332
  4.0 9.9 %collective-permute-start.1 = (bf16[2,32,1024]{2,1,0:T(8,128)(2,1)S(1)}, bf16[2,32,1024]{2,1,0:T(8,128)(2,1)S(1)}, u32[]{:S(2)}, u32[]{:S(2)}) collective-permute-start(bf16[2,32,1024]{2,1,0:T(8,128)(2,1)S(1)} %get-tuple-element.47), channel_id=1, source_target_pairs={{0,1},{1,0},{2,65},{3,64},{4,17},{5,16},{6,81},{7,80},{8,33},{9,32... | collective-permute-start | bytes 393224 | tf_op jit(solution)/shard_map/ppermute | solution.py:331
  4.1 9.8 %collective-permute-start = (bf16[2,32,1024]{2,1,0:T(8,128)(2,1)S(1)}, bf16[2,32,1024]{2,1,0:T(8,128)(2,1)S(1)}, u32[]{:S(2)}, u32[]{:S(2)}) collective-permute-start(bf16[2,32,1024]{2,1,0:T(8,128)(2,1)S(1)} %get-tuple-element.46), channel_id=1, source_target_pairs={{0,0},{1,1},{2,64},{3,65},{4,16},{5,17},{6,80},{7,81},{8,32},{9,33... | collective-permute-start | bytes 393224 | tf_op jit(solution)/shard_map/ppermute | solution.py:330
  9.1 29.3 %collective-permute-start.6 = (bf16[2,2,32,2048]{3,2,1,0:T(8,128)(2,1)S(1)}, bf16[2,2,32,2048]{3,2,1,0:T(8,128)(2,1)S(1)}, u32[]{:S(2)}, u32[]{:S(2)}) collective-permute-start(bf16[2,2,32,2048]{3,2,1,0:T(8,128)(2,1)S(1)} %get-tuple-element.45.own), channel_id=1, source_target_pairs={{0,4},{4,8},{8,12},{12,0},{1,5},{5,9},{9,13},{13,1},{2,6},{6,10},{... | collective-permute-start | bytes 1572872 | tf_op jit(solution)/shard_map/ppermute | solution.py:336
  11.0 27.4 %collective-permute-start.7 = (bf16[2,2,32,2048]{3,2,1,0:T(8,128)(2,1)S(1)}, bf16[2,2,32,2048]{3,2,1,0:T(8,128)(2,1)S(1)}, u32[]{:S(2)}, u32[]{:S(2)}) collective-permute-start(bf16[2,2,32,2048]{3,2,1,0:T(8,128)(2,1)S(1)} %get-tuple-element.45.own), channel_id=1, source_target_pairs={{0,12},{4,0},{8,4},{12,8},{1,13},{5,1},{9,5},{13,9},{2,14},{6,2},{... | collective-permute-start | bytes 1572872 | tf_op jit(solution)/shard_map/ppermute | solution.py:337
  13.9 19.0 %collective-permute-start.2 = (bf16[2,2,32,1024]{3,2,1,0:T(8,128)(2,1)S(1)}, bf16[2,2,32,1024]{3,2,1,0:T(8,128)(2,1)S(1)}, u32[]{:S(2)}, u32[]{:S(2)}) collective-permute-start(bf16[2,2,32,1024]{3,2,1,0:T(8,128)(2,1)S(1)} %pad_maximum_fusion.3.own), channel_id=1, source_target_pairs={{0,64},{64,0},{1,65},{65,1},{2,66},{66,2},{3,67},{67,3},{4,68},{68... | collective-permute-start | bytes 786440 | tf_op jit(solution)/shard_map/ppermute | solution.py:340
  19.4 15.8 %collective-permute-start.3 = (bf16[2,2,32,1024]{3,2,1,0:T(8,128)(2,1)S(1)}, bf16[2,2,32,1024]{3,2,1,0:T(8,128)(2,1)S(1)}, u32[]{:S(2)}, u32[]{:S(2)}) collective-permute-start(bf16[2,2,32,1024]{3,2,1,0:T(8,128)(2,1)S(1)} %pad_maximum_fusion.3.own), channel_id=1, source_target_pairs={{0,16},{16,32},{32,48},{48,0},{1,17},{17,33},{33,49},{49,1},{2,18}... | collective-permute-start | bytes 786440 | tf_op jit(solution)/shard_map/ppermute | solution.py:338
  22.6 12.6 %collective-permute-start.4 = (bf16[2,2,32,1024]{3,2,1,0:T(8,128)(2,1)S(1)}, bf16[2,2,32,1024]{3,2,1,0:T(8,128)(2,1)S(1)}, u32[]{:S(2)}, u32[]{:S(2)}) collective-permute-start(bf16[2,2,32,1024]{3,2,1,0:T(8,128)(2,1)S(1)} %pad_maximum_fusion.3.own), channel_id=1, source_target_pairs={{0,48},{16,0},{32,16},{48,32},{1,49},{17,1},{33,17},{49,33},{2,50}... | collective-permute-start | bytes 786440 | tf_op jit(solution)/shard_map/ppermute | solution.py:339
  35.2 10.3 %collective-permute-start.10 = (bf16[2,2,32,1024]{3,2,1,0:T(8,128)(2,1)S(1)}, bf16[2,2,32,1024]{3,2,1,0:T(8,128)(2,1)S(1)}, u32[]{:S(2)}, u32[]{:S(2)}) collective-permute-start(bf16[2,2,32,1024]{3,2,1,0:T(8,128)(2,1)S(1)} %collective-permute-done.2.near), channel_id=1, source_target_pairs={{0,16},{16,32},{32,48},{48,0},{1,17},{17,33},{33,49},{49,1},{2,18}... | collective-permute-start | bytes 786440 | tf_op jit(solution)/shard_map/ppermute | solution.py:359
  36.4 9.1 %collective-permute-start.11 = (bf16[2,2,32,1024]{3,2,1,0:T(8,128)(2,1)S(1)}, bf16[2,2,32,1024]{3,2,1,0:T(8,128)(2,1)S(1)}, u32[]{:S(2)}, u32[]{:S(2)}) collective-permute-start(bf16[2,2,32,1024]{3,2,1,0:T(8,128)(2,1)S(1)} %collective-permute-done.2.near), channel_id=1, source_target_pairs={{0,48},{16,0},{32,16},{48,32},{1,49},{17,1},{33,17},{49,33},{2,50}... | collective-permute-start | bytes 786440 | tf_op jit(solution)/shard_map/ppermute | solution.py:360
  38.6 13.6 %collective-permute-start.12 = (bf16[3,2,2,32,2048]{4,3,2,1,0:T(8,128)(2,1)S(1)}, bf16[3,2,2,32,2048]{4,3,2,1,0:T(8,128)(2,1)S(1)}, u32[]{:S(2)}, u32[]{:S(2)}) collective-permute-start(bf16[3,2,2,32,2048]{4,3,2,1,0:T(8,128)(2,1)S(1)} %pad_maximum_fusion), channel_id=1, source_target_pairs={{0,1},{1,0},{2,3},{3,2},{4,5},{5,4},{6,7},{7,6},{8,9},{9,8},{10,11... | collective-permute-start | bytes 4718600 | tf_op jit(solution)/shard_map/ppermute | solution.py:356
  38.8 10.0 %collective-permute-start.8 = (bf16[2,32,2048]{2,1,0:T(8,128)(2,1)S(1)}, bf16[2,32,2048]{2,1,0:T(8,128)(2,1)S(1)}, u32[]{:S(2)}, u32[]{:S(2)}) collective-permute-start(bf16[2,32,2048]{2,1,0:T(8,128)(2,1)S(1)} %slice_bitcast_fusion.1), channel_id=1, source_target_pairs={{0,4},{4,8},{8,12},{12,0},{1,5},{5,9},{9,13},{13,1},{2,6},{6,10},{... | collective-permute-start | bytes 786440 | tf_op jit(solution)/shard_map/ppermute | solution.py:357
  38.9 9.9 %collective-permute-start.9 = (bf16[2,32,2048]{2,1,0:T(8,128)(2,1)S(1)}, bf16[2,32,2048]{2,1,0:T(8,128)(2,1)S(1)}, u32[]{:S(2)}, u32[]{:S(2)}) collective-permute-start(bf16[2,32,2048]{2,1,0:T(8,128)(2,1)S(1)} %slice_bitcast_fusion), channel_id=1, source_target_pairs={{0,12},{4,0},{8,4},{12,8},{1,13},{5,1},{9,5},{13,9},{2,14},{6,2},{... | collective-permute-start | bytes 786440 | tf_op jit(solution)/shard_map/ppermute | solution.py:358
  48.8 3.4 %collective-permute-start.13 = (bf16[2,2,32,2048]{3,2,1,0:T(8,128)(2,1)S(1)}, bf16[2,2,32,2048]{3,2,1,0:T(8,128)(2,1)S(1)}, u32[]{:S(2)}, u32[]{:S(2)}) collective-permute-start(bf16[2,2,32,2048]{3,2,1,0:T(8,128)(2,1)S(1)} %pad_maximum_fusion.2), channel_id=1, source_target_pairs={{0,1},{1,0},{2,3},{3,2},{4,5},{5,4},{6,7},{7,6},{8,9},{9,8},{10,11... | collective-permute-start | bytes 1572872 | tf_op jit(solution)/shard_map/ppermute | solution.py:376
  48.9 9.9 %collective-permute-start.14 = (bf16[2,2,32,1024]{3,2,1,0:T(8,128)(2,1)S(1)}, bf16[2,2,32,1024]{3,2,1,0:T(8,128)(2,1)S(1)}, u32[]{:S(2)}, u32[]{:S(2)}) collective-permute-start(bf16[2,2,32,1024]{3,2,1,0:T(8,128)(2,1)S(1)} %collective-permute-done.3.after), channel_id=1, source_target_pairs={{0,16},{16,32},{32,48},{48,0},{1,17},{17,33},{33,49},{49,1},{2,18}... | collective-permute-start | bytes 786440 | tf_op jit(solution)/shard_map/ppermute | solution.py:361
  49.0 9.9 %collective-permute-start.15 = (bf16[2,2,32,1024]{3,2,1,0:T(8,128)(2,1)S(1)}, bf16[2,2,32,1024]{3,2,1,0:T(8,128)(2,1)S(1)}, u32[]{:S(2)}, u32[]{:S(2)}) collective-permute-start(bf16[2,2,32,1024]{3,2,1,0:T(8,128)(2,1)S(1)} %collective-permute-done.11.near_before), channel_id=1, source_target_pairs={{0,48},{16,0},{32,16},{48,32},{1,49},{17,1},{33,17},{49,33},{2,50}... | collective-permute-start | bytes 786440 | tf_op jit(solution)/shard_map/ppermute | solution.py:377
  64.8 2.7 %collective-permute-start.16 = (bf16[64,8,512]{2,1,0:T(8,128)(2,1)S(1)}, bf16[64,8,512]{2,1,0:T(8,128)(2,1)S(1)}, u32[]{:S(2)}, u32[]{:S(2)}) collective-permute-start(bf16[64,8,512]{2,1,0:T(8,128)(2,1)S(1)} %get-tuple-element.36), channel_id=1, source_target_pairs={{0,1},{1,0},{2,3},{3,2},{4,5},{5,4},{6,7},{7,6},{8,9},{9,8},{10,11... | collective-permute-start | bytes 1572872 | tf_op jit(solution)/shard_map/ppermute | solution.py:412

commit v5 on v4

--- a/solution.py
+++ b/solution.py
@@ -73,65 +73,77 @@
     visit(lambda copy: copy.wait())
 
 
-def project(st, abuf, acc, fb, left_of, targets):
+BLOCK = 2 * SHARD
+
+
+def accumulators(blocks):
+    return [pltpu.ACC(unit)((BLOCK, TILE), jnp.float32) for unit in range(2) for _ in range(blocks)]
+
+
+def project(st, abuf, accs, saved, fb, left_of, targets):
+    blocks = len(targets)
+
+    def push(c, i):
+        rows = pl.ds(pl.multiple_of(i * TILE, TILE), TILE)
+        for unit in range(2):
+            pltpu.matmul_push_rhs(abuf[c, unit, rows, :], 0, unit)
+
+    def stream(t, after_first=None):
+        left = left_of(t)
+        for b in range(blocks):
+            for unit in range(2):
+                pltpu.matmul_acc_lhs(
+                    accs[unit * blocks + b],
+                    left[b * BLOCK : (b + 1) * BLOCK],
+                    load_staged_rhs=0 if b == 0 else None,
+                )
+            if b == 0 and after_first:
+                after_first()
+
     def column(c, carry):
         n = st[c]
+        on_diag = st[40 + c] != 0
         lanes = pl.ds(pl.multiple_of(c * TILE, TILE), TILE)
 
-        def product(tiles, start):
-            left = jnp.concatenate([left_of(t) for t in tiles], axis=1)
-            rows = pl.ds(pl.multiple_of(start * TILE, TILE), len(tiles) * TILE)
-            right = jnp.concatenate([abuf[c, 0, rows, :], abuf[c, 1, rows, :]], axis=1)
-            return dot(left, right)
-
-        def listed(first, count):
-            return [st[8 + c * ROW_TILES + first + i] for i in range(count)]
-
-        @pl.when(n < 4)
+        def popped(b):
+            by_real = pltpu.matmul_pop(accs[b])
+            by_imag = pltpu.matmul_pop(accs[blocks + b])
+            return by_real[:SHARD], by_imag[:SHARD], by_real[SHARD:], by_imag[SHARD:]
+
+        @pl.when(n > 0)
         def _():
-            acc[...] = jnp.zeros_like(acc)
-
-        @pl.when(n >= 4)
+            push(c, 0)
+
+            def step(i, inner):
+                stream(st[8 + c * ROW_TILES + i], lambda: push(c, i + 1))
+                return inner
+
+            lax.fori_loop(0, n - 1, step, 0)
+            stream(st[8 + c * ROW_TILES + n - 1])
+
+        for b, row in enumerate(targets):
+            rows = pl.ds(pl.multiple_of(row, SHARD), SHARD)
+            rr, ri, ir, ii = popped(b)
+            fb[0, rows, lanes] = (rr + ii).astype(jnp.bfloat16)
+            fb[1, rows, lanes] = (ri - ir).astype(jnp.bfloat16)
+            fb[2, rows, lanes] = (rr - ii).astype(jnp.bfloat16)
+            fb[3, rows, lanes] = (ri + ir).astype(jnp.bfloat16)
+
+            @pl.when(on_diag)
+            def _():
+                saved[0, b * SHARD : (b + 1) * SHARD, :] = rr + ii
+                saved[1, b * SHARD : (b + 1) * SHARD, :] = ri - ir
+
+        @pl.when(on_diag)
         def _():
-            acc[...] = product(listed(0, 4), 0)
-
-        @pl.when(n == 8)
-        def _():
-            acc[...] += product(listed(4, 4), 4)
-
-        @pl.when((n & 2) != 0)
-        def _():
-            first = n & 4
-            acc[...] += product(listed(first, 2), first)
-
-        @pl.when((n & 1) != 0)
-        def _():
-            acc[...] += product(listed(n - 1, 1), n - 1)
-
-        def store(front, back):
+            push(c, ROW_TILES)
+            stream(st[44 + c])
             for b, row in enumerate(targets):
                 rows = pl.ds(pl.multiple_of(row, SHARD), SHARD)
-                at = 2 * SHARD * b
-                rr = acc[at : at + SHARD, :TILE]
-                ri = acc[at : at + SHARD, TILE:]
-                ir = acc[at + SHARD : at + 2 * SHARD, :TILE]
-                ii = acc[at + SHARD : at + 2 * SHARD, TILE:]
-                if front:
-                    fb[0, rows, lanes] = (rr + ii).astype(jnp.bfloat16)
-                    fb[1, rows, lanes] = (ri - ir).astype(jnp.bfloat16)
-                if back:
-                    fb[2, rows, lanes] = (rr - ii).astype(jnp.bfloat16)
-                    fb[3, rows, lanes] = (ri + ir).astype(jnp.bfloat16)
-
-        @pl.when(st[40 + c] == 0)
-        def _():
-            store(True, True)
-
-        @pl.when(st[40 + c] != 0)
-        def _():
-            store(False, True)
-            acc[...] += product([st[44 + c]], ROW_TILES)
-            store(True, False)
+                rr, ri, ir, ii = popped(b)
+                at = slice(b * SHARD, (b + 1) * SHARD)
+                fb[0, rows, lanes] = (saved[0, at, :] + (rr + ii)).astype(jnp.bfloat16)
+                fb[1, rows, lanes] = (saved[1, at, :] + (ri - ir)).astype(jnp.bfloat16)
 
         return carry
 
@@ -148,7 +160,7 @@
     return pl.ds(pl.multiple_of(t * TILE, TILE), TILE)
 
 
-def near_kernel(st, abuf, own, after, before, fb, acc):
+def near_kernel(st, abuf, own, after, before, fb, saved):
     @pl.when(st[48] != 0)
     def _():
         def left_of(t):
@@ -157,7 +169,9 @@
             )
 
         targets = [line_row(st, x, step, False) for step in (0, -1, 1) for x in range(2)]
-        project(st, abuf, acc, fb, left_of, targets)
+        pl.run_scoped(
+            lambda *accs: project(st, abuf, accs, saved, fb, left_of, targets), *accumulators(len(targets))
+        )
 
 
 def row_copies(st, gbuf, sem, pieces):
@@ -176,7 +190,7 @@
 def rest_kernel(
     st, abuf, fb_in, swap, g_far_a, g_far_b, swap_far,
     own, near, after, before, near_after, near_before,
-    fb, gbuf, acc, gsem,
+    fb, gbuf, saved, gsem,
 ):
     @pl.when(st[48] != 0)
     def _():
@@ -210,15 +224,19 @@
 
         targets = [line_row(st, x, step, True) for step in (0, -1, 1) for x in range(2)]
         targets += [line_row(st, x, 2, other) for other in (False, True) for x in range(2)]
-        project(st, abuf, acc, fb, left_of, targets)
+        pl.run_scoped(
+            lambda *accs: project(st, abuf, accs, saved, fb, left_of, targets), *accumulators(len(targets))
+        )
         for copy in copies:
             copy.wait()
 
 
-def finish_kernel(st, fb, gbuf_in, far_a, far_b, gbuf, keep, send, wide, gsem):
+def finish_kernel(st, fb, gbuf_in, far_a, far_b, gbuf, keep, send, gsem):
     core = st[49]
-    sub = lax.broadcasted_iota(jnp.int32, (N_CHIPS, 8, P_SIZE), 1)
-    low = sub < 4
+    half = P_SIZE
+    blocks = 2 * half // BLOCK
+    chips = BLOCK // 8
+    low = lax.broadcasted_iota(jnp.int32, (chips, 8, TILE), 1) < 4
 
     @pl.when(st[48] != 0)
     def _():
@@ -227,38 +245,59 @@
             copy.start()
         for copy in copies:
             copy.wait()
+
+        steps = []
         for c in range(COL_TILES):
             cols = slice(c * TILE, (c + 1) * TILE)
-            gr = gbuf[0, :, cols]
-            gi = gbuf[1, :, cols]
-            fr = fb[0, :, cols]
-            fi = fb[1, :, cols]
-            left = jnp.concatenate(
-                [
-                    jnp.concatenate([fr, -fi, gr, gi], axis=1),
-                    jnp.concatenate([fi, fr, -gi, gr], axis=1),
-                ],
-                axis=0,
-            )
-            right = jnp.concatenate([gr, gi, fb[2, :, cols], fb[3, :, cols]], axis=1)
-            if c == 0:
-                wide[...] = dot_nt(left, right)
-            else:
-                wide[...] += dot_nt(left, right)
-        re = wide[:P_SIZE].reshape(N_CHIPS, 8, P_SIZE)
-        im = wide[P_SIZE:].reshape(N_CHIPS, 8, P_SIZE)
-        first = jnp.where(low, re, pltpu.roll(im, 4, 1)).astype(jnp.bfloat16)
-        second = jnp.where(low, pltpu.roll(re, 4, 1), im).astype(jnp.bfloat16)
-
-        @pl.when(core == 0)
-        def _():
-            keep[...] = first
-            send[...] = second
-
-        @pl.when(core != 0)
-        def _():
-            keep[...] = second
-            send[...] = first
+            steps += [
+                (lambda cols=cols: (fb[0, :, cols], fb[1, :, cols]), (gbuf, 0, cols)),
+                (lambda cols=cols: (-fb[1, :, cols], fb[0, :, cols]), (gbuf, 1, cols)),
+                (lambda cols=cols: (gbuf[0, :, cols], -gbuf[1, :, cols]), (fb, 2, cols)),
+                (lambda cols=cols: (gbuf[1, :, cols], gbuf[0, :, cols]), (fb, 3, cols)),
+            ]
+
+        def push(step):
+            ref, slot, cols = steps[step][1]
+            for unit in range(2):
+                right = ref[slot, unit * TILE : (unit + 1) * TILE, cols]
+                pltpu.matmul_push_rhs(right, 0, unit, transpose=True)
+
+        def multiply(*accs):
+            push(0)
+            for step in range(len(steps)):
+                top, bottom = steps[step][0]()
+                for b in range(blocks):
+                    source = top if b < blocks // 2 else bottom
+                    at = (b % (blocks // 2)) * BLOCK
+                    for unit in range(2):
+                        pltpu.matmul_acc_lhs(
+                            accs[unit * blocks + b],
+                            source[at : at + BLOCK],
+                            load_staged_rhs=0 if b == 0 else None,
+                        )
+                    if b == 0 and step + 1 < len(steps):
+                        push(step + 1)
+
+            for b in range(blocks // 2):
+                for unit in range(2):
+                    re = pltpu.matmul_pop(accs[unit * blocks + b]).reshape(chips, 8, TILE)
+                    im = pltpu.matmul_pop(accs[unit * blocks + blocks // 2 + b]).reshape(chips, 8, TILE)
+                    first = jnp.where(low, re, pltpu.roll(im, 4, 1)).astype(jnp.bfloat16)
+                    second = jnp.where(low, pltpu.roll(re, 4, 1), im).astype(jnp.bfloat16)
+                    at = slice(b * chips, (b + 1) * chips)
+                    lanes = slice(unit * TILE, (unit + 1) * TILE)
+
+                    @pl.when(core == 0)
+                    def _():
+                        keep[at, :, lanes] = first
+                        send[at, :, lanes] = second
+
+                    @pl.when(core != 0)
+                    def _():
+                        keep[at, :, lanes] = second
+                        send[at, :, lanes] = first
+
+        pl.run_scoped(multiply, *accumulators(blocks))
 
     @pl.when(st[48] == 0)
     def _():
@@ -364,7 +403,7 @@
         out_shape=fb_shape,
         in_specs=[smem_spec()] + [vmem_spec()] * 4,
         out_specs=vmem_spec(),
-        scratch_shapes=[pltpu.VMEM((12 * SHARD, 2 * TILE), jnp.float32)],
+        scratch_shapes=[pltpu.VMEM((2, 6 * SHARD, TILE), jnp.float32)],
         compiler_params=pltpu.CompilerParams(vmem_limit_bytes=24 << 20),
         cost_estimate=pl.CostEstimate(flops=3 << 30, transcendentals=0, bytes_accessed=8 << 20),
         name="near",
@@ -382,7 +421,7 @@
         in_specs=[smem_spec()] + [vmem_spec()] * 6 + [any_spec()] * 6,
         out_specs=(vmem_spec(), vmem_spec()),
         scratch_shapes=[
-            pltpu.VMEM((20 * SHARD, 2 * TILE), jnp.float32),
+            pltpu.VMEM((2, 10 * SHARD, TILE), jnp.float32),
             pltpu.SemaphoreType.DMA((12,)),
         ],
         input_output_aliases={2: 0},
@@ -400,10 +439,7 @@
         out_shape=(gbuf_shape, block, block),
         in_specs=[smem_spec(), vmem_spec(), vmem_spec(), any_spec(), any_spec()],
         out_specs=(vmem_spec(),) * 3,
-        scratch_shapes=[
-            pltpu.VMEM((2 * P_SIZE, P_SIZE), jnp.float32),
-            pltpu.SemaphoreType.DMA((4,)),
-        ],
+        scratch_shapes=[pltpu.SemaphoreType.DMA((4,))],
         input_output_aliases={2: 0},
         compiler_params=pltpu.CompilerParams(vmem_limit_bytes=32 << 20),
         cost_estimate=pl.CostEstimate(flops=4 << 30, transcendentals=0, bytes_accessed=8 << 20),

time: 90.2 us -> 90 us (level)
  waiting for transfers between devices: 11.7 us -> 14.1 us
  Pallas kernels: 19.2 us -> 17 us
  starting transfers between devices: 33.3 us -> 32.2 us
    ppermute x1, starting transfers between devices: 1.12 us -> 0.09 us  [body(): taken = lax.ppermute(send, 'core', SWAP)]
    pallas_call x1, Pallas kernels: 5.4 us -> 4.4 us  [body(): pl.pallas_call(rest_kernel, out_shape=(fb_shape, gbuf_shape), in_specs=[s...]
    ppermute x1, waiting for transfers between devices: 1.21 us -> 2.21 us  [body(): far_a = lax.ppermute(after, 'z', ring(1))]
  transfers between devices with their start and end apart: 17 -> 17, of which waited for: 5 -> 5; matrix products, arithmetic and copies ran while one was open for 5% -> 5% of each run, Pallas kernels for 13% -> 11%
where the time goes in v5:
time: 90 us; the launch traced here: 89.7 us
  starting transfers between devices  32.2 us (36%)
  blocking collectives  21.2 us (24%)
  Pallas kernels  17 us (19%)
  waiting for transfers between devices  14.1 us (16%)
  other arithmetic  3.12 us (3%)
  local copies, waits for them, and re-layouts  1.94 us (2%)
    all_to_all x1, blocking collectives, body(): parts = lax.all_to_all(summed, CHIPS, 0, 0)  21.2 us
    ppermute x1, starting transfers between devices, body(): before = lax.ppermute(own, 'z', ring(-1))  6.37 us
    pallas_call x1, Pallas kernels, body(): pl.pallas_call(finish_kernel, out_shape=(gbuf_shape, block, block), in_sp...  5.7 us
    ppermute x1, starting transfers between devices, body(): near = lax.ppermute(own, 'xh', SWAP)  5.47 us
    pallas_call x1, Pallas kernels, body(): pl.pallas_call(rest_kernel, out_shape=(fb_shape, gbuf_shape), in_specs=[s...  4.4 us
    ppermute x1, waiting for transfers between devices, body(): g_far_a = lax.ppermute(g_after[0], 'y', ring(1))  4.1 us
    ppermute x1, waiting for transfers between devices, body(): beside = lax.ppermute(lines, 'xl', SWAP)  3.36 us
    ppermute x1, starting transfers between devices, body(): g_far_b = lax.ppermute(g_before[1], 'y', ring(-1))  3.29 us
  transfers between devices with their start and end apart: 17, of which 5 were waited for; matrix products, arithmetic and copies ran while one was open for 5% of the time, Pallas kernels for 11%

profile of v5, /device:TPU:0, one launch (start us, length us, event | category | flops | bytes accessed | tf_op | source)
XLA Modules:
  0.0 89.7 jit_solution(2949691476069374178)
XLA Ops:
  0.0 1.6 %collective-permute-start.5 = (bf16[2,32,2048]{2,1,0:T(8,128)(2,1)}, bf16[2,32,2048]{2,1,0:T(8,128)(2,1)S(1)}, u32[]{:S(2)}, u32[]{:S(2)}) collective-permute-start(bf16[2,32,2048]{2,1,0:T(8,128)(2,1)} %bitcast.33), channel_id=1, source_target_pairs={{0,2},{2,0},{1,3},{3,1},{4,6},{6,4},{5,7},{7,5},{8,10},{10,8},{9,1... | collective-permute-start | bytes 786440 | tf_op jit(solution)/shard_map/ppermute | solution.py:371
  1.6 0.8 broadcast_compare_fusion
  3.0 1.0 %dynamic-slice_bitcast_fusion.1 = (bf16[2,32,1024]{2,1,0:T(8,128)(2,1)S(1)}, bf16[2,32,1024]{2,1,0:T(8,128)(2,1)S(1)}) fusion(bf16[2,2048,32]{1,2,0:T(8,128)(2,1)} %param.5, s32[]{:T(128)S(6)} %select_n.19, s32[]{:T(128)S(6)} %select_n.20), kind=kLoop, calls=%fused_computation.8 | loop fusion | bytes 524296 | tf_op jit(solution)/shard_map/dynamic_slice | solution.py:367
  4.7 3.4 %collective-permute-done.5 = bf16[2,32,2048]{2,1,0:T(8,128)(2,1)S(1)} collective-permute-done((bf16[2,32,2048]{2,1,0:T(8,128)(2,1)}, bf16[2,32,2048]{2,1,0:T(8,128)(2,1)S(1)}, u32[]{:S(2)}, u32[]{:S(2)}) %collective-permute-start.5) | collective-permute-done | bytes 262176 | tf_op jit(solution)/shard_map/ppermute | solution.py:371
  8.1 1.0 %fusion.8 = (bf16[1,2,2,32,2048]{4,3,2,1,0:T(8,128)(2,1)S(1)}, bf16[2,2,32,2048]{3,2,1,0:T(8,128)(2,1)S(1)}) fusion(bf16[1,2,32,2048]{3,2,1,0:T(8,128)(2,1)S(1)} %bitcast.35, bf16[1,2,32,2048]{3,2,1,0:T(8,128)(2,1)} %bitcast.34), kind=kLoop, calls=%fused_computation.28 | loop fusion | flops 262144 | bytes 1572864 | tf_op jit(solution)/shard_map/stack | solution.py:395
  9.1 1.9 %collective-permute-start.6 = (bf16[2,2,32,2048]{3,2,1,0:T(8,128)(2,1)S(1)}, bf16[2,2,32,2048]{3,2,1,0:T(8,128)(2,1)S(1)}, u32[]{:S(2)}, u32[]{:S(2)}) collective-permute-start(bf16[2,2,32,2048]{3,2,1,0:T(8,128)(2,1)S(1)} %get-tuple-element.45.own), channel_id=1, source_target_pairs={{0,4},{4,8},{8,12},{12,0},{1,5},{5,9},{9,13},{13,1},{2,6},{6,10},{... | collective-permute-start | bytes 1572872 | tf_op jit(solution)/shard_map/ppermute | solution.py:375
  11.0 2.9 %collective-permute-start.7 = (bf16[2,2,32,2048]{3,2,1,0:T(8,128)(2,1)S(1)}, bf16[2,2,32,2048]{3,2,1,0:T(8,128)(2,1)S(1)}, u32[]{:S(2)}, u32[]{:S(2)}) collective-permute-start(bf16[2,2,32,2048]{3,2,1,0:T(8,128)(2,1)S(1)} %get-tuple-element.45.own), channel_id=1, source_target_pairs={{0,12},{4,0},{8,4},{12,8},{1,13},{5,1},{9,5},{13,9},{2,14},{6,2},{... | collective-permute-start | bytes 1572872 | tf_op jit(solution)/shard_map/ppermute | solution.py:376
  13.9 5.5 %collective-permute-start.2 = (bf16[2,2,32,1024]{3,2,1,0:T(8,128)(2,1)S(1)}, bf16[2,2,32,1024]{3,2,1,0:T(8,128)(2,1)S(1)}, u32[]{:S(2)}, u32[]{:S(2)}) collective-permute-start(bf16[2,2,32,1024]{3,2,1,0:T(8,128)(2,1)S(1)} %pad_maximum_fusion.3.own), channel_id=1, source_target_pairs={{0,64},{64,0},{1,65},{65,1},{2,66},{66,2},{3,67},{67,3},{4,68},{68... | collective-permute-start | bytes 786440 | tf_op jit(solution)/shard_map/ppermute | solution.py:379
  19.4 3.2 %collective-permute-start.3 = (bf16[2,2,32,1024]{3,2,1,0:T(8,128)(2,1)S(1)}, bf16[2,2,32,1024]{3,2,1,0:T(8,128)(2,1)S(1)}, u32[]{:S(2)}, u32[]{:S(2)}) collective-permute-start(bf16[2,2,32,1024]{3,2,1,0:T(8,128)(2,1)S(1)} %pad_maximum_fusion.3.own), channel_id=1, source_target_pairs={{0,16},{16,32},{32,48},{48,0},{1,17},{17,33},{33,49},{49,1},{2,18}... | collective-permute-start | bytes 786440 | tf_op jit(solution)/shard_map/ppermute | solution.py:377
  22.6 6.4 %collective-permute-start.4 = (bf16[2,2,32,1024]{3,2,1,0:T(8,128)(2,1)S(1)}, bf16[2,2,32,1024]{3,2,1,0:T(8,128)(2,1)S(1)}, u32[]{:S(2)}, u32[]{:S(2)}) collective-permute-start(bf16[2,2,32,1024]{3,2,1,0:T(8,128)(2,1)S(1)} %pad_maximum_fusion.3.own), channel_id=1, source_target_pairs={{0,48},{16,0},{32,16},{48,32},{1,49},{17,1},{33,17},{49,33},{2,50}... | collective-permute-start | bytes 786440 | tf_op jit(solution)/shard_map/ppermute | solution.py:378
  30.2 2.6 %load.1.abuf = bf16[4,2,2304,256]{3,2,1,0:T(8,128)(2,1)S(1)} custom-call(s32[54]{0:T(128)S(1)} %concatenate.3.st, bf16[2,2048,1024]{2,1,0:T(8,128)(2,1)} %a.1), custom_call_target="tpu_custom_call" | custom-call | bytes 8388608 | tf_op jit(solution)/shard_map/load/pallas_call | solution.py:382
  32.7 2.5 %collective-permute-done.3.after = bf16[2,2,32,1024]{3,2,1,0:T(8,128)(2,1)S(1)} collective-permute-done((bf16[2,2,32,1024]{3,2,1,0:T(8,128)(2,1)S(1)}, bf16[2,2,32,1024]{3,2,1,0:T(8,128)(2,1)S(1)}, u32[]{:S(2)}, u32[]{:S(2)}) %collective-permute-start.3) | collective-permute-done | bytes 262176 | tf_op jit(solution)/shard_map/ppermute | solution.py:377
  35.2 1.1 %collective-permute-start.10 = (bf16[2,2,32,1024]{3,2,1,0:T(8,128)(2,1)S(1)}, bf16[2,2,32,1024]{3,2,1,0:T(8,128)(2,1)S(1)}, u32[]{:S(2)}, u32[]{:S(2)}) collective-permute-start(bf16[2,2,32,1024]{3,2,1,0:T(8,128)(2,1)S(1)} %collective-permute-done.2.near), channel_id=1, source_target_pairs={{0,16},{16,32},{32,48},{48,0},{1,17},{17,33},{33,49},{49,1},{2,18}... | collective-permute-start | bytes 786440 | tf_op jit(solution)/shard_map/ppermute | solution.py:398
  36.4 2.1 %collective-permute-start.11 = (bf16[2,2,32,1024]{3,2,1,0:T(8,128)(2,1)S(1)}, bf16[2,2,32,1024]{3,2,1,0:T(8,128)(2,1)S(1)}, u32[]{:S(2)}, u32[]{:S(2)}) collective-permute-start(bf16[2,2,32,1024]{3,2,1,0:T(8,128)(2,1)S(1)} %collective-permute-done.2.near), channel_id=1, source_target_pairs={{0,48},{16,0},{32,16},{48,32},{1,49},{17,1},{33,17},{49,33},{2,50}... | collective-permute-start | bytes 786440 | tf_op jit(solution)/shard_map/ppermute | solution.py:399
  38.9 3.3 %collective-permute-start.9 = (bf16[2,32,2048]{2,1,0:T(8,128)(2,1)S(1)}, bf16[2,32,2048]{2,1,0:T(8,128)(2,1)S(1)}, u32[]{:S(2)}, u32[]{:S(2)}) collective-permute-start(bf16[2,32,2048]{2,1,0:T(8,128)(2,1)S(1)} %slice_bitcast_fusion), channel_id=1, source_target_pairs={{0,12},{4,0},{8,4},{12,8},{1,13},{5,1},{9,5},{13,9},{2,14},{6,2},{... | collective-permute-start | bytes 786440 | tf_op jit(solution)/shard_map/ppermute | solution.py:397
  42.2 2.5 %near.1.fb_in = bf16[4,512,1024]{2,1,0:T(8,128)(2,1)S(1)} custom-call(s32[54]{0:T(128)S(1)} %concatenate.3.st, bf16[4,2,2304,256]{3,2,1,0:T(8,128)(2,1)S(1)} %load.1.abuf, bf16[2,2,32,2048]{3,2,1,0:T(8,128)(2,1)S(1)} %get-tuple-element.45.own, bf16[2,2,32,2048]{3,2,1,0:T(8,128)(2,1)S(1)} %collective-permute-done.6.after, ...), custom_call_target="tpu_custom_call" | custom-call | flops 3221225472 | bytes 8388608 | tf_op jit(solution)/shard_map/near/pallas_call | solution.py:401
  44.6 4.1 %collective-permute-done.8.g_far_a = bf16[2,32,2048]{2,1,0:T(8,128)(2,1)S(1)} collective-permute-done((bf16[2,32,2048]{2,1,0:T(8,128)(2,1)S(1)}, bf16[2,32,2048]{2,1,0:T(8,128)(2,1)S(1)}, u32[]{:S(2)}, u32[]{:S(2)}) %collective-permute-start.8) | collective-permute-done | bytes 262176 | tf_op jit(solution)/shard_map/ppermute | solution.py:396
  49.0 3.2 %collective-permute-start.15 = (bf16[2,2,32,1024]{3,2,1,0:T(8,128)(2,1)S(1)}, bf16[2,2,32,1024]{3,2,1,0:T(8,128)(2,1)S(1)}, u32[]{:S(2)}, u32[]{:S(2)}) collective-permute-start(bf16[2,2,32,1024]{3,2,1,0:T(8,128)(2,1)S(1)} %collective-permute-done.11.near_before), channel_id=1, source_target_pairs={{0,48},{16,0},{32,16},{48,32},{1,49},{17,1},{33,17},{49,33},{2,50}... | collective-permute-start | bytes 786440 | tf_op jit(solution)/shard_map/ppermute | solution.py:416
  52.2 4.4 %rest.1 = (bf16[4,512,1024]{2,1,0:T(8,128)(2,1)S(1)}, bf16[2,512,1024]{2,1,0:T(8,128)(2,1)S(1)}) custom-call(s32[54]{0:T(128)S(1)} %concatenate.3.st, bf16[4,2,2304,256]{3,2,1,0:T(8,128)(2,1)S(1)} %load.1.abuf, bf16[4,512,1024]{2,1,0:T(8,128)(2,1)S(1)} %near.1.fb_in, ...), custom_call_target="tpu_custom_call", output_to_operand_aliasing={{0}: (2, {})} | custom-call | flops 5368709120 | bytes 8388608 | tf_op jit(solution)/shard_map/rest/pallas_call | solution.py:418
  56.6 2.2 %collective-permute-done.14.far_a = bf16[2,2,32,1024]{3,2,1,0:T(8,128)(2,1)S(1)} collective-permute-done((bf16[2,2,32,1024]{3,2,1,0:T(8,128)(2,1)S(1)}, bf16[2,2,32,1024]{3,2,1,0:T(8,128)(2,1)S(1)}, u32[]{:S(2)}, u32[]{:S(2)}) %collective-permute-start.14) | collective-permute-done | bytes 262176 | tf_op jit(solution)/shard_map/ppermute | solution.py:400
  58.8 5.7 %finish.1 = (bf16[2,512,1024]{2,1,0:T(8,128)(2,1)S(1)}, bf16[64,8,512]{2,1,0:T(8,128)(2,1)S(1)}, bf16[64,8,512]{2,1,0:T(8,128)(2,1)S(1)}) custom-call(s32[54]{0:T(128)S(1)} %concatenate.3.st, bf16[4,512,1024]{2,1,0:T(8,128)(2,1)S(1)} %get-tuple-element.33.fb, bf16[2,512,1024]{2,1,0:T(8,128)(2,1)S(1)} %get-tuple-element.34.gbuf_in, ...), custom_call_target="tpu_custom_call", output_to_operand_aliasing={{0}: (2, {})} | custom-call | flops 4294967296 | bytes 8388608 | tf_op jit(solution)/shard_map/finish/pallas_call | solution.py:437
  64.6 1.9 %collective-permute-done.16 = bf16[64,8,512]{2,1,0:T(8,128)(2,1)S(1)} collective-permute-done((bf16[64,8,512]{2,1,0:T(8,128)(2,1)S(1)}, bf16[64,8,512]{2,1,0:T(8,128)(2,1)S(1)}, u32[]{:S(2)}, u32[]{:S(2)}) %collective-permute-start.16) | collective-permute-done | bytes 524320 | tf_op jit(solution)/shard_map/ppermute | solution.py:448
  66.7 21.2 %all_to_all.5.parts = bf16[64,8,512]{2,1,0:T(8,128)(2,1)} all-to-all(bf16[64,8,512]{2,1,0:T(8,128)(2,1)S(1)} %add_convert_fusion), channel_id=1, replica_groups=mesh['xh'=2,'z'=4,'y'=4,'xl'=2,'core'=2] {'xh','z','y','xl'}, dimensions={0} | all-to-all | bytes 1048576 | tf_op jit(solution)/shard_map/all_to_all | solution.py:450
  87.8 1.8 %align.1 = f32[4,2,512]{2,1,0:T(2,128)} custom-call(s32[4]{0:T(128)} %index.1, bf16[64,8,512]{2,1,0:T(8,128)(2,1)} %all_to_all.5.parts), custom_call_target="tpu_custom_call" | custom-call | tf_op jit(solution)/shard_map/align/pallas_call | solution.py:451
  (36 shorter events, 3.5 us)
Async XLA Ops:
  0.0 8.1 %collective-permute-start.5 = (bf16[2,32,2048]{2,1,0:T(8,128)(2,1)}, bf16[2,32,2048]{2,1,0:T(8,128)(2,1)S(1)}, u32[]{:S(2)}, u32[]{:S(2)}) collective-permute-start(bf16[2,32,2048]{2,1,0:T(8,128)(2,1)} %bitcast.33), channel_id=1, source_target_pairs={{0,2},{2,0},{1,3},{3,1},{4,6},{6,4},{5,7},{7,5},{8,10},{10,8},{9,1... | collective-permute-start | bytes 786440 | tf_op jit(solution)/shard_map/ppermute | solution.py:371
  4.0 9.9 %collective-permute-start.1 = (bf16[2,32,1024]{2,1,0:T(8,128)(2,1)S(1)}, bf16[2,32,1024]{2,1,0:T(8,128)(2,1)S(1)}, u32[]{:S(2)}, u32[]{:S(2)}) collective-permute-start(bf16[2,32,1024]{2,1,0:T(8,128)(2,1)S(1)} %get-tuple-element.47), channel_id=1, source_target_pairs={{0,1},{1,0},{2,65},{3,64},{4,17},{5,16},{6,81},{7,80},{8,33},{9,32... | collective-permute-start | bytes 393224 | tf_op jit(solution)/shard_map/ppermute | solution.py:370
  4.1 9.8 %collective-permute-start = (bf16[2,32,1024]{2,1,0:T(8,128)(2,1)S(1)}, bf16[2,32,1024]{2,1,0:T(8,128)(2,1)S(1)}, u32[]{:S(2)}, u32[]{:S(2)}) collective-permute-start(bf16[2,32,1024]{2,1,0:T(8,128)(2,1)S(1)} %get-tuple-element.46), channel_id=1, source_target_pairs={{0,0},{1,1},{2,64},{3,65},{4,16},{5,17},{6,80},{7,81},{8,32},{9,33... | collective-permute-start | bytes 393224 | tf_op jit(solution)/shard_map/ppermute | solution.py:369
  9.1 29.3 %collective-permute-start.6 = (bf16[2,2,32,2048]{3,2,1,0:T(8,128)(2,1)S(1)}, bf16[2,2,32,2048]{3,2,1,0:T(8,128)(2,1)S(1)}, u32[]{:S(2)}, u32[]{:S(2)}) collective-permute-start(bf16[2,2,32,2048]{3,2,1,0:T(8,128)(2,1)S(1)} %get-tuple-element.45.own), channel_id=1, source_target_pairs={{0,4},{4,8},{8,12},{12,0},{1,5},{5,9},{9,13},{13,1},{2,6},{6,10},{... | collective-permute-start | bytes 1572872 | tf_op jit(solution)/shard_map/ppermute | solution.py:375
  11.0 27.4 %collective-permute-start.7 = (bf16[2,2,32,2048]{3,2,1,0:T(8,128)(2,1)S(1)}, bf16[2,2,32,2048]{3,2,1,0:T(8,128)(2,1)S(1)}, u32[]{:S(2)}, u32[]{:S(2)}) collective-permute-start(bf16[2,2,32,2048]{3,2,1,0:T(8,128)(2,1)S(1)} %get-tuple-element.45.own), channel_id=1, source_target_pairs={{0,12},{4,0},{8,4},{12,8},{1,13},{5,1},{9,5},{13,9},{2,14},{6,2},{... | collective-permute-start | bytes 1572872 | tf_op jit(solution)/shard_map/ppermute | solution.py:376
  13.9 18.8 %collective-permute-start.2 = (bf16[2,2,32,1024]{3,2,1,0:T(8,128)(2,1)S(1)}, bf16[2,2,32,1024]{3,2,1,0:T(8,128)(2,1)S(1)}, u32[]{:S(2)}, u32[]{:S(2)}) collective-permute-start(bf16[2,2,32,1024]{3,2,1,0:T(8,128)(2,1)S(1)} %pad_maximum_fusion.3.own), channel_id=1, source_target_pairs={{0,64},{64,0},{1,65},{65,1},{2,66},{66,2},{3,67},{67,3},{4,68},{68... | collective-permute-start | bytes 786440 | tf_op jit(solution)/shard_map/ppermute | solution.py:379
  19.4 15.8 %collective-permute-start.3 = (bf16[2,2,32,1024]{3,2,1,0:T(8,128)(2,1)S(1)}, bf16[2,2,32,1024]{3,2,1,0:T(8,128)(2,1)S(1)}, u32[]{:S(2)}, u32[]{:S(2)}) collective-permute-start(bf16[2,2,32,1024]{3,2,1,0:T(8,128)(2,1)S(1)} %pad_maximum_fusion.3.own), channel_id=1, source_target_pairs={{0,16},{16,32},{32,48},{48,0},{1,17},{17,33},{33,49},{49,1},{2,18}... | collective-permute-start | bytes 786440 | tf_op jit(solution)/shard_map/ppermute | solution.py:377
  22.6 12.6 %collective-permute-start.4 = (bf16[2,2,32,1024]{3,2,1,0:T(8,128)(2,1)S(1)}, bf16[2,2,32,1024]{3,2,1,0:T(8,128)(2,1)S(1)}, u32[]{:S(2)}, u32[]{:S(2)}) collective-permute-start(bf16[2,2,32,1024]{3,2,1,0:T(8,128)(2,1)S(1)} %pad_maximum_fusion.3.own), channel_id=1, source_target_pairs={{0,48},{16,0},{32,16},{48,32},{1,49},{17,1},{33,17},{49,33},{2,50}... | collective-permute-start | bytes 786440 | tf_op jit(solution)/shard_map/ppermute | solution.py:378
  35.2 9.4 %collective-permute-start.10 = (bf16[2,2,32,1024]{3,2,1,0:T(8,128)(2,1)S(1)}, bf16[2,2,32,1024]{3,2,1,0:T(8,128)(2,1)S(1)}, u32[]{:S(2)}, u32[]{:S(2)}) collective-permute-start(bf16[2,2,32,1024]{3,2,1,0:T(8,128)(2,1)S(1)} %collective-permute-done.2.near), channel_id=1, source_target_pairs={{0,16},{16,32},{32,48},{48,0},{1,17},{17,33},{33,49},{49,1},{2,18}... | collective-permute-start | bytes 786440 | tf_op jit(solution)/shard_map/ppermute | solution.py:398
  36.4 8.3 %collective-permute-start.11 = (bf16[2,2,32,1024]{3,2,1,0:T(8,128)(2,1)S(1)}, bf16[2,2,32,1024]{3,2,1,0:T(8,128)(2,1)S(1)}, u32[]{:S(2)}, u32[]{:S(2)}) collective-permute-start(bf16[2,2,32,1024]{3,2,1,0:T(8,128)(2,1)S(1)} %collective-permute-done.2.near), channel_id=1, source_target_pairs={{0,48},{16,0},{32,16},{48,32},{1,49},{17,1},{33,17},{49,33},{2,50}... | collective-permute-start | bytes 786440 | tf_op jit(solution)/shard_map/ppermute | solution.py:399
  38.6 13.6 %collective-permute-start.12 = (bf16[3,2,2,32,2048]{4,3,2,1,0:T(8,128)(2,1)S(1)}, bf16[3,2,2,32,2048]{4,3,2,1,0:T(8,128)(2,1)S(1)}, u32[]{:S(2)}, u32[]{:S(2)}) collective-permute-start(bf16[3,2,2,32,2048]{4,3,2,1,0:T(8,128)(2,1)S(1)} %pad_maximum_fusion), channel_id=1, source_target_pairs={{0,1},{1,0},{2,3},{3,2},{4,5},{5,4},{6,7},{7,6},{8,9},{9,8},{10,11... | collective-permute-start | bytes 4718600 | tf_op jit(solution)/shard_map/ppermute | solution.py:395
  38.8 10.0 %collective-permute-start.8 = (bf16[2,32,2048]{2,1,0:T(8,128)(2,1)S(1)}, bf16[2,32,2048]{2,1,0:T(8,128)(2,1)S(1)}, u32[]{:S(2)}, u32[]{:S(2)}) collective-permute-start(bf16[2,32,2048]{2,1,0:T(8,128)(2,1)S(1)} %slice_bitcast_fusion.1), channel_id=1, source_target_pairs={{0,4},{4,8},{8,12},{12,0},{1,5},{5,9},{9,13},{13,1},{2,6},{6,10},{... | collective-permute-start | bytes 786440 | tf_op jit(solution)/shard_map/ppermute | solution.py:396
  38.9 9.9 %collective-permute-start.9 = (bf16[2,32,2048]{2,1,0:T(8,128)(2,1)S(1)}, bf16[2,32,2048]{2,1,0:T(8,128)(2,1)S(1)}, u32[]{:S(2)}, u32[]{:S(2)}) collective-permute-start(bf16[2,32,2048]{2,1,0:T(8,128)(2,1)S(1)} %slice_bitcast_fusion), channel_id=1, source_target_pairs={{0,12},{4,0},{8,4},{12,8},{1,13},{5,1},{9,5},{13,9},{2,14},{6,2},{... | collective-permute-start | bytes 786440 | tf_op jit(solution)/shard_map/ppermute | solution.py:397
  48.8 3.4 %collective-permute-start.13 = (bf16[2,2,32,2048]{3,2,1,0:T(8,128)(2,1)S(1)}, bf16[2,2,32,2048]{3,2,1,0:T(8,128)(2,1)S(1)}, u32[]{:S(2)}, u32[]{:S(2)}) collective-permute-start(bf16[2,2,32,2048]{3,2,1,0:T(8,128)(2,1)S(1)} %pad_maximum_fusion.2), channel_id=1, source_target_pairs={{0,1},{1,0},{2,3},{3,2},{4,5},{5,4},{6,7},{7,6},{8,9},{9,8},{10,11... | collective-permute-start | bytes 1572872 | tf_op jit(solution)/shard_map/ppermute | solution.py:415
  48.9 9.9 %collective-permute-start.14 = (bf16[2,2,32,1024]{3,2,1,0:T(8,128)(2,1)S(1)}, bf16[2,2,32,1024]{3,2,1,0:T(8,128)(2,1)S(1)}, u32[]{:S(2)}, u32[]{:S(2)}) collective-permute-start(bf16[2,2,32,1024]{3,2,1,0:T(8,128)(2,1)S(1)} %collective-permute-done.3.after), channel_id=1, source_target_pairs={{0,16},{16,32},{32,48},{48,0},{1,17},{17,33},{33,49},{49,1},{2,18}... | collective-permute-start | bytes 786440 | tf_op jit(solution)/shard_map/ppermute | solution.py:400
  49.0 9.9 %collective-permute-start.15 = (bf16[2,2,32,1024]{3,2,1,0:T(8,128)(2,1)S(1)}, bf16[2,2,32,1024]{3,2,1,0:T(8,128)(2,1)S(1)}, u32[]{:S(2)}, u32[]{:S(2)}) collective-permute-start(bf16[2,2,32,1024]{3,2,1,0:T(8,128)(2,1)S(1)} %collective-permute-done.11.near_before), channel_id=1, source_target_pairs={{0,48},{16,0},{32,16},{48,32},{1,49},{17,1},{33,17},{49,33},{2,50}... | collective-permute-start | bytes 786440 | tf_op jit(solution)/shard_map/ppermute | solution.py:416
  64.5 2.0 %collective-permute-start.16 = (bf16[64,8,512]{2,1,0:T(8,128)(2,1)S(1)}, bf16[64,8,512]{2,1,0:T(8,128)(2,1)S(1)}, u32[]{:S(2)}, u32[]{:S(2)}) collective-permute-start(bf16[64,8,512]{2,1,0:T(8,128)(2,1)S(1)} %get-tuple-element.36), channel_id=1, source_target_pairs={{0,1},{1,0},{2,3},{3,2},{4,5},{5,4},{6,7},{7,6},{8,9},{9,8},{10,11... | collective-permute-start | bytes 1572872 | tf_op jit(solution)/shard_map/ppermute | solution.py:448

commit v6 on v5

--- a/solution.py
+++ b/solution.py
@@ -121,21 +121,26 @@
             lax.fori_loop(0, n - 1, step, 0)
             stream(st[8 + c * ROW_TILES + n - 1])
 
-        for b, row in enumerate(targets):
-            rows = pl.ds(pl.multiple_of(row, SHARD), SHARD)
-            rr, ri, ir, ii = popped(b)
-            fb[0, rows, lanes] = (rr + ii).astype(jnp.bfloat16)
-            fb[1, rows, lanes] = (ri - ir).astype(jnp.bfloat16)
-            fb[2, rows, lanes] = (rr - ii).astype(jnp.bfloat16)
-            fb[3, rows, lanes] = (ri + ir).astype(jnp.bfloat16)
-
-            @pl.when(on_diag)
-            def _():
-                saved[0, b * SHARD : (b + 1) * SHARD, :] = rr + ii
-                saved[1, b * SHARD : (b + 1) * SHARD, :] = ri - ir
+        def flush(save):
+            for b, row in enumerate(targets):
+                rows = pl.ds(pl.multiple_of(row, SHARD), SHARD)
+                rr, ri, ir, ii = popped(b)
+                fb[2, rows, lanes] = (rr - ii).astype(jnp.bfloat16)
+                fb[3, rows, lanes] = (ri + ir).astype(jnp.bfloat16)
+                if save:
+                    saved[0, b * SHARD : (b + 1) * SHARD, :] = rr + ii
+                    saved[1, b * SHARD : (b + 1) * SHARD, :] = ri - ir
+                else:
+                    fb[0, rows, lanes] = (rr + ii).astype(jnp.bfloat16)
+                    fb[1, rows, lanes] = (ri - ir).astype(jnp.bfloat16)
+
+        @pl.when(jnp.logical_not(on_diag))
+        def _():
+            flush(False)
 
         @pl.when(on_diag)
         def _():
+            flush(True)
             push(c, ROW_TILES)
             stream(st[44 + c])
             for b, row in enumerate(targets):
@@ -188,7 +193,7 @@
 
 
 def rest_kernel(
-    st, abuf, fb_in, swap, g_far_a, g_far_b, swap_far,
+    st, abuf, fb_in, swap, g_far_a, g_far_b, swap_far_a, swap_far_b,
     own, near, after, before, near_after, near_before,
     fb, gbuf, saved, gsem,
 ):
@@ -215,9 +220,10 @@
             return jnp.concatenate(
                 [
                     swap[:, :, :, :, lanes].reshape(12 * SHARD, TILE),
-                    g_far_a[:, :, lanes].reshape(2 * SHARD, TILE),
-                    g_far_b[:, :, lanes].reshape(2 * SHARD, TILE),
-                    swap_far[:, :, :, lanes].reshape(4 * SHARD, TILE),
+                ]
+                + [
+                    ref[:, :, lanes].reshape(2 * SHARD, TILE)
+                    for ref in (g_far_a, g_far_b, swap_far_a, swap_far_b)
                 ],
                 axis=0,
             )
@@ -282,20 +288,13 @@
                 for unit in range(2):
                     re = pltpu.matmul_pop(accs[unit * blocks + b]).reshape(chips, 8, TILE)
                     im = pltpu.matmul_pop(accs[unit * blocks + blocks // 2 + b]).reshape(chips, 8, TILE)
-                    first = jnp.where(low, re, pltpu.roll(im, 4, 1)).astype(jnp.bfloat16)
-                    second = jnp.where(low, pltpu.roll(re, 4, 1), im).astype(jnp.bfloat16)
+                    first = jnp.where(low, re, pltpu.roll(im, 4, 1))
+                    second = jnp.where(low, pltpu.roll(re, 4, 1), im)
                     at = slice(b * chips, (b + 1) * chips)
                     lanes = slice(unit * TILE, (unit + 1) * TILE)
 
-                    @pl.when(core == 0)
-                    def _():
-                        keep[at, :, lanes] = first
-                        send[at, :, lanes] = second
-
-                    @pl.when(core != 0)
-                    def _():
-                        keep[at, :, lanes] = second
-                        send[at, :, lanes] = first
+                    keep[at, :, lanes] = jnp.where(core == 0, first, second).astype(jnp.bfloat16)
+                    send[at, :, lanes] = jnp.where(core == 0, second, first).astype(jnp.bfloat16)
 
         pl.run_scoped(multiply, *accumulators(blocks))
 
@@ -389,8 +388,8 @@
         cost_estimate=pl.CostEstimate(flops=0, transcendentals=0, bytes_accessed=8 << 20),
         name="load",
     )(state, pltpu.with_memory_space_constraint(reflection, pltpu.HBM))
-    g_after, g_before, _ = lax.optimization_barrier((g_after, g_before, own))
     abuf, near, after, before = lax.optimization_barrier((abuf, near, after, before))
+    g_after, g_before, _, _ = lax.optimization_barrier((g_after, g_before, near, abuf))
 
     swap = lax.ppermute(jnp.stack([g_own, g_after, g_before]), "core", SWAP)
     g_far_a = lax.ppermute(g_after[0], "y", ring(1))
@@ -412,13 +411,14 @@
         (g_far_a, g_far_b, near_after, near_before, fb)
     )
 
-    swap_far = lax.ppermute(jnp.stack([g_far_a, g_far_b]), "core", SWAP)
+    swap_far_a = lax.ppermute(g_far_a, "core", SWAP)
+    swap_far_b = lax.ppermute(g_far_b, "core", SWAP)
     far_b = lax.ppermute(near_before, "z", ring(-1))
     gbuf_shape = jax.ShapeDtypeStruct((2, P_SIZE, COLS), jnp.bfloat16)
     fb, gbuf = pl.pallas_call(
         rest_kernel,
         out_shape=(fb_shape, gbuf_shape),
-        in_specs=[smem_spec()] + [vmem_spec()] * 6 + [any_spec()] * 6,
+        in_specs=[smem_spec()] + [vmem_spec()] * 7 + [any_spec()] * 6,
         out_specs=(vmem_spec(), vmem_spec()),
         scratch_shapes=[
             pltpu.VMEM((2, 10 * SHARD, TILE), jnp.float32),
@@ -429,7 +429,7 @@
         cost_estimate=pl.CostEstimate(flops=5 << 30, transcendentals=0, bytes_accessed=8 << 20),
         name="rest",
     )(
-        state, abuf, fb, swap, g_far_a, g_far_b, swap_far,
+        state, abuf, fb, swap, g_far_a, g_far_b, swap_far_a, swap_far_b,
         own, near, after, before, near_after, near_before,
     )
 

time: 90 us -> 89.3 us (level)
    ppermute x1, waiting for transfers between devices: 4.1 us -> 2.76 us  [body(): g_far_a = lax.ppermute(g_after[0], 'y', ring(1))]
    ppermute x1, waiting for transfers between devices: 0.01 us -> 0.93 us  [body(): near_after = lax.ppermute(near, 'z', ring(1))]
  transfers between devices with their start and end apart: 17 -> 18, of which waited for: 5 -> 6; matrix products, arithmetic and copies ran while one was open for 5% -> 5% of each run, Pallas kernels for 11% -> 10%
where the time goes in v6:
time: 89.3 us; the launch traced here: 89 us
  starting transfers between devices  32.7 us (37%)
  blocking collectives  21.2 us (24%)
  Pallas kernels  16.4 us (18%)
  waiting for transfers between devices  13.5 us (15%)
  other arithmetic  3.1 us (3%)
  local copies, waits for them, and re-layouts  2.01 us (2%)
    all_to_all x1, blocking collectives, body(): parts = lax.all_to_all(summed, CHIPS, 0, 0)  21.2 us
    ppermute x1, starting transfers between devices, body(): before = lax.ppermute(own, 'z', ring(-1))  6.37 us
    pallas_call x1, Pallas kernels, body(): pl.pallas_call(finish_kernel, out_shape=(gbuf_shape, block, block), in_sp...  5.66 us
    ppermute x1, starting transfers between devices, body(): near = lax.ppermute(own, 'xh', SWAP)  5.47 us
    pallas_call x1, Pallas kernels, body(): pl.pallas_call(rest_kernel, out_shape=(fb_shape, gbuf_shape), in_specs=[s...  4 us
    ppermute x1, waiting for transfers between devices, body(): beside = lax.ppermute(lines, 'xl', SWAP)  3.32 us
    ppermute x1, starting transfers between devices, body(): g_far_b = lax.ppermute(g_before[1], 'y', ring(-1))  3.29 us
    ppermute x1, starting transfers between devices, body(): far_b = lax.ppermute(near_before, 'z', ring(-1))  3.23 us
  transfers between devices with their start and end apart: 18, of which 6 were waited for; matrix products, arithmetic and copies ran while one was open for 5% of the time, Pallas kernels for 10%

profile of v6, /device:TPU:0, one launch (start us, length us, event | category | flops | bytes accessed | tf_op | source)
XLA Modules:
  0.0 89.0 jit_solution(12211212649705611367)
XLA Ops:
  0.0 1.6 %collective-permute-start.5 = (bf16[2,32,2048]{2,1,0:T(8,128)(2,1)}, bf16[2,32,2048]{2,1,0:T(8,128)(2,1)S(1)}, u32[]{:S(2)}, u32[]{:S(2)}) collective-permute-start(bf16[2,32,2048]{2,1,0:T(8,128)(2,1)} %bitcast.29), channel_id=1, source_target_pairs={{0,2},{2,0},{1,3},{3,1},{4,6},{6,4},{5,7},{7,5},{8,10},{10,8},{9,1... | collective-permute-start | bytes 786440 | tf_op jit(solution)/shard_map/ppermute | solution.py:370
  3.0 1.0 %dynamic-slice_bitcast_fusion.1 = (bf16[2,32,1024]{2,1,0:T(8,128)(2,1)S(1)}, bf16[2,32,1024]{2,1,0:T(8,128)(2,1)S(1)}) fusion(bf16[2,2048,32]{1,2,0:T(8,128)(2,1)} %param.5, s32[]{:T(128)S(6)} %select_n.19, s32[]{:T(128)S(6)} %select_n.20), kind=kLoop, calls=%fused_computation.7 | loop fusion | bytes 524296 | tf_op jit(solution)/shard_map/dynamic_slice | solution.py:366
  4.8 3.3 %collective-permute-done.5 = bf16[2,32,2048]{2,1,0:T(8,128)(2,1)S(1)} collective-permute-done((bf16[2,32,2048]{2,1,0:T(8,128)(2,1)}, bf16[2,32,2048]{2,1,0:T(8,128)(2,1)S(1)}, u32[]{:S(2)}, u32[]{:S(2)}) %collective-permute-start.5) | collective-permute-done | bytes 262176 | tf_op jit(solution)/shard_map/ppermute | solution.py:370
  8.1 1.0 %fusion.8 = (bf16[1,2,2,32,2048]{4,3,2,1,0:T(8,128)(2,1)S(1)}, bf16[2,2,32,2048]{3,2,1,0:T(8,128)(2,1)S(1)}) fusion(bf16[1,2,32,2048]{3,2,1,0:T(8,128)(2,1)S(1)} %bitcast.31, bf16[1,2,32,2048]{3,2,1,0:T(8,128)(2,1)} %bitcast.30), kind=kLoop, calls=%fused_computation.27 | loop fusion | flops 262144 | bytes 1572864 | tf_op jit(solution)/shard_map/stack | solution.py:394
  9.1 1.9 %collective-permute-start.6 = (bf16[2,2,32,2048]{3,2,1,0:T(8,128)(2,1)S(1)}, bf16[2,2,32,2048]{3,2,1,0:T(8,128)(2,1)S(1)}, u32[]{:S(2)}, u32[]{:S(2)}) collective-permute-start(bf16[2,2,32,2048]{3,2,1,0:T(8,128)(2,1)S(1)} %get-tuple-element.45.own), channel_id=1, source_target_pairs={{0,4},{4,8},{8,12},{12,0},{1,5},{5,9},{9,13},{13,1},{2,6},{6,10},{... | collective-permute-start | bytes 1572872 | tf_op jit(solution)/shard_map/ppermute | solution.py:374
  11.0 2.9 %collective-permute-start.7 = (bf16[2,2,32,2048]{3,2,1,0:T(8,128)(2,1)S(1)}, bf16[2,2,32,2048]{3,2,1,0:T(8,128)(2,1)S(1)}, u32[]{:S(2)}, u32[]{:S(2)}) collective-permute-start(bf16[2,2,32,2048]{3,2,1,0:T(8,128)(2,1)S(1)} %get-tuple-element.45.own), channel_id=1, source_target_pairs={{0,12},{4,0},{8,4},{12,8},{1,13},{5,1},{9,5},{13,9},{2,14},{6,2},{... | collective-permute-start | bytes 1572872 | tf_op jit(solution)/shard_map/ppermute | solution.py:375
  14.0 5.5 %collective-permute-start.2 = (bf16[2,2,32,1024]{3,2,1,0:T(8,128)(2,1)S(1)}, bf16[2,2,32,1024]{3,2,1,0:T(8,128)(2,1)S(1)}, u32[]{:S(2)}, u32[]{:S(2)}) collective-permute-start(bf16[2,2,32,1024]{3,2,1,0:T(8,128)(2,1)S(1)} %pad_maximum_fusion.2.own), channel_id=1, source_target_pairs={{0,64},{64,0},{1,65},{65,1},{2,66},{66,2},{3,67},{67,3},{4,68},{68... | collective-permute-start | bytes 786440 | tf_op jit(solution)/shard_map/ppermute | solution.py:378
  19.4 3.2 %collective-permute-start.3 = (bf16[2,2,32,1024]{3,2,1,0:T(8,128)(2,1)S(1)}, bf16[2,2,32,1024]{3,2,1,0:T(8,128)(2,1)S(1)}, u32[]{:S(2)}, u32[]{:S(2)}) collective-permute-start(bf16[2,2,32,1024]{3,2,1,0:T(8,128)(2,1)S(1)} %pad_maximum_fusion.2.own), channel_id=1, source_target_pairs={{0,16},{16,32},{32,48},{48,0},{1,17},{17,33},{33,49},{49,1},{2,18}... | collective-permute-start | bytes 786440 | tf_op jit(solution)/shard_map/ppermute | solution.py:376
  22.6 6.4 %collective-permute-start.4 = (bf16[2,2,32,1024]{3,2,1,0:T(8,128)(2,1)S(1)}, bf16[2,2,32,1024]{3,2,1,0:T(8,128)(2,1)S(1)}, u32[]{:S(2)}, u32[]{:S(2)}) collective-permute-start(bf16[2,2,32,1024]{3,2,1,0:T(8,128)(2,1)S(1)} %pad_maximum_fusion.2.own), channel_id=1, source_target_pairs={{0,48},{16,0},{32,16},{48,32},{1,49},{17,1},{33,17},{49,33},{2,50}... | collective-permute-start | bytes 786440 | tf_op jit(solution)/shard_map/ppermute | solution.py:377
  30.3 2.6 %load.1.abuf = bf16[4,2,2304,256]{3,2,1,0:T(8,128)(2,1)S(1)} custom-call(s32[54]{0:T(128)S(1)} %concatenate.3.st, bf16[2,2048,1024]{2,1,0:T(8,128)(2,1)} %a.1), custom_call_target="tpu_custom_call" | custom-call | bytes 8388608 | tf_op jit(solution)/shard_map/load/pallas_call | solution.py:381
  32.9 2.4 %collective-permute-done.3.after = bf16[2,2,32,1024]{3,2,1,0:T(8,128)(2,1)S(1)} collective-permute-done((bf16[2,2,32,1024]{3,2,1,0:T(8,128)(2,1)S(1)}, bf16[2,2,32,1024]{3,2,1,0:T(8,128)(2,1)S(1)}, u32[]{:S(2)}, u32[]{:S(2)}) %collective-permute-start.3) | collective-permute-done | bytes 262176 | tf_op jit(solution)/shard_map/ppermute | solution.py:376
  35.5 1.2 %collective-permute-start.10 = (bf16[2,2,32,1024]{3,2,1,0:T(8,128)(2,1)S(1)}, bf16[2,2,32,1024]{3,2,1,0:T(8,128)(2,1)S(1)}, u32[]{:S(2)}, u32[]{:S(2)}) collective-permute-start(bf16[2,2,32,1024]{3,2,1,0:T(8,128)(2,1)S(1)} %collective-permute-done.2.near), channel_id=1, source_target_pairs={{0,16},{16,32},{32,48},{48,0},{1,17},{17,33},{33,49},{49,1},{2,18}... | collective-permute-start | bytes 786440 | tf_op jit(solution)/shard_map/ppermute | solution.py:397
  36.7 2.1 %collective-permute-start.11 = (bf16[2,2,32,1024]{3,2,1,0:T(8,128)(2,1)S(1)}, bf16[2,2,32,1024]{3,2,1,0:T(8,128)(2,1)S(1)}, u32[]{:S(2)}, u32[]{:S(2)}) collective-permute-start(bf16[2,2,32,1024]{3,2,1,0:T(8,128)(2,1)S(1)} %collective-permute-done.2.near), channel_id=1, source_target_pairs={{0,48},{16,0},{32,16},{48,32},{1,49},{17,1},{33,17},{49,33},{2,50}... | collective-permute-start | bytes 786440 | tf_op jit(solution)/shard_map/ppermute | solution.py:398
  39.0 3.3 %collective-permute-start.9 = (bf16[2,32,2048]{2,1,0:T(8,128)(2,1)S(1)}, bf16[2,32,2048]{2,1,0:T(8,128)(2,1)S(1)}, u32[]{:S(2)}, u32[]{:S(2)}) collective-permute-start(bf16[2,32,2048]{2,1,0:T(8,128)(2,1)S(1)} %slice_bitcast_fusion), channel_id=1, source_target_pairs={{0,12},{4,0},{8,4},{12,8},{1,13},{5,1},{9,5},{13,9},{2,14},{6,2},{... | collective-permute-start | bytes 786440 | tf_op jit(solution)/shard_map/ppermute | solution.py:396
  42.3 2.3 %near.1.fb_in = bf16[4,512,1024]{2,1,0:T(8,128)(2,1)S(1)} custom-call(s32[54]{0:T(128)S(1)} %concatenate.3.st, bf16[4,2,2304,256]{3,2,1,0:T(8,128)(2,1)S(1)} %load.1.abuf, bf16[2,2,32,2048]{3,2,1,0:T(8,128)(2,1)S(1)} %get-tuple-element.45.own, bf16[2,2,32,2048]{3,2,1,0:T(8,128)(2,1)S(1)} %collective-permute-done.6.after, ...), custom_call_target="tpu_custom_call" | custom-call | flops 3221225472 | bytes 8388608 | tf_op jit(solution)/shard_map/near/pallas_call | solution.py:400
  44.5 0.9 %collective-permute-done.10.near_after = bf16[2,2,32,1024]{3,2,1,0:T(8,128)(2,1)S(1)} collective-permute-done((bf16[2,2,32,1024]{3,2,1,0:T(8,128)(2,1)S(1)}, bf16[2,2,32,1024]{3,2,1,0:T(8,128)(2,1)S(1)}, u32[]{:S(2)}, u32[]{:S(2)}) %collective-permute-start.10) | collective-permute-done | bytes 262176 | tf_op jit(solution)/shard_map/ppermute | solution.py:397
  45.5 2.8 %collective-permute-done.8.g_far_a = bf16[2,32,2048]{2,1,0:T(8,128)(2,1)S(1)} collective-permute-done((bf16[2,32,2048]{2,1,0:T(8,128)(2,1)S(1)}, bf16[2,32,2048]{2,1,0:T(8,128)(2,1)S(1)}, u32[]{:S(2)}, u32[]{:S(2)}) %collective-permute-start.8) | collective-permute-done | bytes 262176 | tf_op jit(solution)/shard_map/ppermute | solution.py:395
  48.7 3.2 %collective-permute-start.16 = (bf16[2,2,32,1024]{3,2,1,0:T(8,128)(2,1)S(1)}, bf16[2,2,32,1024]{3,2,1,0:T(8,128)(2,1)S(1)}, u32[]{:S(2)}, u32[]{:S(2)}) collective-permute-start(bf16[2,2,32,1024]{3,2,1,0:T(8,128)(2,1)S(1)} %collective-permute-done.11.near_before), channel_id=1, source_target_pairs={{0,48},{16,0},{32,16},{48,32},{1,49},{17,1},{33,17},{49,33},{2,50}... | collective-permute-start | bytes 786440 | tf_op jit(solution)/shard_map/ppermute | solution.py:416
  52.0 4.0 %rest.1 = (bf16[4,512,1024]{2,1,0:T(8,128)(2,1)S(1)}, bf16[2,512,1024]{2,1,0:T(8,128)(2,1)S(1)}) custom-call(s32[54]{0:T(128)S(1)} %concatenate.3.st, bf16[4,2,2304,256]{3,2,1,0:T(8,128)(2,1)S(1)} %load.1.abuf, bf16[4,512,1024]{2,1,0:T(8,128)(2,1)S(1)} %near.1.fb_in, ...), custom_call_target="tpu_custom_call", output_to_operand_aliasing={{0}: (2, {})} | custom-call | flops 5368709120 | bytes 8388608 | tf_op jit(solution)/shard_map/rest/pallas_call | solution.py:418
  56.0 2.2 %collective-permute-done.15.far_a = bf16[2,2,32,1024]{3,2,1,0:T(8,128)(2,1)S(1)} collective-permute-done((bf16[2,2,32,1024]{3,2,1,0:T(8,128)(2,1)S(1)}, bf16[2,2,32,1024]{3,2,1,0:T(8,128)(2,1)S(1)}, u32[]{:S(2)}, u32[]{:S(2)}) %collective-permute-start.15) | collective-permute-done | bytes 262176 | tf_op jit(solution)/shard_map/ppermute | solution.py:399
  58.2 5.7 %finish.1 = (bf16[2,512,1024]{2,1,0:T(8,128)(2,1)S(1)}, bf16[64,8,512]{2,1,0:T(8,128)(2,1)S(1)}, bf16[64,8,512]{2,1,0:T(8,128)(2,1)S(1)}) custom-call(s32[54]{0:T(128)S(1)} %concatenate.3.st, bf16[4,512,1024]{2,1,0:T(8,128)(2,1)S(1)} %get-tuple-element.33.fb, bf16[2,512,1024]{2,1,0:T(8,128)(2,1)S(1)} %get-tuple-element.34.gbuf_in, ...), custom_call_target="tpu_custom_call", output_to_operand_aliasing={{0}: (2, {})} | custom-call | flops 4294967296 | bytes 8388608 | tf_op jit(solution)/shard_map/finish/pallas_call | solution.py:437
  63.9 1.9 %collective-permute-done.17 = bf16[64,8,512]{2,1,0:T(8,128)(2,1)S(1)} collective-permute-done((bf16[64,8,512]{2,1,0:T(8,128)(2,1)S(1)}, bf16[64,8,512]{2,1,0:T(8,128)(2,1)S(1)}, u32[]{:S(2)}, u32[]{:S(2)}) %collective-permute-start.17) | collective-permute-done | bytes 524320 | tf_op jit(solution)/shard_map/ppermute | solution.py:448
  66.0 21.2 %all_to_all.5.parts = bf16[64,8,512]{2,1,0:T(8,128)(2,1)} all-to-all(bf16[64,8,512]{2,1,0:T(8,128)(2,1)S(1)} %add_convert_fusion), channel_id=1, replica_groups=mesh['xh'=2,'z'=4,'y'=4,'xl'=2,'core'=2] {'xh','z','y','xl'}, dimensions={0} | all-to-all | bytes 1048576 | tf_op jit(solution)/shard_map/all_to_all | solution.py:450
  87.1 1.8 %align.1 = f32[4,2,512]{2,1,0:T(2,128)} custom-call(s32[4]{0:T(128)} %index.1, bf16[64,8,512]{2,1,0:T(8,128)(2,1)} %all_to_all.5.parts), custom_call_target="tpu_custom_call" | custom-call | tf_op jit(solution)/shard_map/align/pallas_call | solution.py:451
  (37 shorter events, 4.6 us)
Async XLA Ops:
  0.0 8.1 %collective-permute-start.5 = (bf16[2,32,2048]{2,1,0:T(8,128)(2,1)}, bf16[2,32,2048]{2,1,0:T(8,128)(2,1)S(1)}, u32[]{:S(2)}, u32[]{:S(2)}) collective-permute-start(bf16[2,32,2048]{2,1,0:T(8,128)(2,1)} %bitcast.29), channel_id=1, source_target_pairs={{0,2},{2,0},{1,3},{3,1},{4,6},{6,4},{5,7},{7,5},{8,10},{10,8},{9,1... | collective-permute-start | bytes 786440 | tf_op jit(solution)/shard_map/ppermute | solution.py:370
  4.0 9.9 %collective-permute-start.1 = (bf16[2,32,1024]{2,1,0:T(8,128)(2,1)S(1)}, bf16[2,32,1024]{2,1,0:T(8,128)(2,1)S(1)}, u32[]{:S(2)}, u32[]{:S(2)}) collective-permute-start(bf16[2,32,1024]{2,1,0:T(8,128)(2,1)S(1)} %get-tuple-element.47), channel_id=1, source_target_pairs={{0,1},{1,0},{2,65},{3,64},{4,17},{5,16},{6,81},{7,80},{8,33},{9,32... | collective-permute-start | bytes 393224 | tf_op jit(solution)/shard_map/ppermute | solution.py:369
  4.1 9.8 %collective-permute-start = (bf16[2,32,1024]{2,1,0:T(8,128)(2,1)S(1)}, bf16[2,32,1024]{2,1,0:T(8,128)(2,1)S(1)}, u32[]{:S(2)}, u32[]{:S(2)}) collective-permute-start(bf16[2,32,1024]{2,1,0:T(8,128)(2,1)S(1)} %get-tuple-element.46), channel_id=1, source_target_pairs={{0,0},{1,1},{2,64},{3,65},{4,16},{5,17},{6,80},{7,81},{8,32},{9,33... | collective-permute-start | bytes 393224 | tf_op jit(solution)/shard_map/ppermute | solution.py:368
  9.1 26.1 %collective-permute-start.6 = (bf16[2,2,32,2048]{3,2,1,0:T(8,128)(2,1)S(1)}, bf16[2,2,32,2048]{3,2,1,0:T(8,128)(2,1)S(1)}, u32[]{:S(2)}, u32[]{:S(2)}) collective-permute-start(bf16[2,2,32,2048]{3,2,1,0:T(8,128)(2,1)S(1)} %get-tuple-element.45.own), channel_id=1, source_target_pairs={{0,4},{4,8},{8,12},{12,0},{1,5},{5,9},{9,13},{13,1},{2,6},{6,10},{... | collective-permute-start | bytes 1572872 | tf_op jit(solution)/shard_map/ppermute | solution.py:374
  11.0 24.2 %collective-permute-start.7 = (bf16[2,2,32,2048]{3,2,1,0:T(8,128)(2,1)S(1)}, bf16[2,2,32,2048]{3,2,1,0:T(8,128)(2,1)S(1)}, u32[]{:S(2)}, u32[]{:S(2)}) collective-permute-start(bf16[2,2,32,2048]{3,2,1,0:T(8,128)(2,1)S(1)} %get-tuple-element.45.own), channel_id=1, source_target_pairs={{0,12},{4,0},{8,4},{12,8},{1,13},{5,1},{9,5},{13,9},{2,14},{6,2},{... | collective-permute-start | bytes 1572872 | tf_op jit(solution)/shard_map/ppermute | solution.py:375
  14.0 18.9 %collective-permute-start.2 = (bf16[2,2,32,1024]{3,2,1,0:T(8,128)(2,1)S(1)}, bf16[2,2,32,1024]{3,2,1,0:T(8,128)(2,1)S(1)}, u32[]{:S(2)}, u32[]{:S(2)}) collective-permute-start(bf16[2,2,32,1024]{3,2,1,0:T(8,128)(2,1)S(1)} %pad_maximum_fusion.2.own), channel_id=1, source_target_pairs={{0,64},{64,0},{1,65},{65,1},{2,66},{66,2},{3,67},{67,3},{4,68},{68... | collective-permute-start | bytes 786440 | tf_op jit(solution)/shard_map/ppermute | solution.py:378
  19.4 15.8 %collective-permute-start.3 = (bf16[2,2,32,1024]{3,2,1,0:T(8,128)(2,1)S(1)}, bf16[2,2,32,1024]{3,2,1,0:T(8,128)(2,1)S(1)}, u32[]{:S(2)}, u32[]{:S(2)}) collective-permute-start(bf16[2,2,32,1024]{3,2,1,0:T(8,128)(2,1)S(1)} %pad_maximum_fusion.2.own), channel_id=1, source_target_pairs={{0,16},{16,32},{32,48},{48,0},{1,17},{17,33},{33,49},{49,1},{2,18}... | collective-permute-start | bytes 786440 | tf_op jit(solution)/shard_map/ppermute | solution.py:376
  22.6 12.6 %collective-permute-start.4 = (bf16[2,2,32,1024]{3,2,1,0:T(8,128)(2,1)S(1)}, bf16[2,2,32,1024]{3,2,1,0:T(8,128)(2,1)S(1)}, u32[]{:S(2)}, u32[]{:S(2)}) collective-permute-start(bf16[2,2,32,1024]{3,2,1,0:T(8,128)(2,1)S(1)} %pad_maximum_fusion.2.own), channel_id=1, source_target_pairs={{0,48},{16,0},{32,16},{48,32},{1,49},{17,1},{33,17},{49,33},{2,50}... | collective-permute-start | bytes 786440 | tf_op jit(solution)/shard_map/ppermute | solution.py:377
  35.4 16.6 %collective-permute-start.12 = (bf16[3,2,2,32,2048]{4,3,2,1,0:T(8,128)(2,1)S(1)}, bf16[3,2,2,32,2048]{4,3,2,1,0:T(8,128)(2,1)S(1)}, u32[]{:S(2)}, u32[]{:S(2)}) collective-permute-start(bf16[3,2,2,32,2048]{4,3,2,1,0:T(8,128)(2,1)S(1)} %pad_maximum_fusion), channel_id=1, source_target_pairs={{0,1},{1,0},{2,3},{3,2},{4,5},{5,4},{6,7},{7,6},{8,9},{9,8},{10,11... | collective-permute-start | bytes 4718600 | tf_op jit(solution)/shard_map/ppermute | solution.py:394
  35.5 9.9 %collective-permute-start.10 = (bf16[2,2,32,1024]{3,2,1,0:T(8,128)(2,1)S(1)}, bf16[2,2,32,1024]{3,2,1,0:T(8,128)(2,1)S(1)}, u32[]{:S(2)}, u32[]{:S(2)}) collective-permute-start(bf16[2,2,32,1024]{3,2,1,0:T(8,128)(2,1)S(1)} %collective-permute-done.2.near), channel_id=1, source_target_pairs={{0,16},{16,32},{32,48},{48,0},{1,17},{17,33},{33,49},{49,1},{2,18}... | collective-permute-start | bytes 786440 | tf_op jit(solution)/shard_map/ppermute | solution.py:397
  36.7 8.7 %collective-permute-start.11 = (bf16[2,2,32,1024]{3,2,1,0:T(8,128)(2,1)S(1)}, bf16[2,2,32,1024]{3,2,1,0:T(8,128)(2,1)S(1)}, u32[]{:S(2)}, u32[]{:S(2)}) collective-permute-start(bf16[2,2,32,1024]{3,2,1,0:T(8,128)(2,1)S(1)} %collective-permute-done.2.near), channel_id=1, source_target_pairs={{0,48},{16,0},{32,16},{48,32},{1,49},{17,1},{33,17},{49,33},{2,50}... | collective-permute-start | bytes 786440 | tf_op jit(solution)/shard_map/ppermute | solution.py:398
  38.9 9.4 %collective-permute-start.8 = (bf16[2,32,2048]{2,1,0:T(8,128)(2,1)S(1)}, bf16[2,32,2048]{2,1,0:T(8,128)(2,1)S(1)}, u32[]{:S(2)}, u32[]{:S(2)}) collective-permute-start(bf16[2,32,2048]{2,1,0:T(8,128)(2,1)S(1)} %slice_bitcast_fusion.1), channel_id=1, source_target_pairs={{0,4},{4,8},{8,12},{12,0},{1,5},{5,9},{9,13},{13,1},{2,6},{6,10},{... | collective-permute-start | bytes 786440 | tf_op jit(solution)/shard_map/ppermute | solution.py:395
  39.0 9.3 %collective-permute-start.9 = (bf16[2,32,2048]{2,1,0:T(8,128)(2,1)S(1)}, bf16[2,32,2048]{2,1,0:T(8,128)(2,1)S(1)}, u32[]{:S(2)}, u32[]{:S(2)}) collective-permute-start(bf16[2,32,2048]{2,1,0:T(8,128)(2,1)S(1)} %slice_bitcast_fusion), channel_id=1, source_target_pairs={{0,12},{4,0},{8,4},{12,8},{1,13},{5,1},{9,5},{13,9},{2,14},{6,2},{... | collective-permute-start | bytes 786440 | tf_op jit(solution)/shard_map/ppermute | solution.py:396
  48.2 3.8 %collective-permute-start.13 = (bf16[2,32,2048]{2,1,0:T(8,128)(2,1)S(1)}, bf16[2,32,2048]{2,1,0:T(8,128)(2,1)S(1)}, u32[]{:S(2)}, u32[]{:S(2)}) collective-permute-start(bf16[2,32,2048]{2,1,0:T(8,128)(2,1)S(1)} %collective-permute-done.8.g_far_a), channel_id=1, source_target_pairs={{0,1},{1,0},{2,3},{3,2},{4,5},{5,4},{6,7},{7,6},{8,9},{9,8},{10,11... | collective-permute-start | bytes 786440 | tf_op jit(solution)/shard_map/ppermute | solution.py:414
  48.2 3.8 %collective-permute-start.14 = (bf16[2,32,2048]{2,1,0:T(8,128)(2,1)S(1)}, bf16[2,32,2048]{2,1,0:T(8,128)(2,1)S(1)}, u32[]{:S(2)}, u32[]{:S(2)}) collective-permute-start(bf16[2,32,2048]{2,1,0:T(8,128)(2,1)S(1)} %collective-permute-done.9.g_far_b), channel_id=1, source_target_pairs={{0,1},{1,0},{2,3},{3,2},{4,5},{5,4},{6,7},{7,6},{8,9},{9,8},{10,11... | collective-permute-start | bytes 786440 | tf_op jit(solution)/shard_map/ppermute | solution.py:415
  48.7 9.4 %collective-permute-start.15 = (bf16[2,2,32,1024]{3,2,1,0:T(8,128)(2,1)S(1)}, bf16[2,2,32,1024]{3,2,1,0:T(8,128)(2,1)S(1)}, u32[]{:S(2)}, u32[]{:S(2)}) collective-permute-start(bf16[2,2,32,1024]{3,2,1,0:T(8,128)(2,1)S(1)} %collective-permute-done.3.after), channel_id=1, source_target_pairs={{0,16},{16,32},{32,48},{48,0},{1,17},{17,33},{33,49},{49,1},{2,18}... | collective-permute-start | bytes 786440 | tf_op jit(solution)/shard_map/ppermute | solution.py:399
  48.7 9.4 %collective-permute-start.16 = (bf16[2,2,32,1024]{3,2,1,0:T(8,128)(2,1)S(1)}, bf16[2,2,32,1024]{3,2,1,0:T(8,128)(2,1)S(1)}, u32[]{:S(2)}, u32[]{:S(2)}) collective-permute-start(bf16[2,2,32,1024]{3,2,1,0:T(8,128)(2,1)S(1)} %collective-permute-done.11.near_before), channel_id=1, source_target_pairs={{0,48},{16,0},{32,16},{48,32},{1,49},{17,1},{33,17},{49,33},{2,50}... | collective-permute-start | bytes 786440 | tf_op jit(solution)/shard_map/ppermute | solution.py:416
  63.8 2.0 %collective-permute-start.17 = (bf16[64,8,512]{2,1,0:T(8,128)(2,1)S(1)}, bf16[64,8,512]{2,1,0:T(8,128)(2,1)S(1)}, u32[]{:S(2)}, u32[]{:S(2)}) collective-permute-start(bf16[64,8,512]{2,1,0:T(8,128)(2,1)S(1)} %get-tuple-element.36), channel_id=1, source_target_pairs={{0,1},{1,0},{2,3},{3,2},{4,5},{5,4},{6,7},{7,6},{8,9},{9,8},{10,11... | collective-permute-start | bytes 1572872 | tf_op jit(solution)/shard_map/ppermute | solution.py:448

commit v7 on v6

--- a/solution.py
+++ b/solution.py
@@ -306,15 +306,15 @@
 
 def align_kernel(index, parts, out):
     total = jnp.sum(parts[...].astype(jnp.float32), axis=0)
-    lane = lax.broadcasted_iota(jnp.int32, (1, P_SIZE), 1)
-    for i in range(4):
-        re = total[i : i + 1]
-        im = total[4 + i : 5 + i]
-        chosen = lane == index[i]
-        anchor_re = jnp.sum(jnp.where(chosen, re, 0.0), axis=1, keepdims=True)
-        anchor_im = jnp.sum(jnp.where(chosen, im, 0.0), axis=1, keepdims=True)
-        out[i, 0:1, :] = re * anchor_re + im * anchor_im
-        out[i, 1:2, :] = im * anchor_re - re * anchor_im
+    re = total[:4]
+    im = total[4:]
+    row = lax.broadcasted_iota(jnp.int32, (4, P_SIZE), 0)
+    target = jnp.where(row < 2, jnp.where(row == 0, index[0], index[1]), jnp.where(row == 2, index[2], index[3]))
+    chosen = lax.broadcasted_iota(jnp.int32, (4, P_SIZE), 1) == target
+    anchor_re = jnp.sum(jnp.where(chosen, re, 0.0), axis=1, keepdims=True)
+    anchor_im = jnp.sum(jnp.where(chosen, im, 0.0), axis=1, keepdims=True)
+    out[:, 0, :] = re * anchor_re + im * anchor_im
+    out[:, 1, :] = im * anchor_re - re * anchor_im
 
 
 def any_spec():

time: 89.3 us -> 89.2 us (level)
  transfers between devices with their start and end apart: 18 -> 18, of which waited for: 6 -> 6; matrix products, arithmetic and copies ran while one was open for 5% -> 5% of each run, Pallas kernels for 10% -> 9%
where the time goes in v7:
time: 89.2 us; the launch traced here: 89 us
  starting transfers between devices  32.7 us (37%)
  blocking collectives  21.2 us (24%)
  Pallas kernels  15.8 us (18%)
  waiting for transfers between devices  14 us (16%)
  other arithmetic  3.1 us (3%)
  local copies, waits for them, and re-layouts  2.01 us (2%)
    all_to_all x1, blocking collectives, body(): parts = lax.all_to_all(summed, CHIPS, 0, 0)  21.2 us
    ppermute x1, starting transfers between devices, body(): before = lax.ppermute(own, 'z', ring(-1))  6.37 us
    pallas_call x1, Pallas kernels, body(): pl.pallas_call(finish_kernel, out_shape=(gbuf_shape, block, block), in_sp...  5.66 us
    ppermute x1, starting transfers between devices, body(): near = lax.ppermute(own, 'xh', SWAP)  5.47 us
    pallas_call x1, Pallas kernels, body(): pl.pallas_call(rest_kernel, out_shape=(fb_shape, gbuf_shape), in_specs=[s...  3.77 us
    ppermute x1, waiting for transfers between devices, body(): beside = lax.ppermute(lines, 'xl', SWAP)  3.32 us
    ppermute x1, starting transfers between devices, body(): g_far_b = lax.ppermute(g_before[1], 'y', ring(-1))  3.29 us
    ppermute x1, starting transfers between devices, body(): far_b = lax.ppermute(near_before, 'z', ring(-1))  3.23 us
  transfers between devices with their start and end apart: 18, of which 6 were waited for; matrix products, arithmetic and copies ran while one was open for 5% of the time, Pallas kernels for 9%

profile of v7, /device:TPU:0, one launch (start us, length us, event | category | flops | bytes accessed | tf_op | source)
XLA Modules:
  0.0 89.0 jit_solution(4078362218665486093)
XLA Ops:
  0.0 1.6 %collective-permute-start.5 = (bf16[2,32,2048]{2,1,0:T(8,128)(2,1)}, bf16[2,32,2048]{2,1,0:T(8,128)(2,1)S(1)}, u32[]{:S(2)}, u32[]{:S(2)}) collective-permute-start(bf16[2,32,2048]{2,1,0:T(8,128)(2,1)} %bitcast.29), channel_id=1, source_target_pairs={{0,2},{2,0},{1,3},{3,1},{4,6},{6,4},{5,7},{7,5},{8,10},{10,8},{9,1... | collective-permute-start | bytes 786440 | tf_op jit(solution)/shard_map/ppermute | solution.py:370
  3.0 1.0 %dynamic-slice_bitcast_fusion.1 = (bf16[2,32,1024]{2,1,0:T(8,128)(2,1)S(1)}, bf16[2,32,1024]{2,1,0:T(8,128)(2,1)S(1)}) fusion(bf16[2,2048,32]{1,2,0:T(8,128)(2,1)} %param.5, s32[]{:T(128)S(6)} %select_n.19, s32[]{:T(128)S(6)} %select_n.20), kind=kLoop, calls=%fused_computation.7 | loop fusion | bytes 524296 | tf_op jit(solution)/shard_map/dynamic_slice | solution.py:366
  4.8 3.3 %collective-permute-done.5 = bf16[2,32,2048]{2,1,0:T(8,128)(2,1)S(1)} collective-permute-done((bf16[2,32,2048]{2,1,0:T(8,128)(2,1)}, bf16[2,32,2048]{2,1,0:T(8,128)(2,1)S(1)}, u32[]{:S(2)}, u32[]{:S(2)}) %collective-permute-start.5) | collective-permute-done | bytes 262176 | tf_op jit(solution)/shard_map/ppermute | solution.py:370
  8.1 1.0 %fusion.8 = (bf16[1,2,2,32,2048]{4,3,2,1,0:T(8,128)(2,1)S(1)}, bf16[2,2,32,2048]{3,2,1,0:T(8,128)(2,1)S(1)}) fusion(bf16[1,2,32,2048]{3,2,1,0:T(8,128)(2,1)S(1)} %bitcast.31, bf16[1,2,32,2048]{3,2,1,0:T(8,128)(2,1)} %bitcast.30), kind=kLoop, calls=%fused_computation.27 | loop fusion | flops 262144 | bytes 1572864 | tf_op jit(solution)/shard_map/stack | solution.py:394
  9.1 1.9 %collective-permute-start.6 = (bf16[2,2,32,2048]{3,2,1,0:T(8,128)(2,1)S(1)}, bf16[2,2,32,2048]{3,2,1,0:T(8,128)(2,1)S(1)}, u32[]{:S(2)}, u32[]{:S(2)}) collective-permute-start(bf16[2,2,32,2048]{3,2,1,0:T(8,128)(2,1)S(1)} %get-tuple-element.45.own), channel_id=1, source_target_pairs={{0,4},{4,8},{8,12},{12,0},{1,5},{5,9},{9,13},{13,1},{2,6},{6,10},{... | collective-permute-start | bytes 1572872 | tf_op jit(solution)/shard_map/ppermute | solution.py:374
  11.0 2.9 %collective-permute-start.7 = (bf16[2,2,32,2048]{3,2,1,0:T(8,128)(2,1)S(1)}, bf16[2,2,32,2048]{3,2,1,0:T(8,128)(2,1)S(1)}, u32[]{:S(2)}, u32[]{:S(2)}) collective-permute-start(bf16[2,2,32,2048]{3,2,1,0:T(8,128)(2,1)S(1)} %get-tuple-element.45.own), channel_id=1, source_target_pairs={{0,12},{4,0},{8,4},{12,8},{1,13},{5,1},{9,5},{13,9},{2,14},{6,2},{... | collective-permute-start | bytes 1572872 | tf_op jit(solution)/shard_map/ppermute | solution.py:375
  14.0 5.5 %collective-permute-start.2 = (bf16[2,2,32,1024]{3,2,1,0:T(8,128)(2,1)S(1)}, bf16[2,2,32,1024]{3,2,1,0:T(8,128)(2,1)S(1)}, u32[]{:S(2)}, u32[]{:S(2)}) collective-permute-start(bf16[2,2,32,1024]{3,2,1,0:T(8,128)(2,1)S(1)} %pad_maximum_fusion.2.own), channel_id=1, source_target_pairs={{0,64},{64,0},{1,65},{65,1},{2,66},{66,2},{3,67},{67,3},{4,68},{68... | collective-permute-start | bytes 786440 | tf_op jit(solution)/shard_map/ppermute | solution.py:378
  19.4 3.2 %collective-permute-start.3 = (bf16[2,2,32,1024]{3,2,1,0:T(8,128)(2,1)S(1)}, bf16[2,2,32,1024]{3,2,1,0:T(8,128)(2,1)S(1)}, u32[]{:S(2)}, u32[]{:S(2)}) collective-permute-start(bf16[2,2,32,1024]{3,2,1,0:T(8,128)(2,1)S(1)} %pad_maximum_fusion.2.own), channel_id=1, source_target_pairs={{0,16},{16,32},{32,48},{48,0},{1,17},{17,33},{33,49},{49,1},{2,18}... | collective-permute-start | bytes 786440 | tf_op jit(solution)/shard_map/ppermute | solution.py:376
  22.6 6.4 %collective-permute-start.4 = (bf16[2,2,32,1024]{3,2,1,0:T(8,128)(2,1)S(1)}, bf16[2,2,32,1024]{3,2,1,0:T(8,128)(2,1)S(1)}, u32[]{:S(2)}, u32[]{:S(2)}) collective-permute-start(bf16[2,2,32,1024]{3,2,1,0:T(8,128)(2,1)S(1)} %pad_maximum_fusion.2.own), channel_id=1, source_target_pairs={{0,48},{16,0},{32,16},{48,32},{1,49},{17,1},{33,17},{49,33},{2,50}... | collective-permute-start | bytes 786440 | tf_op jit(solution)/shard_map/ppermute | solution.py:377
  30.3 2.5 %load.1.abuf = bf16[4,2,2304,256]{3,2,1,0:T(8,128)(2,1)S(1)} custom-call(s32[54]{0:T(128)S(1)} %concatenate.3.st, bf16[2,2048,1024]{2,1,0:T(8,128)(2,1)} %a.1), custom_call_target="tpu_custom_call" | custom-call | bytes 8388608 | tf_op jit(solution)/shard_map/load/pallas_call | solution.py:381
  32.8 2.5 %collective-permute-done.3.after = bf16[2,2,32,1024]{3,2,1,0:T(8,128)(2,1)S(1)} collective-permute-done((bf16[2,2,32,1024]{3,2,1,0:T(8,128)(2,1)S(1)}, bf16[2,2,32,1024]{3,2,1,0:T(8,128)(2,1)S(1)}, u32[]{:S(2)}, u32[]{:S(2)}) %collective-permute-start.3) | collective-permute-done | bytes 262176 | tf_op jit(solution)/shard_map/ppermute | solution.py:376
  35.5 1.2 %collective-permute-start.10 = (bf16[2,2,32,1024]{3,2,1,0:T(8,128)(2,1)S(1)}, bf16[2,2,32,1024]{3,2,1,0:T(8,128)(2,1)S(1)}, u32[]{:S(2)}, u32[]{:S(2)}) collective-permute-start(bf16[2,2,32,1024]{3,2,1,0:T(8,128)(2,1)S(1)} %collective-permute-done.2.near), channel_id=1, source_target_pairs={{0,16},{16,32},{32,48},{48,0},{1,17},{17,33},{33,49},{49,1},{2,18}... | collective-permute-start | bytes 786440 | tf_op jit(solution)/shard_map/ppermute | solution.py:397
  36.7 2.1 %collective-permute-start.11 = (bf16[2,2,32,1024]{3,2,1,0:T(8,128)(2,1)S(1)}, bf16[2,2,32,1024]{3,2,1,0:T(8,128)(2,1)S(1)}, u32[]{:S(2)}, u32[]{:S(2)}) collective-permute-start(bf16[2,2,32,1024]{3,2,1,0:T(8,128)(2,1)S(1)} %collective-permute-done.2.near), channel_id=1, source_target_pairs={{0,48},{16,0},{32,16},{48,32},{1,49},{17,1},{33,17},{49,33},{2,50}... | collective-permute-start | bytes 786440 | tf_op jit(solution)/shard_map/ppermute | solution.py:398
  39.0 3.3 %collective-permute-start.9 = (bf16[2,32,2048]{2,1,0:T(8,128)(2,1)S(1)}, bf16[2,32,2048]{2,1,0:T(8,128)(2,1)S(1)}, u32[]{:S(2)}, u32[]{:S(2)}) collective-permute-start(bf16[2,32,2048]{2,1,0:T(8,128)(2,1)S(1)} %slice_bitcast_fusion), channel_id=1, source_target_pairs={{0,12},{4,0},{8,4},{12,8},{1,13},{5,1},{9,5},{13,9},{2,14},{6,2},{... | collective-permute-start | bytes 786440 | tf_op jit(solution)/shard_map/ppermute | solution.py:396
  42.3 2.1 %near.1.fb_in = bf16[4,512,1024]{2,1,0:T(8,128)(2,1)S(1)} custom-call(s32[54]{0:T(128)S(1)} %concatenate.3.st, bf16[4,2,2304,256]{3,2,1,0:T(8,128)(2,1)S(1)} %load.1.abuf, bf16[2,2,32,2048]{3,2,1,0:T(8,128)(2,1)S(1)} %get-tuple-element.45.own, bf16[2,2,32,2048]{3,2,1,0:T(8,128)(2,1)S(1)} %collective-permute-done.6.after, ...), custom_call_target="tpu_custom_call" | custom-call | flops 3221225472 | bytes 8388608 | tf_op jit(solution)/shard_map/near/pallas_call | solution.py:400
  44.4 1.1 %collective-permute-done.10.near_after = bf16[2,2,32,1024]{3,2,1,0:T(8,128)(2,1)S(1)} collective-permute-done((bf16[2,2,32,1024]{3,2,1,0:T(8,128)(2,1)S(1)}, bf16[2,2,32,1024]{3,2,1,0:T(8,128)(2,1)S(1)}, u32[]{:S(2)}, u32[]{:S(2)}) %collective-permute-start.10) | collective-permute-done | bytes 262176 | tf_op jit(solution)/shard_map/ppermute | solution.py:397
  45.5 2.8 %collective-permute-done.8.g_far_a = bf16[2,32,2048]{2,1,0:T(8,128)(2,1)S(1)} collective-permute-done((bf16[2,32,2048]{2,1,0:T(8,128)(2,1)S(1)}, bf16[2,32,2048]{2,1,0:T(8,128)(2,1)S(1)}, u32[]{:S(2)}, u32[]{:S(2)}) %collective-permute-start.8) | collective-permute-done | bytes 262176 | tf_op jit(solution)/shard_map/ppermute | solution.py:395
  48.7 3.2 %collective-permute-start.16 = (bf16[2,2,32,1024]{3,2,1,0:T(8,128)(2,1)S(1)}, bf16[2,2,32,1024]{3,2,1,0:T(8,128)(2,1)S(1)}, u32[]{:S(2)}, u32[]{:S(2)}) collective-permute-start(bf16[2,2,32,1024]{3,2,1,0:T(8,128)(2,1)S(1)} %collective-permute-done.11.near_before), channel_id=1, source_target_pairs={{0,48},{16,0},{32,16},{48,32},{1,49},{17,1},{33,17},{49,33},{2,50}... | collective-permute-start | bytes 786440 | tf_op jit(solution)/shard_map/ppermute | solution.py:416
  52.0 3.8 %rest.1 = (bf16[4,512,1024]{2,1,0:T(8,128)(2,1)S(1)}, bf16[2,512,1024]{2,1,0:T(8,128)(2,1)S(1)}) custom-call(s32[54]{0:T(128)S(1)} %concatenate.3.st, bf16[4,2,2304,256]{3,2,1,0:T(8,128)(2,1)S(1)} %load.1.abuf, bf16[4,512,1024]{2,1,0:T(8,128)(2,1)S(1)} %near.1.fb_in, ...), custom_call_target="tpu_custom_call", output_to_operand_aliasing={{0}: (2, {})} | custom-call | flops 5368709120 | bytes 8388608 | tf_op jit(solution)/shard_map/rest/pallas_call | solution.py:418
  55.8 2.4 %collective-permute-done.15.far_a = bf16[2,2,32,1024]{3,2,1,0:T(8,128)(2,1)S(1)} collective-permute-done((bf16[2,2,32,1024]{3,2,1,0:T(8,128)(2,1)S(1)}, bf16[2,2,32,1024]{3,2,1,0:T(8,128)(2,1)S(1)}, u32[]{:S(2)}, u32[]{:S(2)}) %collective-permute-start.15) | collective-permute-done | bytes 262176 | tf_op jit(solution)/shard_map/ppermute | solution.py:399
  58.2 5.7 %finish.1 = (bf16[2,512,1024]{2,1,0:T(8,128)(2,1)S(1)}, bf16[64,8,512]{2,1,0:T(8,128)(2,1)S(1)}, bf16[64,8,512]{2,1,0:T(8,128)(2,1)S(1)}) custom-call(s32[54]{0:T(128)S(1)} %concatenate.3.st, bf16[4,512,1024]{2,1,0:T(8,128)(2,1)S(1)} %get-tuple-element.33.fb, bf16[2,512,1024]{2,1,0:T(8,128)(2,1)S(1)} %get-tuple-element.34.gbuf_in, ...), custom_call_target="tpu_custom_call", output_to_operand_aliasing={{0}: (2, {})} | custom-call | flops 4294967296 | bytes 8388608 | tf_op jit(solution)/shard_map/finish/pallas_call | solution.py:437
  63.9 1.9 %collective-permute-done.17 = bf16[64,8,512]{2,1,0:T(8,128)(2,1)S(1)} collective-permute-done((bf16[64,8,512]{2,1,0:T(8,128)(2,1)S(1)}, bf16[64,8,512]{2,1,0:T(8,128)(2,1)S(1)}, u32[]{:S(2)}, u32[]{:S(2)}) %collective-permute-start.17) | collective-permute-done | bytes 524320 | tf_op jit(solution)/shard_map/ppermute | solution.py:448
  66.0 21.2 %all_to_all.5.parts = bf16[64,8,512]{2,1,0:T(8,128)(2,1)} all-to-all(bf16[64,8,512]{2,1,0:T(8,128)(2,1)S(1)} %add_convert_fusion), channel_id=1, replica_groups=mesh['xh'=2,'z'=4,'y'=4,'xl'=2,'core'=2] {'xh','z','y','xl'}, dimensions={0} | all-to-all | bytes 1048576 | tf_op jit(solution)/shard_map/all_to_all | solution.py:450
  87.1 1.8 %align.1 = f32[4,2,512]{2,1,0:T(2,128)} custom-call(s32[4]{0:T(128)} %index.1, bf16[64,8,512]{2,1,0:T(8,128)(2,1)} %all_to_all.5.parts), custom_call_target="tpu_custom_call" | custom-call | tf_op jit(solution)/shard_map/align/pallas_call | solution.py:451
  (37 shorter events, 4.6 us)
Async XLA Ops:
  0.0 8.1 %collective-permute-start.5 = (bf16[2,32,2048]{2,1,0:T(8,128)(2,1)}, bf16[2,32,2048]{2,1,0:T(8,128)(2,1)S(1)}, u32[]{:S(2)}, u32[]{:S(2)}) collective-permute-start(bf16[2,32,2048]{2,1,0:T(8,128)(2,1)} %bitcast.29), channel_id=1, source_target_pairs={{0,2},{2,0},{1,3},{3,1},{4,6},{6,4},{5,7},{7,5},{8,10},{10,8},{9,1... | collective-permute-start | bytes 786440 | tf_op jit(solution)/shard_map/ppermute | solution.py:370
  4.0 9.9 %collective-permute-start.1 = (bf16[2,32,1024]{2,1,0:T(8,128)(2,1)S(1)}, bf16[2,32,1024]{2,1,0:T(8,128)(2,1)S(1)}, u32[]{:S(2)}, u32[]{:S(2)}) collective-permute-start(bf16[2,32,1024]{2,1,0:T(8,128)(2,1)S(1)} %get-tuple-element.47), channel_id=1, source_target_pairs={{0,1},{1,0},{2,65},{3,64},{4,17},{5,16},{6,81},{7,80},{8,33},{9,32... | collective-permute-start | bytes 393224 | tf_op jit(solution)/shard_map/ppermute | solution.py:369
  4.1 9.8 %collective-permute-start = (bf16[2,32,1024]{2,1,0:T(8,128)(2,1)S(1)}, bf16[2,32,1024]{2,1,0:T(8,128)(2,1)S(1)}, u32[]{:S(2)}, u32[]{:S(2)}) collective-permute-start(bf16[2,32,1024]{2,1,0:T(8,128)(2,1)S(1)} %get-tuple-element.46), channel_id=1, source_target_pairs={{0,0},{1,1},{2,64},{3,65},{4,16},{5,17},{6,80},{7,81},{8,32},{9,33... | collective-permute-start | bytes 393224 | tf_op jit(solution)/shard_map/ppermute | solution.py:368
  9.1 26.1 %collective-permute-start.6 = (bf16[2,2,32,2048]{3,2,1,0:T(8,128)(2,1)S(1)}, bf16[2,2,32,2048]{3,2,1,0:T(8,128)(2,1)S(1)}, u32[]{:S(2)}, u32[]{:S(2)}) collective-permute-start(bf16[2,2,32,2048]{3,2,1,0:T(8,128)(2,1)S(1)} %get-tuple-element.45.own), channel_id=1, source_target_pairs={{0,4},{4,8},{8,12},{12,0},{1,5},{5,9},{9,13},{13,1},{2,6},{6,10},{... | collective-permute-start | bytes 1572872 | tf_op jit(solution)/shard_map/ppermute | solution.py:374
  11.0 24.2 %collective-permute-start.7 = (bf16[2,2,32,2048]{3,2,1,0:T(8,128)(2,1)S(1)}, bf16[2,2,32,2048]{3,2,1,0:T(8,128)(2,1)S(1)}, u32[]{:S(2)}, u32[]{:S(2)}) collective-permute-start(bf16[2,2,32,2048]{3,2,1,0:T(8,128)(2,1)S(1)} %get-tuple-element.45.own), channel_id=1, source_target_pairs={{0,12},{4,0},{8,4},{12,8},{1,13},{5,1},{9,5},{13,9},{2,14},{6,2},{... | collective-permute-start | bytes 1572872 | tf_op jit(solution)/shard_map/ppermute | solution.py:375
  14.0 18.8 %collective-permute-start.2 = (bf16[2,2,32,1024]{3,2,1,0:T(8,128)(2,1)S(1)}, bf16[2,2,32,1024]{3,2,1,0:T(8,128)(2,1)S(1)}, u32[]{:S(2)}, u32[]{:S(2)}) collective-permute-start(bf16[2,2,32,1024]{3,2,1,0:T(8,128)(2,1)S(1)} %pad_maximum_fusion.2.own), channel_id=1, source_target_pairs={{0,64},{64,0},{1,65},{65,1},{2,66},{66,2},{3,67},{67,3},{4,68},{68... | collective-permute-start | bytes 786440 | tf_op jit(solution)/shard_map/ppermute | solution.py:378
  19.4 15.8 %collective-permute-start.3 = (bf16[2,2,32,1024]{3,2,1,0:T(8,128)(2,1)S(1)}, bf16[2,2,32,1024]{3,2,1,0:T(8,128)(2,1)S(1)}, u32[]{:S(2)}, u32[]{:S(2)}) collective-permute-start(bf16[2,2,32,1024]{3,2,1,0:T(8,128)(2,1)S(1)} %pad_maximum_fusion.2.own), channel_id=1, source_target_pairs={{0,16},{16,32},{32,48},{48,0},{1,17},{17,33},{33,49},{49,1},{2,18}... | collective-permute-start | bytes 786440 | tf_op jit(solution)/shard_map/ppermute | solution.py:376
  22.6 12.6 %collective-permute-start.4 = (bf16[2,2,32,1024]{3,2,1,0:T(8,128)(2,1)S(1)}, bf16[2,2,32,1024]{3,2,1,0:T(8,128)(2,1)S(1)}, u32[]{:S(2)}, u32[]{:S(2)}) collective-permute-start(bf16[2,2,32,1024]{3,2,1,0:T(8,128)(2,1)S(1)} %pad_maximum_fusion.2.own), channel_id=1, source_target_pairs={{0,48},{16,0},{32,16},{48,32},{1,49},{17,1},{33,17},{49,33},{2,50}... | collective-permute-start | bytes 786440 | tf_op jit(solution)/shard_map/ppermute | solution.py:377
  35.4 16.6 %collective-permute-start.12 = (bf16[3,2,2,32,2048]{4,3,2,1,0:T(8,128)(2,1)S(1)}, bf16[3,2,2,32,2048]{4,3,2,1,0:T(8,128)(2,1)S(1)}, u32[]{:S(2)}, u32[]{:S(2)}) collective-permute-start(bf16[3,2,2,32,2048]{4,3,2,1,0:T(8,128)(2,1)S(1)} %pad_maximum_fusion), channel_id=1, source_target_pairs={{0,1},{1,0},{2,3},{3,2},{4,5},{5,4},{6,7},{7,6},{8,9},{9,8},{10,11... | collective-permute-start | bytes 4718600 | tf_op jit(solution)/shard_map/ppermute | solution.py:394
  35.5 9.9 %collective-permute-start.10 = (bf16[2,2,32,1024]{3,2,1,0:T(8,128)(2,1)S(1)}, bf16[2,2,32,1024]{3,2,1,0:T(8,128)(2,1)S(1)}, u32[]{:S(2)}, u32[]{:S(2)}) collective-permute-start(bf16[2,2,32,1024]{3,2,1,0:T(8,128)(2,1)S(1)} %collective-permute-done.2.near), channel_id=1, source_target_pairs={{0,16},{16,32},{32,48},{48,0},{1,17},{17,33},{33,49},{49,1},{2,18}... | collective-permute-start | bytes 786440 | tf_op jit(solution)/shard_map/ppermute | solution.py:397
  36.7 8.7 %collective-permute-start.11 = (bf16[2,2,32,1024]{3,2,1,0:T(8,128)(2,1)S(1)}, bf16[2,2,32,1024]{3,2,1,0:T(8,128)(2,1)S(1)}, u32[]{:S(2)}, u32[]{:S(2)}) collective-permute-start(bf16[2,2,32,1024]{3,2,1,0:T(8,128)(2,1)S(1)} %collective-permute-done.2.near), channel_id=1, source_target_pairs={{0,48},{16,0},{32,16},{48,32},{1,49},{17,1},{33,17},{49,33},{2,50}... | collective-permute-start | bytes 786440 | tf_op jit(solution)/shard_map/ppermute | solution.py:398
  38.9 9.4 %collective-permute-start.8 = (bf16[2,32,2048]{2,1,0:T(8,128)(2,1)S(1)}, bf16[2,32,2048]{2,1,0:T(8,128)(2,1)S(1)}, u32[]{:S(2)}, u32[]{:S(2)}) collective-permute-start(bf16[2,32,2048]{2,1,0:T(8,128)(2,1)S(1)} %slice_bitcast_fusion.1), channel_id=1, source_target_pairs={{0,4},{4,8},{8,12},{12,0},{1,5},{5,9},{9,13},{13,1},{2,6},{6,10},{... | collective-permute-start | bytes 786440 | tf_op jit(solution)/shard_map/ppermute | solution.py:395
  39.0 9.3 %collective-permute-start.9 = (bf16[2,32,2048]{2,1,0:T(8,128)(2,1)S(1)}, bf16[2,32,2048]{2,1,0:T(8,128)(2,1)S(1)}, u32[]{:S(2)}, u32[]{:S(2)}) collective-permute-start(bf16[2,32,2048]{2,1,0:T(8,128)(2,1)S(1)} %slice_bitcast_fusion), channel_id=1, source_target_pairs={{0,12},{4,0},{8,4},{12,8},{1,13},{5,1},{9,5},{13,9},{2,14},{6,2},{... | collective-permute-start | bytes 786440 | tf_op jit(solution)/shard_map/ppermute | solution.py:396
  48.2 3.8 %collective-permute-start.13 = (bf16[2,32,2048]{2,1,0:T(8,128)(2,1)S(1)}, bf16[2,32,2048]{2,1,0:T(8,128)(2,1)S(1)}, u32[]{:S(2)}, u32[]{:S(2)}) collective-permute-start(bf16[2,32,2048]{2,1,0:T(8,128)(2,1)S(1)} %collective-permute-done.8.g_far_a), channel_id=1, source_target_pairs={{0,1},{1,0},{2,3},{3,2},{4,5},{5,4},{6,7},{7,6},{8,9},{9,8},{10,11... | collective-permute-start | bytes 786440 | tf_op jit(solution)/shard_map/ppermute | solution.py:414
  48.2 3.8 %collective-permute-start.14 = (bf16[2,32,2048]{2,1,0:T(8,128)(2,1)S(1)}, bf16[2,32,2048]{2,1,0:T(8,128)(2,1)S(1)}, u32[]{:S(2)}, u32[]{:S(2)}) collective-permute-start(bf16[2,32,2048]{2,1,0:T(8,128)(2,1)S(1)} %collective-permute-done.9.g_far_b), channel_id=1, source_target_pairs={{0,1},{1,0},{2,3},{3,2},{4,5},{5,4},{6,7},{7,6},{8,9},{9,8},{10,11... | collective-permute-start | bytes 786440 | tf_op jit(solution)/shard_map/ppermute | solution.py:415
  48.7 9.4 %collective-permute-start.15 = (bf16[2,2,32,1024]{3,2,1,0:T(8,128)(2,1)S(1)}, bf16[2,2,32,1024]{3,2,1,0:T(8,128)(2,1)S(1)}, u32[]{:S(2)}, u32[]{:S(2)}) collective-permute-start(bf16[2,2,32,1024]{3,2,1,0:T(8,128)(2,1)S(1)} %collective-permute-done.3.after), channel_id=1, source_target_pairs={{0,16},{16,32},{32,48},{48,0},{1,17},{17,33},{33,49},{49,1},{2,18}... | collective-permute-start | bytes 786440 | tf_op jit(solution)/shard_map/ppermute | solution.py:399
  48.7 9.4 %collective-permute-start.16 = (bf16[2,2,32,1024]{3,2,1,0:T(8,128)(2,1)S(1)}, bf16[2,2,32,1024]{3,2,1,0:T(8,128)(2,1)S(1)}, u32[]{:S(2)}, u32[]{:S(2)}) collective-permute-start(bf16[2,2,32,1024]{3,2,1,0:T(8,128)(2,1)S(1)} %collective-permute-done.11.near_before), channel_id=1, source_target_pairs={{0,48},{16,0},{32,16},{48,32},{1,49},{17,1},{33,17},{49,33},{2,50}... | collective-permute-start | bytes 786440 | tf_op jit(solution)/shard_map/ppermute | solution.py:416
  63.8 2.0 %collective-permute-start.17 = (bf16[64,8,512]{2,1,0:T(8,128)(2,1)S(1)}, bf16[64,8,512]{2,1,0:T(8,128)(2,1)S(1)}, u32[]{:S(2)}, u32[]{:S(2)}) collective-permute-start(bf16[64,8,512]{2,1,0:T(8,128)(2,1)S(1)} %get-tuple-element.36), channel_id=1, source_target_pairs={{0,1},{1,0},{2,3},{3,2},{4,5},{5,4},{6,7},{7,6},{8,9},{9,8},{10,11... | collective-permute-start | bytes 1572872 | tf_op jit(solution)/shard_map/ppermute | solution.py:448

commit v8 on v7

--- a/solution.py
+++ b/solution.py
@@ -308,9 +308,7 @@
     total = jnp.sum(parts[...].astype(jnp.float32), axis=0)
     re = total[:4]
     im = total[4:]
-    row = lax.broadcasted_iota(jnp.int32, (4, P_SIZE), 0)
-    target = jnp.where(row < 2, jnp.where(row == 0, index[0], index[1]), jnp.where(row == 2, index[2], index[3]))
-    chosen = lax.broadcasted_iota(jnp.int32, (4, P_SIZE), 1) == target
+    chosen = lax.broadcasted_iota(jnp.int32, (4, P_SIZE), 1) == index[:, 0:1]
     anchor_re = jnp.sum(jnp.where(chosen, re, 0.0), axis=1, keepdims=True)
     anchor_im = jnp.sum(jnp.where(chosen, im, 0.0), axis=1, keepdims=True)
     out[:, 0, :] = re * anchor_re + im * anchor_im
@@ -451,10 +449,10 @@
     return pl.pallas_call(
         align_kernel,
         out_shape=jax.ShapeDtypeStruct((4, 2, P_SIZE), jnp.float32),
-        in_specs=[smem_spec(), vmem_spec()],
+        in_specs=[vmem_spec(), vmem_spec()],
         out_specs=vmem_spec(),
         name="align",
-    )(reference_index, parts)
+    )(jnp.broadcast_to(reference_index[:, None], (4, 128)), parts)
 
 
 def solution(mesh):

time: 89.2 us -> 89.9 us (level)
  transfers between devices with their start and end apart: 18 -> 18, of which waited for: 6 -> 6; matrix products, arithmetic and copies ran while one was open for 5% -> 5% of each run, Pallas kernels for 9% -> 10%
where the time goes in v8:
time: 89.9 us; the launch traced here: 89.6 us
  starting transfers between devices  32.7 us (36%)
  blocking collectives  21.2 us (24%)
  Pallas kernels  16.6 us (18%)
  waiting for transfers between devices  13.2 us (15%)
  other arithmetic  3.13 us (3%)
  local copies, waits for them, and re-layouts  2.65 us (3%)
    all_to_all x1, blocking collectives, body(): parts = lax.all_to_all(summed, CHIPS, 0, 0)  21.2 us
    ppermute x1, starting transfers between devices, body(): before = lax.ppermute(own, 'z', ring(-1))  6.37 us
    pallas_call x1, Pallas kernels, body(): pl.pallas_call(finish_kernel, out_shape=(gbuf_shape, block, block), in_sp...  5.65 us
    ppermute x1, starting transfers between devices, body(): near = lax.ppermute(own, 'xh', SWAP)  5.47 us
    pallas_call x1, Pallas kernels, body(): pl.pallas_call(rest_kernel, out_shape=(fb_shape, gbuf_shape), in_specs=[s...  4.15 us
    ppermute x1, waiting for transfers between devices, body(): beside = lax.ppermute(lines, 'xl', SWAP)  3.3 us
    ppermute x1, starting transfers between devices, body(): g_far_b = lax.ppermute(g_before[1], 'y', ring(-1))  3.29 us
    ppermute x1, starting transfers between devices, body(): far_b = lax.ppermute(near_before, 'z', ring(-1))  3.23 us
  transfers between devices with their start and end apart: 18, of which 6 were waited for; matrix products, arithmetic and copies ran while one was open for 5% of the time, Pallas kernels for 10%

profile of v8, /device:TPU:0, one launch (start us, length us, event | category | flops | bytes accessed | tf_op | source)
XLA Modules:
  0.0 89.6 jit_solution(5644464444573432881)
XLA Ops:
  0.0 1.6 %collective-permute-start.5 = (bf16[2,32,2048]{2,1,0:T(8,128)(2,1)}, bf16[2,32,2048]{2,1,0:T(8,128)(2,1)S(1)}, u32[]{:S(2)}, u32[]{:S(2)}) collective-permute-start(bf16[2,32,2048]{2,1,0:T(8,128)(2,1)} %bitcast.29), channel_id=1, source_target_pairs={{0,2},{2,0},{1,3},{3,1},{4,6},{6,4},{5,7},{7,5},{8,10},{10,8},{9,1... | collective-permute-start | bytes 786440 | tf_op jit(solution)/shard_map/ppermute | solution.py:368
  3.0 1.0 %dynamic-slice_bitcast_fusion.1 = (bf16[2,32,1024]{2,1,0:T(8,128)(2,1)S(1)}, bf16[2,32,1024]{2,1,0:T(8,128)(2,1)S(1)}) fusion(bf16[2,2048,32]{1,2,0:T(8,128)(2,1)} %param.5, s32[]{:T(128)S(6)} %select_n.19, s32[]{:T(128)S(6)} %select_n.20), kind=kLoop, calls=%fused_computation.7 | loop fusion | bytes 524296 | tf_op jit(solution)/shard_map/dynamic_slice | solution.py:364
  4.8 3.3 %collective-permute-done.5 = bf16[2,32,2048]{2,1,0:T(8,128)(2,1)S(1)} collective-permute-done((bf16[2,32,2048]{2,1,0:T(8,128)(2,1)}, bf16[2,32,2048]{2,1,0:T(8,128)(2,1)S(1)}, u32[]{:S(2)}, u32[]{:S(2)}) %collective-permute-start.5) | collective-permute-done | bytes 262176 | tf_op jit(solution)/shard_map/ppermute | solution.py:368
  8.1 1.0 %fusion.8 = (bf16[1,2,2,32,2048]{4,3,2,1,0:T(8,128)(2,1)S(1)}, bf16[2,2,32,2048]{3,2,1,0:T(8,128)(2,1)S(1)}) fusion(bf16[1,2,32,2048]{3,2,1,0:T(8,128)(2,1)S(1)} %bitcast.31, bf16[1,2,32,2048]{3,2,1,0:T(8,128)(2,1)} %bitcast.30), kind=kLoop, calls=%fused_computation.27 | loop fusion | flops 262144 | bytes 1572864 | tf_op jit(solution)/shard_map/stack | solution.py:392
  9.1 1.9 %collective-permute-start.6 = (bf16[2,2,32,2048]{3,2,1,0:T(8,128)(2,1)S(1)}, bf16[2,2,32,2048]{3,2,1,0:T(8,128)(2,1)S(1)}, u32[]{:S(2)}, u32[]{:S(2)}) collective-permute-start(bf16[2,2,32,2048]{3,2,1,0:T(8,128)(2,1)S(1)} %get-tuple-element.45.own), channel_id=1, source_target_pairs={{0,4},{4,8},{8,12},{12,0},{1,5},{5,9},{9,13},{13,1},{2,6},{6,10},{... | collective-permute-start | bytes 1572872 | tf_op jit(solution)/shard_map/ppermute | solution.py:372
  11.0 2.9 %collective-permute-start.7 = (bf16[2,2,32,2048]{3,2,1,0:T(8,128)(2,1)S(1)}, bf16[2,2,32,2048]{3,2,1,0:T(8,128)(2,1)S(1)}, u32[]{:S(2)}, u32[]{:S(2)}) collective-permute-start(bf16[2,2,32,2048]{3,2,1,0:T(8,128)(2,1)S(1)} %get-tuple-element.45.own), channel_id=1, source_target_pairs={{0,12},{4,0},{8,4},{12,8},{1,13},{5,1},{9,5},{13,9},{2,14},{6,2},{... | collective-permute-start | bytes 1572872 | tf_op jit(solution)/shard_map/ppermute | solution.py:373
  14.0 5.5 %collective-permute-start.2 = (bf16[2,2,32,1024]{3,2,1,0:T(8,128)(2,1)S(1)}, bf16[2,2,32,1024]{3,2,1,0:T(8,128)(2,1)S(1)}, u32[]{:S(2)}, u32[]{:S(2)}) collective-permute-start(bf16[2,2,32,1024]{3,2,1,0:T(8,128)(2,1)S(1)} %pad_maximum_fusion.2.own), channel_id=1, source_target_pairs={{0,64},{64,0},{1,65},{65,1},{2,66},{66,2},{3,67},{67,3},{4,68},{68... | collective-permute-start | bytes 786440 | tf_op jit(solution)/shard_map/ppermute | solution.py:376
  19.5 3.2 %collective-permute-start.3 = (bf16[2,2,32,1024]{3,2,1,0:T(8,128)(2,1)S(1)}, bf16[2,2,32,1024]{3,2,1,0:T(8,128)(2,1)S(1)}, u32[]{:S(2)}, u32[]{:S(2)}) collective-permute-start(bf16[2,2,32,1024]{3,2,1,0:T(8,128)(2,1)S(1)} %pad_maximum_fusion.2.own), channel_id=1, source_target_pairs={{0,16},{16,32},{32,48},{48,0},{1,17},{17,33},{33,49},{49,1},{2,18}... | collective-permute-start | bytes 786440 | tf_op jit(solution)/shard_map/ppermute | solution.py:374
  22.6 6.4 %collective-permute-start.4 = (bf16[2,2,32,1024]{3,2,1,0:T(8,128)(2,1)S(1)}, bf16[2,2,32,1024]{3,2,1,0:T(8,128)(2,1)S(1)}, u32[]{:S(2)}, u32[]{:S(2)}) collective-permute-start(bf16[2,2,32,1024]{3,2,1,0:T(8,128)(2,1)S(1)} %pad_maximum_fusion.2.own), channel_id=1, source_target_pairs={{0,48},{16,0},{32,16},{48,32},{1,49},{17,1},{33,17},{49,33},{2,50}... | collective-permute-start | bytes 786440 | tf_op jit(solution)/shard_map/ppermute | solution.py:375
  30.3 2.6 %load.1.abuf = bf16[4,2,2304,256]{3,2,1,0:T(8,128)(2,1)S(1)} custom-call(s32[54]{0:T(128)S(1)} %concatenate.3.st, bf16[2,2048,1024]{2,1,0:T(8,128)(2,1)} %a.1), custom_call_target="tpu_custom_call" | custom-call | bytes 8388608 | tf_op jit(solution)/shard_map/load/pallas_call | solution.py:379
  32.9 2.3 %collective-permute-done.3.after = bf16[2,2,32,1024]{3,2,1,0:T(8,128)(2,1)S(1)} collective-permute-done((bf16[2,2,32,1024]{3,2,1,0:T(8,128)(2,1)S(1)}, bf16[2,2,32,1024]{3,2,1,0:T(8,128)(2,1)S(1)}, u32[]{:S(2)}, u32[]{:S(2)}) %collective-permute-start.3) | collective-permute-done | bytes 262176 | tf_op jit(solution)/shard_map/ppermute | solution.py:374
  35.6 1.2 %collective-permute-start.10 = (bf16[2,2,32,1024]{3,2,1,0:T(8,128)(2,1)S(1)}, bf16[2,2,32,1024]{3,2,1,0:T(8,128)(2,1)S(1)}, u32[]{:S(2)}, u32[]{:S(2)}) collective-permute-start(bf16[2,2,32,1024]{3,2,1,0:T(8,128)(2,1)S(1)} %collective-permute-done.2.near), channel_id=1, source_target_pairs={{0,16},{16,32},{32,48},{48,0},{1,17},{17,33},{33,49},{49,1},{2,18}... | collective-permute-start | bytes 786440 | tf_op jit(solution)/shard_map/ppermute | solution.py:395
  36.8 2.1 %collective-permute-start.11 = (bf16[2,2,32,1024]{3,2,1,0:T(8,128)(2,1)S(1)}, bf16[2,2,32,1024]{3,2,1,0:T(8,128)(2,1)S(1)}, u32[]{:S(2)}, u32[]{:S(2)}) collective-permute-start(bf16[2,2,32,1024]{3,2,1,0:T(8,128)(2,1)S(1)} %collective-permute-done.2.near), channel_id=1, source_target_pairs={{0,48},{16,0},{32,16},{48,32},{1,49},{17,1},{33,17},{49,33},{2,50}... | collective-permute-start | bytes 786440 | tf_op jit(solution)/shard_map/ppermute | solution.py:396
  39.0 3.3 %collective-permute-start.9 = (bf16[2,32,2048]{2,1,0:T(8,128)(2,1)S(1)}, bf16[2,32,2048]{2,1,0:T(8,128)(2,1)S(1)}, u32[]{:S(2)}, u32[]{:S(2)}) collective-permute-start(bf16[2,32,2048]{2,1,0:T(8,128)(2,1)S(1)} %slice_bitcast_fusion), channel_id=1, source_target_pairs={{0,12},{4,0},{8,4},{12,8},{1,13},{5,1},{9,5},{13,9},{2,14},{6,2},{... | collective-permute-start | bytes 786440 | tf_op jit(solution)/shard_map/ppermute | solution.py:394
  42.3 2.4 %near.1.fb_in = bf16[4,512,1024]{2,1,0:T(8,128)(2,1)S(1)} custom-call(s32[54]{0:T(128)S(1)} %concatenate.3.st, bf16[4,2,2304,256]{3,2,1,0:T(8,128)(2,1)S(1)} %load.1.abuf, bf16[2,2,32,2048]{3,2,1,0:T(8,128)(2,1)S(1)} %get-tuple-element.45.own, bf16[2,2,32,2048]{3,2,1,0:T(8,128)(2,1)S(1)} %collective-permute-done.6.after, ...), custom_call_target="tpu_custom_call" | custom-call | flops 3221225472 | bytes 8388608 | tf_op jit(solution)/shard_map/near/pallas_call | solution.py:398
  44.6 0.8 collective-permute-done.10.near_after
  45.5 2.8 %collective-permute-done.8.g_far_a = bf16[2,32,2048]{2,1,0:T(8,128)(2,1)S(1)} collective-permute-done((bf16[2,32,2048]{2,1,0:T(8,128)(2,1)S(1)}, bf16[2,32,2048]{2,1,0:T(8,128)(2,1)S(1)}, u32[]{:S(2)}, u32[]{:S(2)}) %collective-permute-start.8) | collective-permute-done | bytes 262176 | tf_op jit(solution)/shard_map/ppermute | solution.py:393
  48.8 3.2 %collective-permute-start.16 = (bf16[2,2,32,1024]{3,2,1,0:T(8,128)(2,1)S(1)}, bf16[2,2,32,1024]{3,2,1,0:T(8,128)(2,1)S(1)}, u32[]{:S(2)}, u32[]{:S(2)}) collective-permute-start(bf16[2,2,32,1024]{3,2,1,0:T(8,128)(2,1)S(1)} %collective-permute-done.11.near_before), channel_id=1, source_target_pairs={{0,48},{16,0},{32,16},{48,32},{1,49},{17,1},{33,17},{49,33},{2,50}... | collective-permute-start | bytes 786440 | tf_op jit(solution)/shard_map/ppermute | solution.py:414
  52.0 4.1 %rest.1 = (bf16[4,512,1024]{2,1,0:T(8,128)(2,1)S(1)}, bf16[2,512,1024]{2,1,0:T(8,128)(2,1)S(1)}) custom-call(s32[54]{0:T(128)S(1)} %concatenate.3.st, bf16[4,2,2304,256]{3,2,1,0:T(8,128)(2,1)S(1)} %load.1.abuf, bf16[4,512,1024]{2,1,0:T(8,128)(2,1)S(1)} %near.1.fb_in, ...), custom_call_target="tpu_custom_call", output_to_operand_aliasing={{0}: (2, {})} | custom-call | flops 5368709120 | bytes 8388608 | tf_op jit(solution)/shard_map/rest/pallas_call | solution.py:416
  56.2 2.0 %collective-permute-done.15.far_a = bf16[2,2,32,1024]{3,2,1,0:T(8,128)(2,1)S(1)} collective-permute-done((bf16[2,2,32,1024]{3,2,1,0:T(8,128)(2,1)S(1)}, bf16[2,2,32,1024]{3,2,1,0:T(8,128)(2,1)S(1)}, u32[]{:S(2)}, u32[]{:S(2)}) %collective-permute-start.15) | collective-permute-done | bytes 262176 | tf_op jit(solution)/shard_map/ppermute | solution.py:397
  58.2 5.7 %finish.1 = (bf16[2,512,1024]{2,1,0:T(8,128)(2,1)S(1)}, bf16[64,8,512]{2,1,0:T(8,128)(2,1)S(1)}, bf16[64,8,512]{2,1,0:T(8,128)(2,1)S(1)}) custom-call(s32[54]{0:T(128)S(1)} %concatenate.3.st, bf16[4,512,1024]{2,1,0:T(8,128)(2,1)S(1)} %get-tuple-element.33.fb, bf16[2,512,1024]{2,1,0:T(8,128)(2,1)S(1)} %get-tuple-element.34.gbuf_in, ...), custom_call_target="tpu_custom_call", output_to_operand_aliasing={{0}: (2, {})} | custom-call | flops 4294967296 | bytes 8388608 | tf_op jit(solution)/shard_map/finish/pallas_call | solution.py:435
  64.0 1.9 %collective-permute-done.17 = bf16[64,8,512]{2,1,0:T(8,128)(2,1)S(1)} collective-permute-done((bf16[64,8,512]{2,1,0:T(8,128)(2,1)S(1)}, bf16[64,8,512]{2,1,0:T(8,128)(2,1)S(1)}, u32[]{:S(2)}, u32[]{:S(2)}) %collective-permute-start.17) | collective-permute-done | bytes 524320 | tf_op jit(solution)/shard_map/ppermute | solution.py:446
  66.0 21.2 %all_to_all.5.parts = bf16[64,8,512]{2,1,0:T(8,128)(2,1)} all-to-all(bf16[64,8,512]{2,1,0:T(8,128)(2,1)S(1)} %add_convert_fusion), channel_id=1, replica_groups=mesh['xh'=2,'z'=4,'y'=4,'xl'=2,'core'=2] {'xh','z','y','xl'}, dimensions={0} | all-to-all | bytes 1048576 | tf_op jit(solution)/shard_map/all_to_all | solution.py:448
  87.8 1.8 %align.1 = f32[4,2,512]{2,1,0:T(2,128)} custom-call(s32[4,128]{1,0:T(4,128)} %broadcast_in_dim.14.index, bf16[64,8,512]{2,1,0:T(8,128)(2,1)} %all_to_all.5.parts), custom_call_target="tpu_custom_call" | custom-call | tf_op jit(solution)/shard_map/align/pallas_call | solution.py:449
  (40 shorter events, 5.3 us)
Async XLA Ops:
  0.0 8.1 %collective-permute-start.5 = (bf16[2,32,2048]{2,1,0:T(8,128)(2,1)}, bf16[2,32,2048]{2,1,0:T(8,128)(2,1)S(1)}, u32[]{:S(2)}, u32[]{:S(2)}) collective-permute-start(bf16[2,32,2048]{2,1,0:T(8,128)(2,1)} %bitcast.29), channel_id=1, source_target_pairs={{0,2},{2,0},{1,3},{3,1},{4,6},{6,4},{5,7},{7,5},{8,10},{10,8},{9,1... | collective-permute-start | bytes 786440 | tf_op jit(solution)/shard_map/ppermute | solution.py:368
  4.0 9.9 %collective-permute-start.1 = (bf16[2,32,1024]{2,1,0:T(8,128)(2,1)S(1)}, bf16[2,32,1024]{2,1,0:T(8,128)(2,1)S(1)}, u32[]{:S(2)}, u32[]{:S(2)}) collective-permute-start(bf16[2,32,1024]{2,1,0:T(8,128)(2,1)S(1)} %get-tuple-element.47), channel_id=1, source_target_pairs={{0,1},{1,0},{2,65},{3,64},{4,17},{5,16},{6,81},{7,80},{8,33},{9,32... | collective-permute-start | bytes 393224 | tf_op jit(solution)/shard_map/ppermute | solution.py:367
  4.1 9.8 %collective-permute-start = (bf16[2,32,1024]{2,1,0:T(8,128)(2,1)S(1)}, bf16[2,32,1024]{2,1,0:T(8,128)(2,1)S(1)}, u32[]{:S(2)}, u32[]{:S(2)}) collective-permute-start(bf16[2,32,1024]{2,1,0:T(8,128)(2,1)S(1)} %get-tuple-element.46), channel_id=1, source_target_pairs={{0,0},{1,1},{2,64},{3,65},{4,16},{5,17},{6,80},{7,81},{8,32},{9,33... | collective-permute-start | bytes 393224 | tf_op jit(solution)/shard_map/ppermute | solution.py:366
  9.1 26.2 %collective-permute-start.6 = (bf16[2,2,32,2048]{3,2,1,0:T(8,128)(2,1)S(1)}, bf16[2,2,32,2048]{3,2,1,0:T(8,128)(2,1)S(1)}, u32[]{:S(2)}, u32[]{:S(2)}) collective-permute-start(bf16[2,2,32,2048]{3,2,1,0:T(8,128)(2,1)S(1)} %get-tuple-element.45.own), channel_id=1, source_target_pairs={{0,4},{4,8},{8,12},{12,0},{1,5},{5,9},{9,13},{13,1},{2,6},{6,10},{... | collective-permute-start | bytes 1572872 | tf_op jit(solution)/shard_map/ppermute | solution.py:372
  11.0 24.3 %collective-permute-start.7 = (bf16[2,2,32,2048]{3,2,1,0:T(8,128)(2,1)S(1)}, bf16[2,2,32,2048]{3,2,1,0:T(8,128)(2,1)S(1)}, u32[]{:S(2)}, u32[]{:S(2)}) collective-permute-start(bf16[2,2,32,2048]{3,2,1,0:T(8,128)(2,1)S(1)} %get-tuple-element.45.own), channel_id=1, source_target_pairs={{0,12},{4,0},{8,4},{12,8},{1,13},{5,1},{9,5},{13,9},{2,14},{6,2},{... | collective-permute-start | bytes 1572872 | tf_op jit(solution)/shard_map/ppermute | solution.py:373
  14.0 18.9 %collective-permute-start.2 = (bf16[2,2,32,1024]{3,2,1,0:T(8,128)(2,1)S(1)}, bf16[2,2,32,1024]{3,2,1,0:T(8,128)(2,1)S(1)}, u32[]{:S(2)}, u32[]{:S(2)}) collective-permute-start(bf16[2,2,32,1024]{3,2,1,0:T(8,128)(2,1)S(1)} %pad_maximum_fusion.2.own), channel_id=1, source_target_pairs={{0,64},{64,0},{1,65},{65,1},{2,66},{66,2},{3,67},{67,3},{4,68},{68... | collective-permute-start | bytes 786440 | tf_op jit(solution)/shard_map/ppermute | solution.py:376
  19.5 15.8 %collective-permute-start.3 = (bf16[2,2,32,1024]{3,2,1,0:T(8,128)(2,1)S(1)}, bf16[2,2,32,1024]{3,2,1,0:T(8,128)(2,1)S(1)}, u32[]{:S(2)}, u32[]{:S(2)}) collective-permute-start(bf16[2,2,32,1024]{3,2,1,0:T(8,128)(2,1)S(1)} %pad_maximum_fusion.2.own), channel_id=1, source_target_pairs={{0,16},{16,32},{32,48},{48,0},{1,17},{17,33},{33,49},{49,1},{2,18}... | collective-permute-start | bytes 786440 | tf_op jit(solution)/shard_map/ppermute | solution.py:374
  22.6 12.6 %collective-permute-start.4 = (bf16[2,2,32,1024]{3,2,1,0:T(8,128)(2,1)S(1)}, bf16[2,2,32,1024]{3,2,1,0:T(8,128)(2,1)S(1)}, u32[]{:S(2)}, u32[]{:S(2)}) collective-permute-start(bf16[2,2,32,1024]{3,2,1,0:T(8,128)(2,1)S(1)} %pad_maximum_fusion.2.own), channel_id=1, source_target_pairs={{0,48},{16,0},{32,16},{48,32},{1,49},{17,1},{33,17},{49,33},{2,50}... | collective-permute-start | bytes 786440 | tf_op jit(solution)/shard_map/ppermute | solution.py:375
  35.5 16.6 %collective-permute-start.12 = (bf16[3,2,2,32,2048]{4,3,2,1,0:T(8,128)(2,1)S(1)}, bf16[3,2,2,32,2048]{4,3,2,1,0:T(8,128)(2,1)S(1)}, u32[]{:S(2)}, u32[]{:S(2)}) collective-permute-start(bf16[3,2,2,32,2048]{4,3,2,1,0:T(8,128)(2,1)S(1)} %pad_maximum_fusion), channel_id=1, source_target_pairs={{0,1},{1,0},{2,3},{3,2},{4,5},{5,4},{6,7},{7,6},{8,9},{9,8},{10,11... | collective-permute-start | bytes 4718600 | tf_op jit(solution)/shard_map/ppermute | solution.py:392
  35.6 9.9 %collective-permute-start.10 = (bf16[2,2,32,1024]{3,2,1,0:T(8,128)(2,1)S(1)}, bf16[2,2,32,1024]{3,2,1,0:T(8,128)(2,1)S(1)}, u32[]{:S(2)}, u32[]{:S(2)}) collective-permute-start(bf16[2,2,32,1024]{3,2,1,0:T(8,128)(2,1)S(1)} %collective-permute-done.2.near), channel_id=1, source_target_pairs={{0,16},{16,32},{32,48},{48,0},{1,17},{17,33},{33,49},{49,1},{2,18}... | collective-permute-start | bytes 786440 | tf_op jit(solution)/shard_map/ppermute | solution.py:395
  36.8 8.7 %collective-permute-start.11 = (bf16[2,2,32,1024]{3,2,1,0:T(8,128)(2,1)S(1)}, bf16[2,2,32,1024]{3,2,1,0:T(8,128)(2,1)S(1)}, u32[]{:S(2)}, u32[]{:S(2)}) collective-permute-start(bf16[2,2,32,1024]{3,2,1,0:T(8,128)(2,1)S(1)} %collective-permute-done.2.near), channel_id=1, source_target_pairs={{0,48},{16,0},{32,16},{48,32},{1,49},{17,1},{33,17},{49,33},{2,50}... | collective-permute-start | bytes 786440 | tf_op jit(solution)/shard_map/ppermute | solution.py:396
  38.9 9.4 %collective-permute-start.8 = (bf16[2,32,2048]{2,1,0:T(8,128)(2,1)S(1)}, bf16[2,32,2048]{2,1,0:T(8,128)(2,1)S(1)}, u32[]{:S(2)}, u32[]{:S(2)}) collective-permute-start(bf16[2,32,2048]{2,1,0:T(8,128)(2,1)S(1)} %slice_bitcast_fusion.1), channel_id=1, source_target_pairs={{0,4},{4,8},{8,12},{12,0},{1,5},{5,9},{9,13},{13,1},{2,6},{6,10},{... | collective-permute-start | bytes 786440 | tf_op jit(solution)/shard_map/ppermute | solution.py:393
  39.0 9.3 %collective-permute-start.9 = (bf16[2,32,2048]{2,1,0:T(8,128)(2,1)S(1)}, bf16[2,32,2048]{2,1,0:T(8,128)(2,1)S(1)}, u32[]{:S(2)}, u32[]{:S(2)}) collective-permute-start(bf16[2,32,2048]{2,1,0:T(8,128)(2,1)S(1)} %slice_bitcast_fusion), channel_id=1, source_target_pairs={{0,12},{4,0},{8,4},{12,8},{1,13},{5,1},{9,5},{13,9},{2,14},{6,2},{... | collective-permute-start | bytes 786440 | tf_op jit(solution)/shard_map/ppermute | solution.py:394
  48.3 3.8 %collective-permute-start.13 = (bf16[2,32,2048]{2,1,0:T(8,128)(2,1)S(1)}, bf16[2,32,2048]{2,1,0:T(8,128)(2,1)S(1)}, u32[]{:S(2)}, u32[]{:S(2)}) collective-permute-start(bf16[2,32,2048]{2,1,0:T(8,128)(2,1)S(1)} %collective-permute-done.8.g_far_a), channel_id=1, source_target_pairs={{0,1},{1,0},{2,3},{3,2},{4,5},{5,4},{6,7},{7,6},{8,9},{9,8},{10,11... | collective-permute-start | bytes 786440 | tf_op jit(solution)/shard_map/ppermute | solution.py:412
  48.3 3.8 %collective-permute-start.14 = (bf16[2,32,2048]{2,1,0:T(8,128)(2,1)S(1)}, bf16[2,32,2048]{2,1,0:T(8,128)(2,1)S(1)}, u32[]{:S(2)}, u32[]{:S(2)}) collective-permute-start(bf16[2,32,2048]{2,1,0:T(8,128)(2,1)S(1)} %collective-permute-done.9.g_far_b), channel_id=1, source_target_pairs={{0,1},{1,0},{2,3},{3,2},{4,5},{5,4},{6,7},{7,6},{8,9},{9,8},{10,11... | collective-permute-start | bytes 786440 | tf_op jit(solution)/shard_map/ppermute | solution.py:413
  48.8 9.4 %collective-permute-start.15 = (bf16[2,2,32,1024]{3,2,1,0:T(8,128)(2,1)S(1)}, bf16[2,2,32,1024]{3,2,1,0:T(8,128)(2,1)S(1)}, u32[]{:S(2)}, u32[]{:S(2)}) collective-permute-start(bf16[2,2,32,1024]{3,2,1,0:T(8,128)(2,1)S(1)} %collective-permute-done.3.after), channel_id=1, source_target_pairs={{0,16},{16,32},{32,48},{48,0},{1,17},{17,33},{33,49},{49,1},{2,18}... | collective-permute-start | bytes 786440 | tf_op jit(solution)/shard_map/ppermute | solution.py:397
  48.8 9.4 %collective-permute-start.16 = (bf16[2,2,32,1024]{3,2,1,0:T(8,128)(2,1)S(1)}, bf16[2,2,32,1024]{3,2,1,0:T(8,128)(2,1)S(1)}, u32[]{:S(2)}, u32[]{:S(2)}) collective-permute-start(bf16[2,2,32,1024]{3,2,1,0:T(8,128)(2,1)S(1)} %collective-permute-done.11.near_before), channel_id=1, source_target_pairs={{0,48},{16,0},{32,16},{48,32},{1,49},{17,1},{33,17},{49,33},{2,50}... | collective-permute-start | bytes 786440 | tf_op jit(solution)/shard_map/ppermute | solution.py:414
  63.9 23.3 %copy-start = (s32[4]{0:T(128)S(1)}, s32[4]{0:T(128)}, u32[]{:S(2)}) copy-start(s32[4]{0:T(128)} %param.7) | copy-start | bytes 52
  63.9 2.0 %collective-permute-start.17 = (bf16[64,8,512]{2,1,0:T(8,128)(2,1)S(1)}, bf16[64,8,512]{2,1,0:T(8,128)(2,1)S(1)}, u32[]{:S(2)}, u32[]{:S(2)}) collective-permute-start(bf16[64,8,512]{2,1,0:T(8,128)(2,1)S(1)} %get-tuple-element.36), channel_id=1, source_target_pairs={{0,1},{1,0},{2,3},{3,2},{4,5},{5,4},{6,7},{7,6},{8,9},{9,8},{10,11... | collective-permute-start | bytes 1572872 | tf_op jit(solution)/shard_map/ppermute | solution.py:446
